TPU v7x, 32 devices: a whole 2x2x4 slice. The times are simulated.
32 devices in a mesh: row: 8 (over y, x, core), col: 4 (over z).
Axes of the slice: x: 2, y: 2, z: 4, core: 2. Of those that a mesh axis runs over, the one named last changes fastest.
Arguments:
- mask: float32 [4096, 4096], P('row', 'col'), may hold values from -6 to 6
- target: bfloat16 [4096, 4096], P('row', 'col'), may hold values from 0 to 1
- live: int32 [8, 8], P('row', 'col'), may hold values from 0 to 1, as said below
- pupils: float32 [2, 12, 144, 144], replicated, may hold values from -8 to 8
- weights: float32 [12], replicated, may hold values from 0.1 to 1
Outputs:
- updated_mask: float32 [4096, 4096], P('row', 'col')
Inputs may be any that keep to these rules, and one draw needn't show every extreme that they name: In each tile row exactly 2 tiles are live and the others are 0; all 2 tiles of at least one device of the row are live.
All inputs are finite; a program needn't handle non-finite values.
Results may differ from a plain program's by a relative error of at most 0.013.
Values may be sent and summed in bfloat16 or wider, within the bound.
No kernel may reach another device: no remote copies, remote signals or barrier semaphores. Data moves between devices by JAX's collectives and lax.ppermute only.
A program may use at most 128 MiB of HBM per device.

v0:
```python
from functools import partial
import math

import jax
import jax.numpy as jnp
from jax import lax
from jax.sharding import PartitionSpec as P

AMBIT = 128


steepness = 4.0
threshold_level = 1.0
step_rate = 8.0


def extended_2(block, sides, width):
    for axis, dim in sides:
        count = lax.axis_size(axis)
        forward = [(i, i + 1) for i in range(count - 1)]
        backward = [(target, source) for source, target in forward]
        low = lax.ppermute(
            lax.slice_in_dim(block, block.shape[dim] - width, None, axis=dim), axis, forward
        )
        high = lax.ppermute(lax.slice_in_dim(block, 0, width, axis=dim), axis, backward)
        block = jnp.concatenate([low, block, high], axis=dim)
    return block


def entering(part, axis, combine, identity):
    place = lax.axis_index(axis)
    gathered = lax.all_gather(part, axis)
    state = jnp.zeros_like(part) + jnp.asarray(identity, part.dtype)

    def one(turn, state):
        return combine(state, lax.dynamic_index_in_dim(gathered, turn, 0, False))

    return lax.fori_loop(0, place, one, state)


def matmul(leading, trailing):
    return jnp.dot(leading, trailing, preferred_element_type=jnp.float32)


def contract_first(leading, trailing):
    return lax.dot_general(
        leading, trailing, (((0,), (0,)), ((), ())), preferred_element_type=jnp.float32
    )


def contract_last(leading, trailing):
    return lax.dot_general(
        leading, trailing, (((1,), (1,)), ((), ())), preferred_element_type=jnp.float32
    )


def cosine_pair(freq_count, pixel_count, offset, period):
    frequency = jnp.arange(freq_count, dtype=jnp.int32) - freq_count // 2
    pixels = jnp.arange(pixel_count, dtype=jnp.int32) + offset
    phases = jnp.mod(frequency[:, None] * pixels[None, :], period).astype(jnp.float32)
    angles = phases * (2.0 * math.pi / period)
    factor = 1.0 / math.sqrt(period)
    return (
        (jnp.cos(angles) * factor).astype(jnp.bfloat16),
        (jnp.sin(angles) * factor).astype(jnp.bfloat16),
    )


def transform_tables(spectrum_size, tile_size, ambit_size):
    extent = tile_size + 2 * ambit_size
    outer_cos, outer_sin = cosine_pair(spectrum_size, extent, 0, extent)
    forward = jnp.concatenate([outer_cos, outer_sin], axis=0)
    inner_cos, inner_sin = cosine_pair(spectrum_size, tile_size, ambit_size, extent)
    inverse = jnp.concatenate([inner_cos, inner_sin], axis=0)
    rotate = jnp.concatenate(
        [
            jnp.concatenate([inner_cos, inner_sin], axis=1),
            jnp.concatenate([-inner_sin, inner_cos], axis=1),
        ],
        axis=0,
    )
    return (forward, inverse, rotate)


def spectrum(extended, forward):
    spectrum_size = forward.shape[0] // 2
    partial_rows = matmul(forward, extended).astype(jnp.bfloat16)
    blocks = contract_last(partial_rows, forward)
    real_spectrum = blocks[:spectrum_size, :spectrum_size] - blocks[spectrum_size:, spectrum_size:]
    imaginary_spectrum = -(
        blocks[:spectrum_size, spectrum_size:] + blocks[spectrum_size:, :spectrum_size]
    )
    return jnp.stack([real_spectrum, imaginary_spectrum]).astype(jnp.bfloat16)


def spectral_gradient(spectra, goal_tile, live_flag, pupils, weights, inverse, rotate):
    real_spectrum = spectra[0].astype(jnp.float32)
    imaginary_spectrum = spectra[1].astype(jnp.float32)
    tile_size = inverse.shape[1]
    spectrum_size = real_spectrum.shape[0]

    def forward_kernel(intensity, inputs):
        pupil_real, pupil_imaginary, weight = inputs
        wave_real = pupil_real * real_spectrum - pupil_imaginary * imaginary_spectrum
        wave_imaginary = pupil_real * imaginary_spectrum + pupil_imaginary * real_spectrum
        amplitude = jnp.concatenate(
            [
                jnp.concatenate([wave_real, -wave_imaginary], axis=1),
                jnp.concatenate([wave_imaginary, wave_real], axis=1),
            ],
            axis=0,
        ).astype(jnp.bfloat16)
        section_one = matmul(amplitude, inverse).astype(jnp.bfloat16)
        field_pair = contract_first(rotate, section_one)
        energy = field_pair[:tile_size] ** 2 + field_pair[tile_size:] ** 2
        return (intensity + weight * energy, field_pair.astype(jnp.bfloat16))

    initial = jnp.zeros((tile_size, tile_size), jnp.float32)
    intensity, fields = lax.scan(forward_kernel, initial, (pupils[0], pupils[1], weights))
    resist = jax.nn.sigmoid(steepness * (intensity - threshold_level))
    slope_map = (
        live_flag * (resist - goal_tile.astype(jnp.float32)) * steepness * resist * (1.0 - resist)
    )
    doubled = jnp.concatenate([slope_map, slope_map], axis=0)

    def backward_kernel(totals, inputs):
        pupil_real, pupil_imaginary, weight, field_pair = inputs
        cotangent = (2.0 * weight * doubled * field_pair.astype(jnp.float32)).astype(jnp.bfloat16)
        section_back = matmul(rotate, cotangent).astype(jnp.bfloat16)
        wave_back = contract_last(section_back, inverse)
        adjoint_real = (
            wave_back[:spectrum_size, :spectrum_size] + wave_back[spectrum_size:, spectrum_size:]
        )
        adjoint_imaginary = (
            wave_back[spectrum_size:, :spectrum_size] - wave_back[:spectrum_size, spectrum_size:]
        )
        total_real = totals[0] + pupil_real * adjoint_real + pupil_imaginary * adjoint_imaginary
        total_imaginary = (
            totals[1] - pupil_imaginary * adjoint_real + pupil_real * adjoint_imaginary
        )
        return ((total_real, total_imaginary), None)

    empty_spec = jnp.zeros((spectrum_size, spectrum_size), jnp.float32)
    sums, unused = lax.scan(
        backward_kernel, (empty_spec, empty_spec), (pupils[0], pupils[1], weights, fields)
    )
    return jnp.stack([sums[0], sums[1]]).astype(jnp.bfloat16)


def pixel_gradient(gradient, forward):
    adjoint_real = gradient[0]
    adjoint_imaginary = gradient[1]
    upper_rows = jnp.concatenate([adjoint_real, -adjoint_imaginary], axis=1)
    lower_rows = jnp.concatenate([-adjoint_imaginary, -adjoint_real], axis=1)
    blocks = jnp.concatenate([upper_rows, lower_rows], axis=0)
    partial_rows = matmul(blocks, forward).astype(jnp.bfloat16)
    return contract_first(forward, partial_rows)


def route_table(slot_flags, first_rank, group_size):
    before = jnp.cumsum(slot_flags) - slot_flags
    slot_ranks = (first_rank + before).astype(jnp.int32)
    target_ids = jnp.arange(group_size, dtype=jnp.int32)
    routes = ((target_ids[:, None] == slot_ranks[None, :]) & (slot_flags[None, :] > 0)).astype(
        jnp.float32
    )
    return (routes, slot_ranks)


def spread_items(routes, items):
    broadcast_shape = (routes.shape[0],) + (1,) * items[0].ndim
    gathered = routes[:, 0].astype(items[0].dtype).reshape(broadcast_shape) * items[0][None]
    weight_column = routes[:, 1].astype(items[0].dtype).reshape(broadcast_shape)
    gathered = gathered + weight_column * items[1][None]
    return gathered


def empty_like_tile(extent):
    return jnp.zeros((extent, extent), jnp.float32)


def fold_rims(total, tile_size, block_width, ambit_size):
    beside_all = extended_2(
        total.astype(jnp.bfloat16), (("row", 0), ("col", 1)), ambit_size
    ).astype(total.dtype)
    middle_rows = beside_all[2 * ambit_size : 2 * ambit_size + tile_size]
    middle_rows = middle_rows.at[:ambit_size].add(beside_all[:ambit_size])
    middle_rows = middle_rows.at[tile_size - ambit_size :].add(
        beside_all[tile_size + 3 * ambit_size :]
    )
    folded = middle_rows[:, 2 * ambit_size : 2 * ambit_size + block_width]
    folded = folded.at[:, :ambit_size].add(middle_rows[:, :ambit_size])
    folded = folded.at[:, block_width - ambit_size :].add(
        middle_rows[:, block_width + 3 * ambit_size :]
    )
    return folded


def body(mask, target, live, pupils, weights):
    tile_size = mask.shape[0]
    slot_count = live.shape[1]
    spectrum_size = pupils.shape[2]
    forward, inverse, rotate = transform_tables(spectrum_size, tile_size, AMBIT)
    extent = tile_size + 2 * AMBIT
    extended = extended_2(mask.astype(jnp.bfloat16), (("row", 0), ("col", 1)), AMBIT)
    slot_flags = live[0]
    windows = [
        extended[:, slot_index * tile_size : slot_index * tile_size + extent]
        for slot_index in range(slot_count)
    ]
    goal_tiles = [
        target[:, slot_index * tile_size : (slot_index + 1) * tile_size]
        for slot_index in range(slot_count)
    ]
    skipped = partial(empty_like_tile, extent)
    pieces = []
    first_rank = entering(jnp.sum(slot_flags), "col", jnp.add, jnp.int32(0))
    routes, slot_ranks = route_table(slot_flags, first_rank, lax.axis_size("col"))
    spectra = [spectrum(window, forward).reshape(-1) for window in windows]
    send_spectra = spread_items(routes, spectra)
    send_goals = spread_items(routes, goal_tiles)
    send_flags = jnp.sum(routes, axis=1).astype(jnp.bfloat16)
    got_spectra, got_goals, got_flags = (
        lax.all_to_all(send_spectra, "col", split_axis=0, concat_axis=0, tiled=True),
        lax.all_to_all(send_goals, "col", split_axis=0, concat_axis=0, tiled=True),
        lax.all_to_all(send_flags, "col", split_axis=0, concat_axis=0, tiled=True),
    )
    own_flag = jnp.sum(got_flags.astype(jnp.float32))
    own_spectra = jnp.sum(got_spectra, axis=0).reshape(2, spectrum_size, spectrum_size)
    own_goal = jnp.sum(got_goals, axis=0)

    def work_spectra():
        return spectral_gradient(
            own_spectra, own_goal, own_flag, pupils, weights, inverse, rotate
        ).reshape(-1)

    def spare_spectra():
        return jnp.zeros((2 * spectrum_size * spectrum_size,), jnp.bfloat16)

    result = lax.cond(own_flag > 0, work_spectra, spare_spectra)
    answers = got_flags[:, None] * result[None, :]
    returned = lax.all_to_all(answers, "col", split_axis=0, concat_axis=0, tiled=True)
    for slot_index in range(slot_count):
        gradient = lax.dynamic_index_in_dim(returned, slot_ranks[slot_index], 0, keepdims=False)
        gradient = gradient.reshape(2, spectrum_size, spectrum_size)
        compute = partial(pixel_gradient, gradient, forward)
        pieces.append(lax.cond(slot_flags[slot_index] > 0, compute, skipped))
    total = jnp.zeros((tile_size + 2 * AMBIT, slot_count * tile_size + 2 * AMBIT), jnp.float32)
    for slot_index in range(slot_count):
        total = total.at[:, slot_index * tile_size : slot_index * tile_size + extent].add(
            pieces[slot_index]
        )
    folded = fold_rims(total, tile_size, slot_count * tile_size, AMBIT)
    return mask - step_rate * folded


def solution(mesh):
    placed = (P("row", "col"), P("row", "col"), P("row", "col"), P(), P())
    return jax.shard_map(
        body, mesh=mesh, in_specs=placed, out_specs=P("row", "col"), check_vma=False
    )
```

profile of v0, /device:TPU:11, one launch (start us, length us, event | category | flops | bytes accessed | tf_op | source)
XLA Modules:
  0.0 363.2 jit_solution(13687422691066525942)
XLA Ops:
  1.8 3.7 %collective-permute-start = (bf16[128,1024]{1,0:T(8,128)(2,1)S(1)}, bf16[128,1024]{1,0:T(8,128)(2,1)S(1)}, u32[]{:S(2)}, u32[]{:S(2)}) collective-permute-start(bf16[128,1024]{1,0:T(8,128)(2,1)S(1)} %get-tuple-element.540), channel_id=1, source_target_pairs={{0,4},{4,8},{8,12},{12,16},{16,20},{20,24},{24,28},{1,5},{5,9},{9,... | collective-permute-start | bytes 786440 | tf_op jit(solution)/shard_map/ppermute | solution.py:22
  10.1 6.4 %all-reduce.1 = s32[4]{0:T(128)S(1)} all-reduce(s32[4]{0:T(128)S(1)} %dynamic-update-slice.18), channel_id=1, replica_groups=mesh['row'=8,'col'=4] {'col'}, use_global_device_ids=true, to_apply=%add.1 | all-reduce | flops 4 | bytes 32
  18.8 5.1 %all-to-all-start = ((bf16[4,1,1]{2,1,0:T(2,128)(2,1)}), bf16[4,1,1]{2,1,0:T(2,128)(2,1)S(1)}, u32[]{:S(2)}, u32[]{:S(2)}) async-start(bf16[4,1,1]{2,1,0:T(2,128)(2,1)} %copy.19), calls=%async_computation | async-start | bytes 4096 | tf_op jit(solution)/shard_map/all_to_all | solution.py:226
  26.2 3.1 collective-permute-start.2
  42.1 3.6 %all-to-all-start.1 = ((bf16[4,2,20736]{2,1,0:T(2,128)(2,1)}), bf16[4,2,20736]{2,1,0:T(2,128)(2,1)S(1)}, u32[]{:S(2)}, u32[]{:S(2)}) async-start(bf16[4,2,20736]{2,1,0:T(2,128)(2,1)} %reshape.444), calls=%async_computation.1 | async-start | bytes 663552 | tf_op jit(solution)/shard_map/all_to_all | solution.py:224
  47.5 4.1 %all-to-all-done.1 = bf16[4,2,20736]{2,1,0:T(2,128)(2,1)S(1)} async-done(((bf16[4,2,20736]{2,1,0:T(2,128)(2,1)}), bf16[4,2,20736]{2,1,0:T(2,128)(2,1)S(1)}, u32[]{:S(2)}, u32[]{:S(2)}) %all-to-all-start.1) | async-done | bytes 331808 | tf_op jit(solution)/shard_map/all_to_all | solution.py:224
  51.7 3.9 %all-to-all-start.2 = ((bf16[4,512,512]{2,1,0:T(8,128)(2,1)}), bf16[4,512,512]{2,1,0:T(8,128)(2,1)S(1)}, u32[]{:S(2)}, u32[]{:S(2)}) async-start(bf16[4,512,512]{2,1,0:T(8,128)(2,1)} %multiply_add_fusion), calls=%async_computation.2 | async-start | bytes 4194304 | tf_op jit(solution)/shard_map/all_to_all | solution.py:225
  60.7 34.9 %all-to-all-done.2 = bf16[4,512,512]{2,1,0:T(8,128)(2,1)S(1)} async-done(((bf16[4,512,512]{2,1,0:T(8,128)(2,1)}), bf16[4,512,512]{2,1,0:T(8,128)(2,1)S(1)}, u32[]{:S(2)}, u32[]{:S(2)}) %all-to-all-start.2) | async-done | bytes 2097184 | tf_op jit(solution)/shard_map/all_to_all | solution.py:225
  95.6 187.0 %conditional.3 = (bf16[41472]{0:T(1024)(128)(2,1)}) conditional(s32[]{:T(128)} %convert_element_type.195, () %tuple.78, (f32[2,12,144,144]{3,2,1,0:T(8,128)}, bf16[4,1,41472]{2,1,0:T(2,128)(2,1)}, f32[12]{0:T(128)S(1)}, bf16[288,512]{1,0:T(8,128)(2,1)S(1)}, bf16[288,1024]{1,0:T(8,128)(2,1)S(1)}, /*index=5*/f32[]{:T(128)}, ...), branch_computations={%region_7.8_spmd, %region_8.0_spmd} | conditional | flops 784163328 | bytes 52339920 | solution.py:240
  95.7 4.8 %slice_bitcast_fusion = (f32[12,144,144]{2,1,0:T(8,128)}, f32[12,144,144]{2,1,0:T(8,128)}) fusion(f32[2,12,144,144]{3,2,1,0:T(8,128)} %get-tuple-element.367), kind=kLoop, calls=%fused_computation.42 | loop fusion | bytes 3981312 | tf_op jit(solution)/shard_map/cond/branch_1_fun/squeeze | solution.py:145
  102.6 82.6 %while.56 = (s32[]{:T(128)}, f32[512,512]{0,1:T(8,128)}, bf16[12,1024,512]{1,2,0:T(8,128)(2,1)}, f32[12]{0:T(128)S(1)}, f32[12,144,144]{2,1,0:T(8,128)}, /*index...) while((s32[]{:T(128)}, f32[512,512]{0,1:T(8,128)}, ...), condition=%wide.region_11.11_spmd.clone, body=%wide.region_10.10_spmd.clone.sunk | while | flops 390040064 | bytes 8806035 | solution.py:119
  112.2 3.2 fusion.134
  119.2 3.2 fusion.134
  126.1 3.2 fusion.134
  133.1 3.2 fusion.134
  140.1 3.2 fusion.134
  147.0 3.2 fusion.134
  154.1 3.2 fusion.134
  161.1 3.2 fusion.134
  168.0 3.2 fusion.134
  175.0 3.2 fusion.134
  182.0 3.2 fusion.134
  185.2 2.7 copy.17
  192.5 88.2 %while.57 = (s32[]{:T(128)}, f32[144,144]{1,0:T(8,128)}, f32[144,144]{1,0:T(8,128)}, f32[12,144,144]{2,1,0:T(8,128)}, f32[12]{0:T(128)S(1)}, /*index=5*/f32[1024...) while((s32[]{:T(128)}, f32[144,144]{1,0:T(8,128)}, ...), condition=%wide.region_14.14_spmd.clone, body=%wide.region_13.13_spmd.clone.sunk | while | flops 389417984 | bytes 10713371 | solution.py:144
  287.7 11.0 %all-to-all-start.3 = ((bf16[4,2,20736]{2,1,0:T(2,128)(2,1)}), bf16[4,2,20736]{2,1,0:T(2,128)(2,1)S(1)}, u32[]{:S(2)}, u32[]{:S(2)}) async-start(bf16[4,2,20736]{2,1,0:T(2,128)(2,1)} %reshape.446), calls=%async_computation.3 | async-start | bytes 663552 | tf_op jit(solution)/shard_map/all_to_all | solution.py:242
  301.2 4.5 %all-to-all-done.3 = bf16[4,2,20736]{2,1,0:T(2,128)(2,1)S(1)} async-done(((bf16[4,2,20736]{2,1,0:T(2,128)(2,1)}), bf16[4,2,20736]{2,1,0:T(2,128)(2,1)S(1)}, u32[]{:S(2)}, u32[]{:S(2)}) %all-to-all-start.3) | async-done | bytes 331808 | tf_op jit(solution)/shard_map/all_to_all | solution.py:242
  313.2 3.4 add_dynamic-update-slice_fusion
  319.0 4.8 %collective-permute-start.4 = (bf16[128,1280]{1,0:T(8,128)(2,1)S(1)}, bf16[128,1280]{1,0:T(8,128)(2,1)S(1)}, u32[]{:S(2)}, u32[]{:S(2)}) collective-permute-start(bf16[128,1280]{1,0:T(8,128)(2,1)S(1)} %get-tuple-element.534), channel_id=1, source_target_pairs={{0,4},{4,8},{8,12},{12,16},{16,20},{20,24},{24,28},{1,5},{5,9},{9,... | collective-permute-start | bytes 983048 | tf_op jit(solution)/shard_map/ppermute | solution.py:22
  323.9 13.8 %collective-permute-start.5 = (bf16[128,1280]{1,0:T(8,128)(2,1)S(1)}, bf16[128,1280]{1,0:T(8,128)(2,1)S(1)}, u32[]{:S(2)}, u32[]{:S(2)}) collective-permute-start(bf16[128,1280]{1,0:T(8,128)(2,1)S(1)} %get-tuple-element.535), channel_id=1, source_target_pairs={{4,0},{8,4},{12,8},{16,12},{20,16},{24,20},{28,24},{5,1},{9,5},{13... | collective-permute-start | bytes 983048 | tf_op jit(solution)/shard_map/ppermute | solution.py:25
  339.0 8.7 %collective-permute-start.6 = (bf16[1024,128]{1,0:T(8,128)(2,1)S(1)}, bf16[1024,128]{1,0:T(8,128)(2,1)S(1)}, u32[]{:S(2)}, u32[]{:S(2)}) collective-permute-start(bf16[1024,128]{1,0:T(8,128)(2,1)S(1)} %get-tuple-element.532), channel_id=1, source_target_pairs={{0,1},{1,2},{2,3},{4,5},{5,6},{6,7},{8,9},{9,10},{10,11},{12,13},{... | collective-permute-start | bytes 786440 | tf_op jit(solution)/shard_map/ppermute | solution.py:22
  350.3 3.6 collective-permute-done.6
  356.4 3.0 maximum_convert_fusion
  (305 shorter events, 194.3 us)
Async XLA Ops:
  0.0 8.1 %copy-start.14 = (u32[32]{0:T(128)S(1)}, u32[32]{0:T(128)}, u32[]{:S(2)}) copy-start(u32[32]{0:T(128)} %constant.292) | copy-start | bytes 388
  0.0 7.5 %copy-start.12 = (s32[1,2]{1,0:T(1,128)S(1)}, s32[1,2]{1,0:T(1,128)}, u32[]{:S(2)}) copy-start(s32[1,2]{1,0:T(1,128)} %param.31) | copy-start | bytes 28
  1.8 24.3 %collective-permute-start = (bf16[128,1024]{1,0:T(8,128)(2,1)S(1)}, bf16[128,1024]{1,0:T(8,128)(2,1)S(1)}, u32[]{:S(2)}, u32[]{:S(2)}) collective-permute-start(bf16[128,1024]{1,0:T(8,128)(2,1)S(1)} %get-tuple-element.540), channel_id=1, source_target_pairs={{0,4},{4,8},{8,12},{12,16},{16,20},{20,24},{24,28},{1,5},{5,9},{9,... | collective-permute-start | bytes 786440 | tf_op jit(solution)/shard_map/ppermute | solution.py:22
  5.5 20.6 %collective-permute-start.1 = (bf16[128,1024]{1,0:T(8,128)(2,1)S(1)}, bf16[128,1024]{1,0:T(8,128)(2,1)S(1)}, u32[]{:S(2)}, u32[]{:S(2)}) collective-permute-start(bf16[128,1024]{1,0:T(8,128)(2,1)S(1)} %get-tuple-element.541), channel_id=1, source_target_pairs={{4,0},{8,4},{12,8},{16,12},{20,16},{24,20},{28,24},{5,1},{9,5},{13... | collective-permute-start | bytes 786440 | tf_op jit(solution)/shard_map/ppermute | solution.py:25
  18.8 23.3 %all-to-all-start = ((bf16[4,1,1]{2,1,0:T(2,128)(2,1)}), bf16[4,1,1]{2,1,0:T(2,128)(2,1)S(1)}, u32[]{:S(2)}, u32[]{:S(2)}) async-start(bf16[4,1,1]{2,1,0:T(2,128)(2,1)} %copy.19), calls=%async_computation | async-start | bytes 4096 | tf_op jit(solution)/shard_map/all_to_all | solution.py:226
  26.1 9.9 %copy-start.8 = (bf16[144,768]{1,0:T(8,128)(2,1)}, bf16[144,768]{1,0:T(8,128)(2,1)S(1)}, u32[]{:S(2)}) copy-start(bf16[144,768]{1,0:T(8,128)(2,1)S(1)} %get-tuple-element.548) | copy-start | bytes 663556
  26.1 9.9 %copy-start.10 = (bf16[144,768]{1,0:T(8,128)(2,1)}, bf16[144,768]{1,0:T(8,128)(2,1)S(1)}, u32[]{:S(2)}) copy-start(bf16[144,768]{1,0:T(8,128)(2,1)S(1)} %get-tuple-element.549) | copy-start | bytes 663556
  26.2 6.4 %collective-permute-start.2 = (bf16[768,128]{1,0:T(8,128)(2,1)S(1)}, bf16[768,128]{1,0:T(8,128)(2,1)S(1)}, u32[]{:S(2)}, u32[]{:S(2)}) collective-permute-start(bf16[768,128]{1,0:T(8,128)(2,1)S(1)} %get-tuple-element.536), channel_id=1, source_target_pairs={{0,1},{1,2},{2,3},{4,5},{5,6},{6,7},{8,9},{9,10},{10,11},{12,13},{... | collective-permute-start | bytes 589832 | tf_op jit(solution)/shard_map/ppermute | solution.py:22
  29.3 6.7 %collective-permute-start.3 = (bf16[768,128]{1,0:T(8,128)(2,1)S(1)}, bf16[768,128]{1,0:T(8,128)(2,1)S(1)}, u32[]{:S(2)}, u32[]{:S(2)}) collective-permute-start(bf16[768,128]{1,0:T(8,128)(2,1)S(1)} %get-tuple-element.537), channel_id=1, source_target_pairs={{1,0},{2,1},{3,2},{5,4},{6,5},{7,6},{9,8},{10,9},{11,10},{13,12},{... | collective-permute-start | bytes 589832 | tf_op jit(solution)/shard_map/ppermute | solution.py:25
  36.8 8.9 %copy-start.7 = (bf16[512,1024]{1,0:T(8,128)(2,1)S(1)}, bf16[512,1024]{1,0:T(8,128)(2,1)}, u32[]{:S(2)}) copy-start(bf16[512,1024]{1,0:T(8,128)(2,1)} %param.30) | copy-start | bytes 3145732
  42.1 9.5 %all-to-all-start.1 = ((bf16[4,2,20736]{2,1,0:T(2,128)(2,1)}), bf16[4,2,20736]{2,1,0:T(2,128)(2,1)S(1)}, u32[]{:S(2)}, u32[]{:S(2)}) async-start(bf16[4,2,20736]{2,1,0:T(2,128)(2,1)} %reshape.444), calls=%async_computation.1 | async-start | bytes 663552 | tf_op jit(solution)/shard_map/all_to_all | solution.py:224
  51.7 44.0 %all-to-all-start.2 = ((bf16[4,512,512]{2,1,0:T(8,128)(2,1)}), bf16[4,512,512]{2,1,0:T(8,128)(2,1)S(1)}, u32[]{:S(2)}, u32[]{:S(2)}) async-start(bf16[4,512,512]{2,1,0:T(8,128)(2,1)} %multiply_add_fusion), calls=%async_computation.2 | async-start | bytes 4194304 | tf_op jit(solution)/shard_map/all_to_all | solution.py:225
  55.5 40.1 %copy-start.13 = (f32[12]{0:T(128)S(1)}, f32[12]{0:T(128)}, u32[]{:S(2)}) copy-start(f32[12]{0:T(128)} %param.33) | copy-start | bytes 148
  95.6 4.8 %copy-start.1 = (bf16[4,512,512]{2,1,0:T(8,128)(2,1)}, bf16[4,512,512]{2,1,0:T(8,128)(2,1)S(1)}, u32[]{:S(2)}) copy-start(bf16[4,512,512]{2,1,0:T(8,128)(2,1)S(1)} %get-tuple-element.353) | copy-start | bytes 6291460 | tf_op jit(solution)/shard_map/cond
  185.2 2.7 copy-start.2
  195.6 2.4 copy-start.3
  195.6 2.4 copy-start.5
  202.9 2.4 copy-start.3
  202.9 2.4 copy-start.5
  210.3 2.4 copy-start.3
  210.3 2.4 copy-start.5
  217.6 2.4 copy-start.3
  217.6 2.4 copy-start.5
  225.0 2.4 copy-start.3
  225.0 2.4 copy-start.5
  282.6 18.6 %copy-start.9 = (bf16[144,768]{1,0:T(8,128)(2,1)S(1)}, bf16[144,768]{1,0:T(8,128)(2,1)}, u32[]{:S(2)}) copy-start(bf16[144,768]{1,0:T(8,128)(2,1)} %copy-done.8) | copy-start | bytes 663556
  282.6 18.6 %copy-start.11 = (bf16[144,768]{1,0:T(8,128)(2,1)S(1)}, bf16[144,768]{1,0:T(8,128)(2,1)}, u32[]{:S(2)}) copy-start(bf16[144,768]{1,0:T(8,128)(2,1)} %copy-done.10) | copy-start | bytes 663556
  287.7 18.1 %all-to-all-start.3 = ((bf16[4,2,20736]{2,1,0:T(2,128)(2,1)}), bf16[4,2,20736]{2,1,0:T(2,128)(2,1)S(1)}, u32[]{:S(2)}, u32[]{:S(2)}) async-start(bf16[4,2,20736]{2,1,0:T(2,128)(2,1)} %reshape.446), calls=%async_computation.3 | async-start | bytes 663552 | tf_op jit(solution)/shard_map/all_to_all | solution.py:242
  319.0 18.7 %collective-permute-start.4 = (bf16[128,1280]{1,0:T(8,128)(2,1)S(1)}, bf16[128,1280]{1,0:T(8,128)(2,1)S(1)}, u32[]{:S(2)}, u32[]{:S(2)}) collective-permute-start(bf16[128,1280]{1,0:T(8,128)(2,1)S(1)} %get-tuple-element.534), channel_id=1, source_target_pairs={{0,4},{4,8},{8,12},{12,16},{16,20},{20,24},{24,28},{1,5},{5,9},{9,... | collective-permute-start | bytes 983048 | tf_op jit(solution)/shard_map/ppermute | solution.py:22
  323.9 15.1 %collective-permute-start.5 = (bf16[128,1280]{1,0:T(8,128)(2,1)S(1)}, bf16[128,1280]{1,0:T(8,128)(2,1)S(1)}, u32[]{:S(2)}, u32[]{:S(2)}) collective-permute-start(bf16[128,1280]{1,0:T(8,128)(2,1)S(1)} %get-tuple-element.535), channel_id=1, source_target_pairs={{4,0},{8,4},{12,8},{16,12},{20,16},{24,20},{28,24},{5,1},{9,5},{13... | collective-permute-start | bytes 983048 | tf_op jit(solution)/shard_map/ppermute | solution.py:25
  339.0 14.8 %collective-permute-start.6 = (bf16[1024,128]{1,0:T(8,128)(2,1)S(1)}, bf16[1024,128]{1,0:T(8,128)(2,1)S(1)}, u32[]{:S(2)}, u32[]{:S(2)}) collective-permute-start(bf16[1024,128]{1,0:T(8,128)(2,1)S(1)} %get-tuple-element.532), channel_id=1, source_target_pairs={{0,1},{1,2},{2,3},{4,5},{5,6},{6,7},{8,9},{9,10},{10,11},{12,13},{... | collective-permute-start | bytes 786440 | tf_op jit(solution)/shard_map/ppermute | solution.py:22
  347.7 8.7 %collective-permute-start.7 = (bf16[1024,128]{1,0:T(8,128)(2,1)S(1)}, bf16[1024,128]{1,0:T(8,128)(2,1)S(1)}, u32[]{:S(2)}, u32[]{:S(2)}) collective-permute-start(bf16[1024,128]{1,0:T(8,128)(2,1)S(1)} %get-tuple-element.533), channel_id=1, source_target_pairs={{1,0},{2,1},{3,2},{5,4},{6,5},{7,6},{9,8},{10,9},{11,10},{13,12},{... | collective-permute-start | bytes 786440 | tf_op jit(solution)/shard_map/ppermute | solution.py:25
  (39 other events, 51.4 us)
where the time goes:
time: 367 us; the launch traced here: 363 us
  other arithmetic  105 us (29%)
  local copies, waits for them, and re-layouts  67.6 us (18%)
  starting transfers between devices  63.8 us (17%)
  matrix products  54.9 us (15%)
  waiting for transfers between devices  54.2 us (15%)
  loops' own time  9.34 us (3%)
  blocking collectives  6.43 us (2%)
    add x12, other arithmetic, forward_kernel(): return (intensity + weight * energy, field_pair.astype(jnp.bfloat16))  37.3 us
    all_to_all x1, waiting for transfers between devices, body(): lax.all_to_all(send_goals, 'col', split_axis=0, concat_axis=0, tiled=True)  34.9 us
    dot_general x14, matrix products, contract_last(): lax.dot_general(leading, trailing, (((1,), (1,)), ((), ())), preferred_el...  29.8 us
    dot_general x12, matrix products, contract_first(): lax.dot_general(leading, trailing, (((0,), (0,)), ((), ())), preferred_el...  25.1 us
    dynamic_slice x24, local copies, waits for them, and re-layouts, spectral_gradient(): lax.scan(backward_kernel, (empty_spec, empty_spec), (pupils[0], pupils[1]...  22.1 us
    ppermute x4, starting transfers between devices, extended_2(): lax.ppermute(lax.slice_in_dim(block, block.shape[dim] - width, None, axis...  20.3 us
    ppermute x4, starting transfers between devices, extended_2(): lax.ppermute(lax.slice_in_dim(block, 0, width, axis=dim), axis, backward)  19.9 us
    another operation x17, other arithmetic  16.4 us
  transfers between devices with their start and end apart: 12, of which 8 were waited for; matrix products, arithmetic and copies ran while one was open for 6% of the time, Pallas kernels for 0%

commit v1 on v0

v1 whole, which is shorter than its diff:
```python
from functools import partial
import math

import jax
import jax.numpy as jnp
import numpy as np
from jax import lax
from jax.experimental import pallas as pl
from jax.experimental.pallas import tpu as pltpu
from jax.sharding import PartitionSpec as P

AMBIT = 128

steepness = 4.0
threshold_level = 1.0
step_rate = 8.0

VMEM_LIMIT = 60 * 1024 * 1024


def round_up(value, unit):
    return -(-value // unit) * unit


def shifted(block, axis, step):
    count = lax.axis_size(axis)
    pairs = [(i, i + step) for i in range(count) if 0 <= i + step < count]
    return lax.ppermute(block, axis, pairs)


def dot(leading, trailing):
    return jnp.dot(leading, trailing, preferred_element_type=jnp.float32)


def half_tables(half, rows, extent):
    frequency = np.arange(half + 1, dtype=np.int64)
    pixels = np.arange(extent, dtype=np.int64)
    phases = np.mod(frequency[:, None] * pixels[None, :], extent).astype(np.float32)
    angles = phases * np.float32(2.0 * math.pi / extent)
    factor = np.float32(1.0 / math.sqrt(extent))
    table = np.zeros((2 * rows, extent), np.float32)
    table[: half + 1] = np.cos(angles) * factor
    table[rows : rows + half + 1] = np.sin(angles) * factor
    return table


def pick_tables(half, rows, lanes):
    size = 2 * half
    row_pick = np.zeros((2 * rows, size), np.float32)
    col_pick = np.zeros((size, 2 * lanes), np.float32)
    for index in range(half):
        row_pick[index, half + index] = 1.0
        col_pick[half + index, index] = 1.0
        row_pick[rows + half - index, index] = 1.0
        col_pick[index, lanes + half - index] = 1.0
    return row_pick, col_pick


def vmem(count):
    return [pl.BlockSpec(memory_space=pltpu.VMEM)] * count


def call(kernel, outs, specs, scratch=(), cost=None, **kwargs):
    return pl.pallas_call(
        kernel,
        out_shape=outs,
        in_specs=specs,
        out_specs=jax.tree.map(lambda _: pl.BlockSpec(memory_space=pltpu.VMEM), outs),
        scratch_shapes=list(scratch),
        cost_estimate=cost,
        compiler_params=pltpu.CompilerParams(vmem_limit_bytes=VMEM_LIMIT),
        **kwargs,
    )


def pupil_kernel(rows, lanes, pupils_ref, weights_ref, row_ref, col_ref, out_ref):
    kernels = pupils_ref.shape[1]

    def one(k, carry):
        scale = jnp.sqrt(jnp.full((1, 1), weights_ref[k], jnp.float32))

        def picked(part):
            values = pupils_ref[part, k] * scale
            high = values.astype(jnp.bfloat16)
            low = (values - high.astype(jnp.float32)).astype(jnp.bfloat16)
            total = None
            for piece in (high, low):
                columns = dot(piece, col_ref[...]).astype(jnp.bfloat16)
                term = dot(row_ref[...], columns)
                total = term if total is None else total + term
            return total

        for part in range(2):
            full = picked(part)
            pos_pos, pos_neg = full[:rows, :lanes], full[:rows, lanes:]
            neg_pos, neg_neg = full[rows:, :lanes], full[rows:, lanes:]
            out_ref[k, 0 + part] = (pos_pos + neg_neg).astype(jnp.bfloat16)
            out_ref[k, 2 + part] = (pos_pos - neg_neg).astype(jnp.bfloat16)
            out_ref[k, 4 + part] = (pos_neg + neg_pos).astype(jnp.bfloat16)
            out_ref[k, 6 + part] = (pos_neg - neg_pos).astype(jnp.bfloat16)
        return carry

    lax.fori_loop(0, kernels, one, 0)


def middle_kernel(mask_ref, table_ref, out_ref):
    tile = mask_ref.shape[0]
    out_ref[...] = dot(
        table_ref[:, AMBIT : AMBIT + tile], mask_ref[...].astype(jnp.bfloat16)
    )


def partial_kernel(mid_ref, top_ref, bottom_ref, table_ref, own_ref, low_ref, high_ref):
    extent = table_ref.shape[1]
    width = mid_ref.shape[1]
    total = mid_ref[...] + dot(table_ref[:, :AMBIT], top_ref[...])
    total = total + dot(table_ref[:, extent - AMBIT :], bottom_ref[...])
    total = total.astype(jnp.bfloat16)
    own_ref[...] = total
    low_ref[...] = total[:, :AMBIT]
    high_ref[...] = total[:, width - AMBIT :]


def core_kernel(
    rows,
    lanes,
    slots,
    live_ref,
    own_ref,
    left_ref,
    right_ref,
    goal_ref,
    pupil_ref,
    row_ref,
    row_t_ref,
    col_ref,
    col_t_ref,
    *rest,
):
    outs = rest[:slots]
    ext_ref, amp_ref, sec_ref, field_ref, total_ref, slope_ref, back_ref, wave_ref, sum_ref = rest[
        slots:
    ]
    width = own_ref.shape[1]
    tile = goal_ref.shape[0]
    extent = row_ref.shape[1]
    kernels = pupil_ref.shape[0]
    inner = slice(AMBIT, AMBIT + tile)
    ext_ref[:, :AMBIT] = left_ref[...]
    ext_ref[:, AMBIT : AMBIT + width] = own_ref[...]
    ext_ref[:, AMBIT + width :] = right_ref[...]

    def pupil(k, index):
        return pupil_ref[k, index].astype(jnp.float32)

    for slot in range(slots):
        out_ref = outs[slot]
        live = live_ref[0, slot] > 0

        @pl.when(jnp.logical_not(live))
        def _():
            out_ref[...] = jnp.zeros_like(out_ref)

        @pl.when(live)
        def _():
            spec = dot(ext_ref[:, slot * tile : slot * tile + extent], col_t_ref[...])
            cc, cs = spec[:rows, :lanes], spec[:rows, lanes:]
            sc, ss = spec[rows:, :lanes], spec[rows:, lanes:]
            sum_ref[0] = cc - ss
            sum_ref[1] = sc + cs
            sum_ref[2] = cc + ss
            sum_ref[3] = sc - cs

            def amplitude(k, carry):
                u, v, m, n = sum_ref[0], sum_ref[1], sum_ref[2], sum_ref[3]
                pr, pi, mr, mi = (pupil(k, index) for index in range(4))
                big_re = pr * u + mi * v
                big_im = pi * u - mr * v
                small_re = mr * u + pi * v
                small_im = mi * u - pr * v
                pr, pi, mr, mi = (pupil(k, index) for index in range(4, 8))
                big_re2 = pr * m + mi * n
                big_im2 = pi * m - mr * n
                small_re2 = mr * m + pi * n
                small_im2 = mi * m - pr * n
                base = pl.multiple_of(k * 4 * rows, 16)

                def put(place, left, right):
                    where = pl.ds(base + place * rows, rows)
                    amp_ref[where, :lanes] = left.astype(jnp.bfloat16)
                    amp_ref[where, lanes:] = right.astype(jnp.bfloat16)

                put(0, big_re + big_re2, small_im2 - small_im)
                put(1, -(small_im + small_im2), big_re2 - big_re)
                put(2, big_im + big_im2, small_re - small_re2)
                put(3, small_re + small_re2, big_im2 - big_im)
                return carry

            lax.fori_loop(0, kernels, amplitude, 0)

            def section(k, carry):
                where = pl.ds(pl.multiple_of(k * 4 * rows, 16), 4 * rows)
                sec_ref[where] = dot(amp_ref[where], col_ref[:, inner]).astype(jnp.bfloat16)
                return carry

            lax.fori_loop(0, kernels, section, 0)
            total_ref[...] = jnp.zeros_like(total_ref)

            def field(k, carry):
                where_re = pl.ds(pl.multiple_of(k * 4 * rows, 16), 2 * rows)
                where_im = pl.ds(pl.multiple_of(k * 4 * rows + 2 * rows, 16), 2 * rows)
                real = dot(row_t_ref[inner], sec_ref[where_re])
                imag = dot(row_t_ref[inner], sec_ref[where_im])
                total_ref[...] += real * real + imag * imag
                field_ref[k, 0] = real.astype(jnp.bfloat16)
                field_ref[k, 1] = imag.astype(jnp.bfloat16)
                return carry

            lax.fori_loop(0, kernels, field, 0)
            resist = 1.0 / (1.0 + jnp.exp(-steepness * (total_ref[...] - threshold_level)))
            goal = goal_ref[:, slot * tile : (slot + 1) * tile].astype(jnp.float32)
            slope = (resist - goal) * (2.0 * steepness) * resist * (1.0 - resist)
            slope_ref[...] = slope.astype(jnp.bfloat16)

            def back(k, carry):
                for part in range(2):
                    cotangent = slope_ref[...] * field_ref[k, part]
                    where = pl.ds(pl.multiple_of((k * 2 + part) * 2 * rows, 16), 2 * rows)
                    back_ref[where] = dot(row_ref[:, inner], cotangent).astype(jnp.bfloat16)
                return carry

            lax.fori_loop(0, kernels, back, 0)

            def wave(k, carry):
                where = pl.ds(pl.multiple_of(k * 4 * rows, 16), 4 * rows)
                wave_ref[where] = dot(back_ref[where], col_t_ref[inner])
                return carry

            lax.fori_loop(0, kernels, wave, 0)
            sum_ref[...] = jnp.zeros_like(sum_ref)

            def adjoint(k, carry):
                base = pl.multiple_of(k * 4 * rows, 8)

                def quarters(place):
                    cos_rows = pl.ds(base + place * 2 * rows, rows)
                    sin_rows = pl.ds(base + place * 2 * rows + rows, rows)
                    return (
                        wave_ref[cos_rows, :lanes],
                        wave_ref[cos_rows, lanes:],
                        wave_ref[sin_rows, :lanes],
                        wave_ref[sin_rows, lanes:],
                    )

                rcc, rcs, rsc, rss = quarters(0)
                icc, ics, isc, iss = quarters(1)
                ur, ui, vr, vi = rcc - rss, icc - iss, rsc + rcs, isc + ics
                pr, pi, mr, mi = (pupil(k, index) for index in range(4))
                sum_ref[0] += pr * ur + pi * ui + mr * vi - mi * vr
                sum_ref[1] += mr * ui - mi * ur - pr * vr - pi * vi
                ur, ui, vr, vi = rcc + rss, icc + iss, rsc - rcs, isc - ics
                pr, pi, mr, mi = (pupil(k, index) for index in range(4, 8))
                sum_ref[2] += pr * ur + pi * ui + mr * vi - mi * vr
                sum_ref[3] += mr * ui - mi * ur - pr * vr - pi * vi
                return carry

            lax.fori_loop(0, kernels, adjoint, 0)
            out_ref[:rows, :lanes] = (sum_ref[0] + sum_ref[2]).astype(jnp.bfloat16)
            out_ref[:rows, lanes:] = (sum_ref[3] - sum_ref[1]).astype(jnp.bfloat16)
            out_ref[rows:, :lanes] = (-(sum_ref[1] + sum_ref[3])).astype(jnp.bfloat16)
            out_ref[rows:, lanes:] = (sum_ref[2] - sum_ref[0]).astype(jnp.bfloat16)


def returned_kernel(tile, slots, *refs):
    spectral = refs[: slots + 2]
    row_t_ref, col_ref, out_ref, up_ref, down_ref = refs[slots + 2 : slots + 7]
    sum_ref = refs[slots + 7]
    width = out_ref.shape[1]
    extent = row_t_ref.shape[0]
    sum_ref[...] = jnp.zeros_like(sum_ref)
    for place, ref in zip(range(-1, slots + 1), spectral):
        start = place * tile - AMBIT
        low, high = max(0, start), min(width, start + extent)
        sum_ref[:, low:high] += dot(ref[...], col_ref[:, low - start : high - start])
    mixed = sum_ref[...].astype(jnp.bfloat16)
    out_ref[...] = mixed
    up_ref[...] = dot(row_t_ref[:AMBIT], mixed).astype(jnp.bfloat16)
    down_ref[...] = dot(row_t_ref[extent - AMBIT :], mixed).astype(jnp.bfloat16)


def update_kernel(mask_ref, mixed_ref, row_t_ref, out_ref):
    tile = mask_ref.shape[0]
    out_ref[...] = mask_ref[...] - step_rate * dot(
        row_t_ref[AMBIT : AMBIT + tile], mixed_ref[...]
    )


def body(mask, target, live, pupils, weights):
    tile, width = mask.shape
    slots = live.shape[1]
    kernels, size = pupils.shape[1], pupils.shape[2]
    half = size // 2
    rows, lanes = round_up(half + 1, 16), round_up(half + 1, 128)
    extent = tile + 2 * AMBIT
    row_np = half_tables(half, rows, extent)
    col_np = half_tables(half, lanes, extent)
    row_pick, col_pick = (
        jnp.asarray(pick, jnp.bfloat16) for pick in pick_tables(half, rows, lanes)
    )
    row_table, row_table_t = jnp.asarray(row_np, jnp.bfloat16), jnp.asarray(row_np.T, jnp.bfloat16)
    col_table, col_table_t = jnp.asarray(col_np, jnp.bfloat16), jnp.asarray(col_np.T, jnp.bfloat16)
    bf16, f32 = jnp.bfloat16, jnp.float32
    shape = jax.ShapeDtypeStruct
    smem = pl.BlockSpec(memory_space=pltpu.SMEM)

    def cost(us):
        return pl.CostEstimate(
            flops=int(us * 5e8), bytes_accessed=int(us * 1e6), transcendentals=0
        )

    top = shifted(mask[tile - AMBIT :].astype(bf16), "row", 1)
    bottom = shifted(mask[:AMBIT].astype(bf16), "row", -1)
    middle = call(middle_kernel, shape((2 * rows, width), f32), vmem(2), cost=cost(2))(
        mask, row_table
    )
    quads = call(
        partial(pupil_kernel, rows, lanes),
        shape((kernels, 8, rows, lanes), bf16),
        [*vmem(1), smem, *vmem(2)],
        cost=cost(5),
    )(pupils, weights, row_pick, col_pick)
    own, low, high = call(
        partial_kernel,
        (
            shape((2 * rows, width), bf16),
            shape((2 * rows, AMBIT), bf16),
            shape((2 * rows, AMBIT), bf16),
        ),
        vmem(4),
        cost=cost(1),
    )(middle, top, bottom, row_table)
    left = shifted(high, "col", 1)
    right = shifted(low, "col", -1)
    spectral = call(
        partial(core_kernel, rows, lanes, slots),
        tuple(shape((2 * rows, 2 * lanes), bf16) for _ in range(slots)),
        [smem, *vmem(9)],
        scratch=[
            pltpu.VMEM((2 * rows, width + 2 * AMBIT), bf16),
            pltpu.VMEM((kernels * 4 * rows, 2 * lanes), bf16),
            pltpu.VMEM((kernels * 4 * rows, tile), bf16),
            pltpu.VMEM((kernels, 2, tile, tile), bf16),
            pltpu.VMEM((tile, tile), f32),
            pltpu.VMEM((tile, tile), bf16),
            pltpu.VMEM((kernels * 4 * rows, tile), bf16),
            pltpu.VMEM((kernels * 4 * rows, 2 * lanes), f32),
            pltpu.VMEM((4, rows, lanes), f32),
        ],
        cost=cost(20),
    )(live, own, left, right, target, quads, row_table, row_table_t, col_table, col_table_t)
    before = shifted(spectral[-1], "col", 1)
    after = shifted(spectral[0], "col", -1)
    mixed, up, down = call(
        partial(returned_kernel, tile, slots),
        (shape((2 * rows, width), bf16), shape((AMBIT, width), bf16), shape((AMBIT, width), bf16)),
        vmem(slots + 4),
        scratch=[pltpu.VMEM((2 * rows, width), f32)],
        cost=cost(1),
    )(before, *spectral, after, row_table_t, col_table)
    from_above = shifted(down, "row", 1)
    from_below = shifted(up, "row", -1)
    base = call(update_kernel, shape((tile, width), f32), vmem(3), cost=cost(2))(
        mask, mixed, row_table_t
    )
    return call_rims(base, from_above, from_below)


def rims_kernel(above_ref, below_ref, base_ref, out_ref):
    @pl.when(pl.program_id(0) == 0)
    def _():
        out_ref[...] = base_ref[...] - step_rate * above_ref[...].astype(jnp.float32)

    @pl.when(pl.program_id(0) > 0)
    def _():
        out_ref[...] = base_ref[...] - step_rate * below_ref[...].astype(jnp.float32)


def call_rims(base, from_above, from_below):
    tile, width = base.shape
    last = tile // AMBIT - 1
    edge = pl.BlockSpec((AMBIT, width), lambda i: (0, 0))
    moving = pl.BlockSpec((AMBIT, width), lambda i: (i * last, 0))
    return pl.pallas_call(
        rims_kernel,
        out_shape=jax.ShapeDtypeStruct((tile, width), jnp.float32),
        grid=(2,),
        in_specs=[edge, edge, moving],
        out_specs=moving,
        input_output_aliases={2: 0},
    )(from_above, from_below, base)


def solution(mesh):
    placed = (P("row", "col"), P("row", "col"), P("row", "col"), P(), P())
    return jax.shard_map(
        body, mesh=mesh, in_specs=placed, out_specs=P("row", "col"), check_vma=False
    )
```

time: 367 us -> 99.6 us (0.27); the launches traced: 363 us -> 99.6 us
  other arithmetic: 105 us -> 1.74 us
  local copies, waits for them, and re-layouts: 67.6 us -> 3.04 us
  matrix products: 54.9 us -> 0 us
  waiting for transfers between devices: 54.2 us -> 7.36 us
  Pallas kernels: 0 us -> 25.3 us
  loops' own time: 9.34 us -> 0 us
  blocking collectives: 6.43 us -> 0 us
    add x29 -> x0, other arithmetic: 56.3 us -> none  [the longest x12 37.3 us: forward_kernel(): return (intensity + weight * energy, field_pair.astype(jnp.bfloat16))]
    dot_general x26 -> x0, matrix products: 54.9 us -> none  [the longest x14 29.8 us: contract_last(): lax.dot_general(leading, trailing, (((1,), (1,)), ((), ())), preferred_el...]
    all_to_all x4 -> x0, waiting for transfers between devices: 43.6 us -> none  [the longest x1 34.9 us: body(): lax.all_to_all(send_goals, 'col', split_axis=0, concat_axis=0, tiled=True)]
    dynamic_slice x49 -> x0, local copies, waits for them, and re-layouts: 37.8 us -> none  [the longest x24 22.1 us: spectral_gradient(): lax.scan(backward_kernel, (empty_spec, empty_spec), (pupils[0], pupils[1]...]
    pallas_call x0 -> x7, Pallas kernels: none -> 25.3 us  [the longest x1 8.8 us: body(): call(partial(pupil_kernel, rows, lanes), shape((kernels, 8, rows, lanes),...]
    all_to_all x4 -> x0, starting transfers between devices: 23.7 us -> none  [the longest x1 11 us: body(): lax.all_to_all(answers, 'col', split_axis=0, concat_axis=0, tiled=True)]
    ppermute x8, starting transfers between devices: 40.2 us -> 62.1 us  [shifted(): return lax.ppermute(block, axis, pairs)]
    another operation x23 -> x1, other arithmetic: 17.7 us -> 1.74 us
  transfers between devices with their start and end apart: 12 -> 8, of which waited for: 8 -> 4; matrix products, arithmetic and copies ran while one was open for 6% -> 0% of each run, Pallas kernels for 0% -> 15%
where the time goes in v1:
time: 99.6 us
  starting transfers between devices  62.1 us (62%)
  Pallas kernels  25.3 us (25%)
  waiting for transfers between devices  7.36 us (7%)
  local copies, waits for them, and re-layouts  3.04 us (3%)
  other arithmetic  1.74 us (2%)
    ppermute x8, starting transfers between devices, shifted(): return lax.ppermute(block, axis, pairs)  62.1 us
    pallas_call x1, Pallas kernels, body(): call(partial(pupil_kernel, rows, lanes), shape((kernels, 8, rows, lanes),...  8.8 us
    ppermute x8, waiting for transfers between devices, shifted(): return lax.ppermute(block, axis, pairs)  7.36 us
    pallas_call x1, Pallas kernels, body(): call(update_kernel, shape((tile, width), f32), vmem(3), cost=cost(2))  3.47 us
    pallas_call x1, Pallas kernels, body(): call(partial(core_kernel, rows, lanes, slots), tuple((shape((2 * rows, 2...  3.09 us
    unnamed x16, local copies, waits for them, and re-layouts  3 us
    pallas_call x1, Pallas kernels, body(): call(middle_kernel, shape((2 * rows, width), f32), vmem(2), cost=cost(2))  2.78 us
    pallas_call x1, Pallas kernels, body(): call(partial(returned_kernel, tile, slots), (shape((2 * rows, width), bf1...  2.58 us
  transfers between devices with their start and end apart: 8, of which 4 were waited for; matrix products, arithmetic and copies ran while one was open for 0% of the time, Pallas kernels for 15%

profile of v1, /device:TPU:11, one launch (start us, length us, event | category | flops | bytes accessed | tf_op | source)
XLA Modules:
  0.0 99.6 jit_solution(16446554874883251818)
XLA Ops:
  0.0 1.7 %convert.4 = bf16[512,1024]{1,0:T(8,128)(2,1)S(1)} convert(f32[512,1024]{1,0:T(8,128)} %mask_ref.3) | non-fusion elementwise | flops 524288 | bytes 3145728 | tf_op jit(solution)/shard_map/convert.1
  1.8 2.6 %collective-permute-start.1 = (bf16[128,1024]{1,0:T(8,128)(2,1)S(1)}, bf16[128,1024]{1,0:T(8,128)(2,1)S(1)}, u32[]{:S(2)}, u32[]{:S(2)}) collective-permute-start(bf16[128,1024]{1,0:T(8,128)(2,1)S(1)} %get-tuple-element.21), channel_id=1, source_target_pairs={{4,0},{8,4},{12,8},{16,12},{20,16},{24,20},{28,24},{5,1},{9,5},{13... | collective-permute-start | bytes 786440 | tf_op jit(solution)/shard_map/ppermute | solution.py:28
  4.4 3.9 %collective-permute-start = (bf16[128,1024]{1,0:T(8,128)(2,1)S(1)}, bf16[128,1024]{1,0:T(8,128)(2,1)S(1)}, u32[]{:S(2)}, u32[]{:S(2)}) collective-permute-start(bf16[128,1024]{1,0:T(8,128)(2,1)S(1)} %get-tuple-element.22), channel_id=1, source_target_pairs={{0,4},{4,8},{8,12},{12,16},{16,20},{20,24},{24,28},{1,5},{5,9},{9,... | collective-permute-start | bytes 786440 | tf_op jit(solution)/shard_map/ppermute | solution.py:28
  8.3 2.8 %shard_map.109.mid_ref = f32[160,1024]{1,0:T(8,128)} custom-call(f32[512,1024]{1,0:T(8,128)} %mask_ref.3, bf16[160,768]{1,0:T(8,128)(2,1)} %constant.14.clone.table_ref.row_ref), custom_call_target="tpu_custom_call" | custom-call | flops 1000000000 | bytes 2000000 | tf_op jit(solution)/shard_map/pallas_call | solution.py:323
  11.0 0.2 collective-permute-done.1.bottom_ref
  11.2 0.3 collective-permute-done.top_ref
  11.6 0.3 copy-done.2
  11.9 0.7 copy-done.3
  12.6 2.4 %shard_map.110 = (bf16[160,1024]{1,0:T(8,128)(2,1)}, bf16[160,128]{1,0:T(8,128)(2,1)}, bf16[160,128]{1,0:T(8,128)(2,1)}) custom-call(f32[160,1024]{1,0:T(8,128)} %shard_map.109.mid_ref, bf16[128,1024]{1,0:T(8,128)(2,1)} %copy-done.3, bf16[128,1024]{1,0:T(8,128)(2,1)} %copy-done.2, bf16[160,768]{1,0:T(8,128)(2,1)} %constant.14.clone.table_ref.row_ref), custom_call_target="tpu_custom_call" | custom-call | flops 500000000 | bytes 1000000 | tf_op jit(solution)/shard_map/pallas_call | solution.py:332
  15.0 3.2 %collective-permute-start.2 = (bf16[160,128]{1,0:T(8,128)(2,1)}, bf16[160,128]{1,0:T(8,128)(2,1)S(1)}, u32[]{:S(2)}, u32[]{:S(2)}) collective-permute-start(bf16[160,128]{1,0:T(8,128)(2,1)} %get-tuple-element.14), channel_id=1, source_target_pairs={{0,1},{1,2},{2,3},{4,5},{5,6},{6,7},{8,9},{9,10},{10,11},{12,13},{... | collective-permute-start | bytes 122888 | tf_op jit(solution)/shard_map/ppermute | solution.py:28
  18.2 2.1 %collective-permute-start.3 = (bf16[160,128]{1,0:T(8,128)(2,1)}, bf16[160,128]{1,0:T(8,128)(2,1)S(1)}, u32[]{:S(2)}, u32[]{:S(2)}) collective-permute-start(bf16[160,128]{1,0:T(8,128)(2,1)} %get-tuple-element.15), channel_id=1, source_target_pairs={{1,0},{2,1},{3,2},{5,4},{6,5},{7,6},{9,8},{10,9},{11,10},{13,12},{... | collective-permute-start | bytes 122888 | tf_op jit(solution)/shard_map/ppermute | solution.py:28
  20.2 8.8 %shard_map.111.pupil_ref = bf16[12,8,80,128]{3,2,1,0:T(8,128)(2,1)} custom-call(f32[2,12,144,144]{3,2,1,0:T(8,128)} %pupils_ref.1, f32[12]{0:T(128)} %weights_ref.1, bf16[160,144]{1,0:T(8,128)(2,1)} %constant.12.clone.row_ref, bf16[144,256]{1,0:T(8,128)(2,1)} %constant.13.clone.col_ref), custom_call_target="tpu_custom_call" | custom-call | flops 2500000000 | bytes 5000000 | tf_op jit(solution)/shard_map/pallas_call | solution.py:326
  29.0 0.0 collective-permute-done.2.left_ref
  29.0 0.0 collective-permute-done.3.right_ref
  29.1 0.0 copy-start.7
  29.1 0.6 copy-done.6
  29.7 0.0 copy-done.7
  29.7 3.1 %shard_map.112 = (bf16[160,256]{1,0:T(8,128)(2,1)}, bf16[160,256]{1,0:T(8,128)(2,1)}) custom-call(s32[1,2]{1,0:T(1,128)} %live_ref.1, bf16[160,1024]{1,0:T(8,128)(2,1)} %get-tuple-element.13.own_ref, bf16[160,128]{1,0:T(8,128)(2,1)} %copy-done.6, bf16[160,128]{1,0:T(8,128)(2,1)} %copy-done.7, bf16[512,1024]{1,0:T(8,128)(2,1)} %goal_ref.1, ...), custom_call_target="tpu_custom_call" | custom-call | flops 10000000000 | bytes 20000000 | tf_op jit(solution)/shard_map/pallas_call | solution.py:344
  32.8 40.0 %collective-permute-start.4 = (bf16[160,256]{1,0:T(8,128)(2,1)}, bf16[160,256]{1,0:T(8,128)(2,1)S(1)}, u32[]{:S(2)}, u32[]{:S(2)}) collective-permute-start(bf16[160,256]{1,0:T(8,128)(2,1)} %get-tuple-element.16.refs_2_), channel_id=1, source_target_pairs={{0,1},{1,2},{2,3},{4,5},{5,6},{6,7},{8,9},{9,10},{10,11},{12,13},{... | collective-permute-start | bytes 245768 | tf_op jit(solution)/shard_map/ppermute | solution.py:28
  72.8 1.9 %collective-permute-start.5 = (bf16[160,256]{1,0:T(8,128)(2,1)}, bf16[160,256]{1,0:T(8,128)(2,1)S(1)}, u32[]{:S(2)}, u32[]{:S(2)}) collective-permute-start(bf16[160,256]{1,0:T(8,128)(2,1)} %get-tuple-element.17.refs_1_), channel_id=1, source_target_pairs={{1,0},{2,1},{3,2},{5,4},{6,5},{7,6},{9,8},{10,9},{11,10},{13,12},{... | collective-permute-start | bytes 245768 | tf_op jit(solution)/shard_map/ppermute | solution.py:28
  74.7 0.0 collective-permute-done.4.refs_0_
  74.7 0.0 copy-start.4
  74.7 3.4 %collective-permute-done.5.refs_3_ = bf16[160,256]{1,0:T(8,128)(2,1)S(1)} collective-permute-done((bf16[160,256]{1,0:T(8,128)(2,1)}, bf16[160,256]{1,0:T(8,128)(2,1)S(1)}, u32[]{:S(2)}, u32[]{:S(2)}) %collective-permute-start.5) | collective-permute-done | bytes 81952 | tf_op jit(solution)/shard_map/ppermute | solution.py:28
  78.2 0.6 copy-done.5
  78.8 2.6 %shard_map.113 = (bf16[160,1024]{1,0:T(8,128)(2,1)}, bf16[128,1024]{1,0:T(8,128)(2,1)}, bf16[128,1024]{1,0:T(8,128)(2,1)}) custom-call(bf16[160,256]{1,0:T(8,128)(2,1)} %copy-done.4, bf16[160,256]{1,0:T(8,128)(2,1)} %get-tuple-element.17.refs_1_, bf16[160,256]{1,0:T(8,128)(2,1)} %get-tuple-element.16.refs_2_, bf16[160,256]{1,0:T(8,128)(2,1)} %copy-done.5, ...), custom_call_target="tpu_custom_call" | custom-call | flops 500000000 | bytes 1000000 | tf_op jit(solution)/shard_map/pallas_call | solution.py:363
  81.4 6.5 %collective-permute-start.6 = (bf16[128,1024]{1,0:T(8,128)(2,1)}, bf16[128,1024]{1,0:T(8,128)(2,1)S(1)}, u32[]{:S(2)}, u32[]{:S(2)}) collective-permute-start(bf16[128,1024]{1,0:T(8,128)(2,1)} %get-tuple-element.18), channel_id=1, source_target_pairs={{0,4},{4,8},{8,12},{12,16},{16,20},{20,24},{24,28},{1,5},{5,9},{9,... | collective-permute-start | bytes 786440 | tf_op jit(solution)/shard_map/ppermute | solution.py:28
  87.9 1.9 %collective-permute-start.7 = (bf16[128,1024]{1,0:T(8,128)(2,1)}, bf16[128,1024]{1,0:T(8,128)(2,1)S(1)}, u32[]{:S(2)}, u32[]{:S(2)}) collective-permute-start(bf16[128,1024]{1,0:T(8,128)(2,1)} %get-tuple-element.19), channel_id=1, source_target_pairs={{4,0},{8,4},{12,8},{16,12},{20,16},{24,20},{28,24},{5,1},{9,5},{13... | collective-permute-start | bytes 786440 | tf_op jit(solution)/shard_map/ppermute | solution.py:28
  89.8 3.5 %shard_map.114.base_ref = f32[512,1024]{1,0:T(8,128)} custom-call(f32[512,1024]{1,0:T(8,128)} %mask_ref.3, bf16[160,1024]{1,0:T(8,128)(2,1)} %get-tuple-element.20.mixed_ref, bf16[768,160]{1,0:T(8,128)(2,1)} %constant.15.clone.row_t_ref.refs_4_), custom_call_target="tpu_custom_call" | custom-call | flops 1000000000 | bytes 2000000 | tf_op jit(solution)/shard_map/pallas_call | solution.py:372
  93.3 0.0 collective-permute-done.6.above_ref
  93.3 3.4 %collective-permute-done.7.below_ref = bf16[128,1024]{1,0:T(8,128)(2,1)S(1)} collective-permute-done((bf16[128,1024]{1,0:T(8,128)(2,1)}, bf16[128,1024]{1,0:T(8,128)(2,1)S(1)}, u32[]{:S(2)}, u32[]{:S(2)}) %collective-permute-start.7) | collective-permute-done | bytes 262176 | tf_op jit(solution)/shard_map/ppermute | solution.py:28
  96.7 0.7 copy-done.1
  97.4 2.2 %shard_map.115 = f32[512,1024]{1,0:T(8,128)} custom-call(bf16[128,1024]{1,0:T(8,128)(2,1)} %copy-done, bf16[128,1024]{1,0:T(8,128)(2,1)} %copy-done.1, f32[512,1024]{1,0:T(8,128)} %shard_map.114.base_ref), custom_call_target="tpu_custom_call", output_to_operand_aliasing={{}: (2, {})} | custom-call | tf_op jit(solution)/shard_map/pallas_call | solution.py:393
  (9 shorter events, 0.0 us)
Async XLA Ops:
  1.8 9.4 %collective-permute-start.1 = (bf16[128,1024]{1,0:T(8,128)(2,1)S(1)}, bf16[128,1024]{1,0:T(8,128)(2,1)S(1)}, u32[]{:S(2)}, u32[]{:S(2)}) collective-permute-start(bf16[128,1024]{1,0:T(8,128)(2,1)S(1)} %get-tuple-element.21), channel_id=1, source_target_pairs={{4,0},{8,4},{12,8},{16,12},{20,16},{24,20},{28,24},{5,1},{9,5},{13... | collective-permute-start | bytes 786440 | tf_op jit(solution)/shard_map/ppermute | solution.py:28
  4.4 7.2 %collective-permute-start = (bf16[128,1024]{1,0:T(8,128)(2,1)S(1)}, bf16[128,1024]{1,0:T(8,128)(2,1)S(1)}, u32[]{:S(2)}, u32[]{:S(2)}) collective-permute-start(bf16[128,1024]{1,0:T(8,128)(2,1)S(1)} %get-tuple-element.22), channel_id=1, source_target_pairs={{0,4},{4,8},{8,12},{12,16},{16,20},{20,24},{24,28},{1,5},{5,9},{9,... | collective-permute-start | bytes 786440 | tf_op jit(solution)/shard_map/ppermute | solution.py:28
  11.2 0.7 copy-start.2
  11.9 0.7 copy-start.3
  15.0 14.1 %collective-permute-start.2 = (bf16[160,128]{1,0:T(8,128)(2,1)}, bf16[160,128]{1,0:T(8,128)(2,1)S(1)}, u32[]{:S(2)}, u32[]{:S(2)}) collective-permute-start(bf16[160,128]{1,0:T(8,128)(2,1)} %get-tuple-element.14), channel_id=1, source_target_pairs={{0,1},{1,2},{2,3},{4,5},{5,6},{6,7},{8,9},{9,10},{10,11},{12,13},{... | collective-permute-start | bytes 122888 | tf_op jit(solution)/shard_map/ppermute | solution.py:28
  18.2 10.9 %collective-permute-start.3 = (bf16[160,128]{1,0:T(8,128)(2,1)}, bf16[160,128]{1,0:T(8,128)(2,1)S(1)}, u32[]{:S(2)}, u32[]{:S(2)}) collective-permute-start(bf16[160,128]{1,0:T(8,128)(2,1)} %get-tuple-element.15), channel_id=1, source_target_pairs={{1,0},{2,1},{3,2},{5,4},{6,5},{7,6},{9,8},{10,9},{11,10},{13,12},{... | collective-permute-start | bytes 122888 | tf_op jit(solution)/shard_map/ppermute | solution.py:28
  29.0 0.6 copy-start.6
  29.1 0.6 copy-start.7
  32.8 41.9 %collective-permute-start.4 = (bf16[160,256]{1,0:T(8,128)(2,1)}, bf16[160,256]{1,0:T(8,128)(2,1)S(1)}, u32[]{:S(2)}, u32[]{:S(2)}) collective-permute-start(bf16[160,256]{1,0:T(8,128)(2,1)} %get-tuple-element.16.refs_2_), channel_id=1, source_target_pairs={{0,1},{1,2},{2,3},{4,5},{5,6},{6,7},{8,9},{9,10},{10,11},{12,13},{... | collective-permute-start | bytes 245768 | tf_op jit(solution)/shard_map/ppermute | solution.py:28
  72.8 5.4 %collective-permute-start.5 = (bf16[160,256]{1,0:T(8,128)(2,1)}, bf16[160,256]{1,0:T(8,128)(2,1)S(1)}, u32[]{:S(2)}, u32[]{:S(2)}) collective-permute-start(bf16[160,256]{1,0:T(8,128)(2,1)} %get-tuple-element.17.refs_1_), channel_id=1, source_target_pairs={{1,0},{2,1},{3,2},{5,4},{6,5},{7,6},{9,8},{10,9},{11,10},{13,12},{... | collective-permute-start | bytes 245768 | tf_op jit(solution)/shard_map/ppermute | solution.py:28
  74.7 3.5 %copy-start.4 = (bf16[160,256]{1,0:T(8,128)(2,1)}, bf16[160,256]{1,0:T(8,128)(2,1)S(1)}, u32[]{:S(2)}) copy-start(bf16[160,256]{1,0:T(8,128)(2,1)S(1)} %collective-permute-done.4.refs_0_) | copy-start | bytes 245764
  78.2 0.6 copy-start.5
  81.4 11.9 %collective-permute-start.6 = (bf16[128,1024]{1,0:T(8,128)(2,1)}, bf16[128,1024]{1,0:T(8,128)(2,1)S(1)}, u32[]{:S(2)}, u32[]{:S(2)}) collective-permute-start(bf16[128,1024]{1,0:T(8,128)(2,1)} %get-tuple-element.18), channel_id=1, source_target_pairs={{0,4},{4,8},{8,12},{12,16},{16,20},{20,24},{24,28},{1,5},{5,9},{9,... | collective-permute-start | bytes 786440 | tf_op jit(solution)/shard_map/ppermute | solution.py:28
  87.9 8.8 %collective-permute-start.7 = (bf16[128,1024]{1,0:T(8,128)(2,1)}, bf16[128,1024]{1,0:T(8,128)(2,1)S(1)}, u32[]{:S(2)}, u32[]{:S(2)}) collective-permute-start(bf16[128,1024]{1,0:T(8,128)(2,1)} %get-tuple-element.19), channel_id=1, source_target_pairs={{4,0},{8,4},{12,8},{16,12},{20,16},{24,20},{28,24},{5,1},{9,5},{13... | collective-permute-start | bytes 786440 | tf_op jit(solution)/shard_map/ppermute | solution.py:28
  93.3 3.4 %copy-start = (bf16[128,1024]{1,0:T(8,128)(2,1)}, bf16[128,1024]{1,0:T(8,128)(2,1)S(1)}, u32[]{:S(2)}) copy-start(bf16[128,1024]{1,0:T(8,128)(2,1)S(1)} %collective-permute-done.6.above_ref) | copy-start | bytes 786436
  96.7 0.7 copy-start.1

commit v2 on v1

v2 whole, which is shorter than its diff:
```python
from functools import partial
import math

import jax
import jax.numpy as jnp
import numpy as np
from jax import lax
from jax.experimental import pallas as pl
from jax.experimental.pallas import tpu as pltpu
from jax.sharding import PartitionSpec as P

AMBIT = 128
LANE = 128

steepness = 4.0
threshold_level = 1.0
step_rate = 8.0

MIB = 1024 * 1024


def round_up(value, unit):
    return -(-value // unit) * unit


def moved(block, axis, target_of):
    count = lax.axis_size(axis)
    pairs = [(i, target_of(i)) for i in range(count)]
    return lax.ppermute(block, axis, [(i, j) for i, j in pairs if j is not None and 0 <= j < count])


def dot(leading, trailing):
    return jnp.dot(leading, trailing, preferred_element_type=jnp.float32)


def half_tables(half, rows, extent):
    frequency = np.arange(half + 1, dtype=np.int64)
    pixels = np.arange(extent, dtype=np.int64)
    phases = np.mod(frequency[:, None] * pixels[None, :], extent).astype(np.float32)
    angles = phases * np.float32(2.0 * math.pi / extent)
    factor = np.float32(1.0 / math.sqrt(extent))
    table = np.zeros((2 * rows, extent), np.float32)
    table[: half + 1] = np.cos(angles) * factor
    table[rows : rows + half + 1] = np.sin(angles) * factor
    return table


def pick_tables(half, rows, lanes):
    size = 2 * half
    row_pick = np.zeros((2 * rows, size), np.float32)
    col_pick = np.zeros((size, 2 * lanes), np.float32)
    for index in range(half):
        row_pick[index, half + index] = 1.0
        col_pick[half + index, index] = 1.0
        row_pick[rows + half - index, index] = 1.0
        col_pick[index, lanes + half - index] = 1.0
    return row_pick, col_pick


def vmem(count):
    return [pl.BlockSpec(memory_space=pltpu.VMEM)] * count


def call(kernel, outs, specs, scratch=(), limit=16, us=1, **kwargs):
    return pl.pallas_call(
        kernel,
        out_shape=outs,
        in_specs=specs,
        out_specs=jax.tree.map(lambda _: pl.BlockSpec(memory_space=pltpu.VMEM), outs),
        scratch_shapes=list(scratch),
        cost_estimate=pl.CostEstimate(
            flops=int(us * 5e8), bytes_accessed=int(us * 1e6), transcendentals=0
        ),
        compiler_params=pltpu.CompilerParams(vmem_limit_bytes=limit * MIB),
        **kwargs,
    )


def pupil_steps(rows, lanes, first, last, pupils_ref, weights_ref, row_ref, col_ref, out_ref):
    for k in range(first, last):
        scale = jnp.sqrt(jnp.full((1, 1), weights_ref[k] * (0.5 * steepness), jnp.float32))
        for part in range(2):
            values = (pupils_ref[part, k] * scale).astype(jnp.bfloat16)
            columns = dot(values, col_ref[...]).astype(jnp.bfloat16)
            full = dot(row_ref[...], columns)
            pos_pos, pos_neg = full[:rows, :lanes], full[:rows, lanes:]
            neg_pos, neg_neg = full[rows:, :lanes], full[rows:, lanes:]
            out_ref[k, 0 + part] = (pos_pos + neg_neg).astype(jnp.bfloat16)
            out_ref[k, 2 + part] = (pos_pos - neg_neg).astype(jnp.bfloat16)
            out_ref[k, 4 + part] = (pos_neg + neg_pos).astype(jnp.bfloat16)
            out_ref[k, 6 + part] = (pos_neg - neg_pos).astype(jnp.bfloat16)


def edges_kernel(low_ref, high_ref, first_ref, last_ref):
    first_ref[...] = low_ref[...].astype(jnp.bfloat16)
    last_ref[...] = high_ref[...].astype(jnp.bfloat16)


def early_kernel(
    rows, lanes, count, mask_ref, table_ref, pupils_ref, weights_ref, row_ref, col_ref, mid_ref, out_ref
):
    tile = mask_ref.shape[0]
    mid_ref[...] = dot(
        table_ref[:, AMBIT : AMBIT + tile], mask_ref[...].astype(jnp.bfloat16)
    )
    pupil_steps(rows, lanes, 0, count, pupils_ref, weights_ref, row_ref, col_ref, out_ref)


def partial_kernel(
    rows, lanes, live_ref, mid_ref, top_ref, bottom_ref, table_ref, col_t_ref, own_ref, low_ref, high_ref, main_ref
):
    extent = table_ref.shape[1]
    width = mid_ref.shape[1]
    tile = extent - 2 * AMBIT
    total = mid_ref[...] + dot(table_ref[:, :AMBIT], top_ref[...])
    total = total + dot(table_ref[:, extent - AMBIT :], bottom_ref[...])
    total = total.astype(jnp.bfloat16)
    own_ref[...] = total[:, : tile + AMBIT]
    low_ref[...] = total[:, :AMBIT]
    high_ref[...] = total[:, width - AMBIT :]
    main = dot(total[:, tile - AMBIT :], col_t_ref[: tile + AMBIT])
    shape = main.shape
    flag = (lax.broadcasted_iota(jnp.int32, shape, 0) == shape[0] - 1) & (
        lax.broadcasted_iota(jnp.int32, shape, 1) == shape[1] - 1
    )
    live = live_ref[0, live_ref.shape[1] - 1].astype(jnp.float32)
    main_ref[...] = jnp.where(flag, live, main).astype(jnp.bfloat16)


def late_kernel(
    rows, lanes, first, last, own_ref, col_t_ref, quads_ref, pupils_ref, weights_ref, row_ref, col_ref, base_ref, out_ref
):
    out_ref[:first] = quads_ref[...]
    base_ref[...] = dot(own_ref[...], col_t_ref[AMBIT:])
    pupil_steps(rows, lanes, first, last, pupils_ref, weights_ref, row_ref, col_ref, out_ref)


def core_kernel(
    rows,
    lanes,
    live_ref,
    base_ref,
    left_ref,
    main_ref,
    low_ref,
    right_ref,
    goal_ref,
    other_ref,
    pupil_ref,
    row_ref,
    row_t_ref,
    col_ref,
    col_t_ref,
    out_ref,
    other_out_ref,
    spec_ref,
    amp_ref,
    sec_ref,
    field_ref,
    total_ref,
    slope_ref,
    back_ref,
    sum_ref,
    ans_ref,
):
    tile = goal_ref.shape[0]
    extent = row_ref.shape[1]
    kernels = pupil_ref.shape[0]
    halves = [slice(start, start + 2 * LANE) for start in range(0, tile, 2 * LANE)]
    inner = slice(AMBIT, AMBIT + tile)
    odd = lax.rem(lax.axis_index("col"), 2) == 1
    spec_ref[0] = base_ref[...] + dot(left_ref[...], col_t_ref[:AMBIT])
    rim = jnp.where(odd, low_ref[...], right_ref[...])
    spec_ref[1] = main_ref[...].astype(jnp.float32) + dot(rim, col_t_ref[extent - AMBIT :])
    other_live = jnp.max(main_ref[2 * rows - 16 :, 2 * lanes - LANE :].astype(jnp.float32)[15:, LANE - 1 :])
    out_ref[...] = jnp.zeros_like(out_ref)
    other_out_ref[...] = jnp.zeros_like(other_out_ref)

    def work(item, carry):
        live = jnp.where(item == 0, live_ref[0, 0].astype(jnp.float32), other_live) > 0.0

        @pl.when(live)
        def _():
            spec = spec_ref[item]
            cc, cs = spec[:rows, :lanes], spec[:rows, lanes:]
            sc, ss = spec[rows:, :lanes], spec[rows:, lanes:]
            sum_ref[0] = cc - ss
            sum_ref[1] = sc + cs
            sum_ref[2] = cc + ss
            sum_ref[3] = sc - cs

            def pupil(k, index):
                return pupil_ref[k, index].astype(jnp.float32)

            def section(k, buf):
                u, v, m, n = sum_ref[0], sum_ref[1], sum_ref[2], sum_ref[3]
                pr, pi, mr, mi = (pupil(k, index) for index in range(4))
                big_re = pr * u + mi * v
                big_im = pi * u - mr * v
                small_re = mr * u + pi * v
                small_im = mi * u - pr * v
                pr, pi, mr, mi = (pupil(k, index) for index in range(4, 8))
                big_re2 = pr * m + mi * n
                big_im2 = pi * m - mr * n
                small_re2 = mr * m + pi * n
                small_im2 = mi * m - pr * n

                def pair(place, left, right):
                    where = slice(place * rows, (place + 1) * rows)
                    amp_ref[buf, where, :lanes] = left.astype(jnp.bfloat16)
                    amp_ref[buf, where, lanes:] = right.astype(jnp.bfloat16)

                pair(0, big_re + big_re2, small_im2 - small_im)
                pair(1, -(small_im + small_im2), big_re2 - big_re)
                pair(2, big_im + big_im2, small_re - small_re2)
                pair(3, small_re + small_re2, big_im2 - big_im)
                sec_ref[buf] = dot(amp_ref[buf], col_ref[:, inner]).astype(jnp.bfloat16)

            def field(ks, bufs):
                for where in halves:
                    energy = None
                    for k, buf in zip(ks, bufs):
                        real = dot(row_t_ref[inner], sec_ref[buf, : 2 * rows, where])
                        imag = dot(row_t_ref[inner], sec_ref[buf, 2 * rows :, where])
                        field_ref[k, 0, :, where] = real.astype(jnp.bfloat16)
                        field_ref[k, 1, :, where] = imag.astype(jnp.bfloat16)
                        term = real * real + imag * imag
                        energy = term if energy is None else energy + term
                    total_ref[:, where] += energy

            section(0, 0)
            total_ref[...] = jnp.zeros_like(total_ref)

            def forward(i, carry):
                k = 2 * i
                field((k,), (0,))
                section(k + 1, 1)
                field((k + 1,), (1,))
                section(jnp.minimum(k + 2, kernels - 1), 0)
                return carry

            lax.fori_loop(0, kernels // 2, forward, 0)

            def slopes(ref):
                for where in halves:
                    level = jnp.tanh(total_ref[:, where] - 0.5 * steepness * threshold_level)
                    excess = 0.5 * level + 0.5 - ref[:, where].astype(jnp.float32)
                    slope_ref[:, where] = (excess * (1.0 - level * level)).astype(jnp.bfloat16)

            @pl.when(item == 0)
            def _():
                slopes(goal_ref)

            @pl.when(item > 0)
            def _():
                slopes(other_ref)

            def back(k, buf):
                for where in halves:
                    for part in range(2):
                        cotangent = slope_ref[:, where] * field_ref[k, part, :, where]
                        place = slice(part * 2 * rows, (part + 1) * 2 * rows)
                        back_ref[buf, place, where] = dot(row_ref[:, inner], cotangent).astype(
                            jnp.bfloat16
                        )

            def adjoint(k, buf):
                wave = dot(back_ref[buf], col_t_ref[inner])
                rcc, rcs = wave[:rows, :lanes], wave[:rows, lanes:]
                rsc, rss = wave[rows : 2 * rows, :lanes], wave[rows : 2 * rows, lanes:]
                icc, ics = wave[2 * rows : 3 * rows, :lanes], wave[2 * rows : 3 * rows, lanes:]
                isc, iss = wave[3 * rows :, :lanes], wave[3 * rows :, lanes:]
                ur, ui, vr, vi = rcc - rss, icc - iss, rsc + rcs, isc + ics
                pr, pi, mr, mi = (pupil(k, index) for index in range(4))
                ans_ref[0] += pr * ur + pi * ui + mr * vi - mi * vr
                ans_ref[1] += mr * ui - mi * ur - pr * vr - pi * vi
                ur, ui, vr, vi = rcc + rss, icc + iss, rsc - rcs, isc - ics
                pr, pi, mr, mi = (pupil(k, index) for index in range(4, 8))
                ans_ref[2] += pr * ur + pi * ui + mr * vi - mi * vr
                ans_ref[3] += mr * ui - mi * ur - pr * vr - pi * vi

            ans_ref[...] = jnp.zeros_like(ans_ref)
            back(0, 0)

            def backward(i, carry):
                k = 2 * i
                adjoint(k, 0)
                back(k + 1, 1)
                adjoint(k + 1, 1)
                back(jnp.minimum(k + 2, kernels - 1), 0)
                return carry

            lax.fori_loop(0, kernels // 2, backward, 0)

            def answer(ref):
                ref[:rows, :lanes] = (ans_ref[0] + ans_ref[2]).astype(jnp.bfloat16)
                ref[:rows, lanes:] = (ans_ref[3] - ans_ref[1]).astype(jnp.bfloat16)
                ref[rows:, :lanes] = (-(ans_ref[1] + ans_ref[3])).astype(jnp.bfloat16)
                ref[rows:, lanes:] = (ans_ref[2] - ans_ref[0]).astype(jnp.bfloat16)

            @pl.when(item == 0)
            def _():
                answer(out_ref)

            @pl.when(item > 0)
            def _():
                answer(other_out_ref)

        return carry

    lax.fori_loop(0, 2, work, 0)


def returned_kernel(
    tile, mine_ref, second_ref, after_ref, before_ref, other_ref, row_t_ref, col_ref, out_ref, up_ref, down_ref, sum_ref
):
    width = out_ref.shape[1]
    extent = row_t_ref.shape[0]
    odd = lax.rem(lax.axis_index("col"), 2) == 1
    before = jnp.where(odd, other_ref[...], before_ref[...])
    sum_ref[...] = jnp.zeros_like(sum_ref)
    for place, value in zip(range(-1, 3), (before, mine_ref[...], second_ref[...], after_ref[...])):
        start = place * tile - AMBIT
        low, high = max(0, start), min(width, start + extent)
        sum_ref[:, low:high] += dot(value, col_ref[:, low - start : high - start])
    mixed = sum_ref[...].astype(jnp.bfloat16)
    out_ref[...] = mixed
    up_ref[...] = dot(row_t_ref[:AMBIT], mixed).astype(jnp.bfloat16)
    down_ref[...] = dot(row_t_ref[extent - AMBIT :], mixed).astype(jnp.bfloat16)


def update_kernel(mask_ref, mixed_ref, row_t_ref, out_ref, rims_ref, stage_ref, sem):
    tile = mask_ref.shape[0]
    stage_ref[...] = mask_ref[...] - step_rate * dot(
        row_t_ref[AMBIT : AMBIT + tile], mixed_ref[...]
    )
    inner = pl.ds(AMBIT, tile - 2 * AMBIT)
    copy = pltpu.make_async_copy(stage_ref.at[inner], out_ref.at[inner], sem)
    copy.start()
    rims_ref[:AMBIT] = stage_ref[:AMBIT]
    rims_ref[AMBIT:] = stage_ref[tile - AMBIT :]
    copy.wait()


def rims_kernel(above_ref, below_ref, rims_ref, base_ref, out_ref, stage_ref, sems):
    tile = out_ref.shape[0]
    copies = []
    for index, (rim_ref, start) in enumerate(((above_ref, 0), (below_ref, tile - AMBIT))):
        where = pl.ds(index * AMBIT, AMBIT)
        stage_ref[where] = rims_ref[where] - step_rate * rim_ref[...].astype(jnp.float32)
        copy = pltpu.make_async_copy(
            stage_ref.at[where], out_ref.at[pl.ds(start, AMBIT)], sems.at[index]
        )
        copy.start()
        copies.append(copy)
    for copy in copies:
        copy.wait()


def body(mask, target, live, pupils, weights):
    tile, width = mask.shape
    kernels, size = pupils.shape[1], pupils.shape[2]
    half = size // 2
    rows, lanes = round_up(half + 1, 16), round_up(half + 2, LANE)
    extent = tile + 2 * AMBIT
    row_np = half_tables(half, rows, extent)
    col_np = half_tables(half, lanes, extent)
    row_pick, col_pick = (
        jnp.asarray(pick, jnp.bfloat16) for pick in pick_tables(half, rows, lanes)
    )
    row_table, row_table_t = jnp.asarray(row_np, jnp.bfloat16), jnp.asarray(row_np.T, jnp.bfloat16)
    col_table, col_table_t = jnp.asarray(col_np, jnp.bfloat16), jnp.asarray(col_np.T, jnp.bfloat16)
    bf16, f32 = jnp.bfloat16, jnp.float32
    shape = jax.ShapeDtypeStruct
    smem = pl.BlockSpec(memory_space=pltpu.SMEM)
    early = kernels // 2

    def paired(index):
        return index + 1 - 2 * (index % 2)

    edge = shape((AMBIT, width), bf16)
    first, last = pl.pallas_call(
        edges_kernel,
        out_shape=(edge, edge),
        grid=(1,),
        in_specs=[
            pl.BlockSpec((AMBIT, width), lambda i: (0, 0)),
            pl.BlockSpec((AMBIT, width), lambda i: (tile // AMBIT - 1, 0)),
        ],
        out_specs=(pl.BlockSpec(memory_space=pltpu.VMEM), pl.BlockSpec(memory_space=pltpu.VMEM)),
        compiler_params=pltpu.CompilerParams(vmem_limit_bytes=8 * MIB),
    )(mask, mask)
    top = moved(last, "row", lambda i: i + 1)
    bottom = moved(first, "row", lambda i: i - 1)
    other_goal = moved(target[:, tile:], "col", paired)
    middle, quads = call(
        partial(early_kernel, rows, lanes, early),
        (shape((2 * rows, width), f32), shape((early, 8, rows, lanes), bf16)),
        [*vmem(3), smem, *vmem(2)],
        us=4,
    )(mask, row_table, pupils, weights, row_pick, col_pick)
    own, low, high, main = call(
        partial(partial_kernel, rows, lanes),
        (
            shape((2 * rows, tile + AMBIT), bf16),
            shape((2 * rows, AMBIT), bf16),
            shape((2 * rows, AMBIT), bf16),
            shape((2 * rows, 2 * lanes), bf16),
        ),
        [smem, *vmem(5)],
    )(live, middle, top, bottom, row_table, col_table_t)
    left = moved(high, "col", lambda i: i + 1)
    other_main = moved(main, "col", paired)
    right = moved(low, "col", lambda i: i - 2 if i % 2 == 0 else None)
    base, all_quads = call(
        partial(late_kernel, rows, lanes, early, kernels),
        (shape((2 * rows, 2 * lanes), f32), shape((kernels, 8, rows, lanes), bf16)),
        [*vmem(4), smem, *vmem(2)],
        us=4,
    )(own, col_table_t, quads, pupils, weights, row_pick, col_pick)
    answer = shape((2 * rows, 2 * lanes), bf16)
    mine, other = call(
        partial(core_kernel, rows, lanes),
        (answer, answer),
        [smem, *vmem(12)],
        scratch=[
            pltpu.VMEM((2, 2 * rows, 2 * lanes), f32),
            pltpu.VMEM((2, 4 * rows, 2 * lanes), bf16),
            pltpu.VMEM((2, 4 * rows, tile), bf16),
            pltpu.VMEM((kernels, 2, tile, tile), bf16),
            pltpu.VMEM((tile, tile), f32),
            pltpu.VMEM((tile, tile), bf16),
            pltpu.VMEM((2, 4 * rows, tile), bf16),
            pltpu.VMEM((4, rows, lanes), f32),
            pltpu.VMEM((4, rows, lanes), f32),
        ],
        limit=36,
        us=15,
    )(
        live, base, left, other_main, low, right, target, other_goal, all_quads,
        row_table, row_table_t, col_table, col_table_t,
    )
    second = moved(other, "col", paired)
    after = moved(mine, "col", lambda i: i - 1)
    before = moved(other, "col", lambda i: i + 2 if i % 2 == 0 else None)
    mixed, up, down = call(
        partial(returned_kernel, tile),
        (shape((2 * rows, width), bf16), shape((AMBIT, width), bf16), shape((AMBIT, width), bf16)),
        vmem(7),
        scratch=[pltpu.VMEM((2 * rows, width), f32)],
    )(mine, second, after, before, other, row_table_t, col_table)
    from_above = moved(down, "row", lambda i: i + 1)
    from_below = moved(up, "row", lambda i: i - 1)
    anywhere = pl.BlockSpec(memory_space=pl.ANY)
    whole, rims = shape((tile, width), f32), shape((2 * AMBIT, width), f32)
    updated, edges = pl.pallas_call(
        update_kernel,
        out_shape=(whole, rims),
        in_specs=vmem(3),
        out_specs=(anywhere, *vmem(1)),
        scratch_shapes=[pltpu.VMEM((tile, width), f32), pltpu.SemaphoreType.DMA],
        cost_estimate=pl.CostEstimate(flops=10**9, bytes_accessed=2 * 10**6, transcendentals=0),
        compiler_params=pltpu.CompilerParams(vmem_limit_bytes=16 * MIB),
    )(mask, mixed, row_table_t)
    return pl.pallas_call(
        rims_kernel,
        out_shape=whole,
        in_specs=[*vmem(3), anywhere],
        out_specs=anywhere,
        scratch_shapes=[pltpu.VMEM((2 * AMBIT, width), f32), pltpu.SemaphoreType.DMA((2,))],
        input_output_aliases={3: 0},
        compiler_params=pltpu.CompilerParams(vmem_limit_bytes=8 * MIB),
    )(from_above, from_below, edges, updated)


def solution(mesh):
    placed = (P("row", "col"), P("row", "col"), P("row", "col"), P(), P())
    return jax.shard_map(
        body, mesh=mesh, in_specs=placed, out_specs=P("row", "col"), check_vma=False
    )
```

time: 99.6 us -> 63.7 us (0.64)
  starting transfers between devices: 62.1 us -> 23.5 us
  waiting for transfers between devices: 7.36 us -> 14.2 us
  Pallas kernels: 25.3 us -> 20.5 us
  other arithmetic: 1.74 us -> 0 us
  local copies, waits for them, and re-layouts: 3.04 us -> 4.71 us
    ppermute x8 -> x11, starting transfers between devices: 62.1 us -> 23.5 us  [moved(): lax.ppermute(block, axis, [(i, j) for i, j in pairs if j is not None and...]
    ppermute x8 -> x11, waiting for transfers between devices: 7.36 us -> 14.2 us  [moved(): lax.ppermute(block, axis, [(i, j) for i, j in pairs if j is not None and...]
    pallas_call x7 -> x8, Pallas kernels: 25.3 us -> 20.5 us  [the longest x1 12.9 us: body(): call(partial(core_kernel, rows, lanes), (answer, answer), [smem, *vmem(12...]
    another operation x1 -> x0, other arithmetic: 1.74 us -> none
    slice x1, local copies, waits for them, and re-layouts: 0.04 us -> 1.08 us  [body(): other_goal = moved(target[:, tile:], 'col', paired)]
    unnamed x16 -> x26, local copies, waits for them, and re-layouts: 3 us -> 3.64 us
  transfers between devices with their start and end apart: 8 -> 11, of which waited for: 4 -> 5; matrix products, arithmetic and copies ran while one was open for 0% -> 0% of each run, Pallas kernels for 15% -> 9%
where the time goes in v2:
time: 63.7 us; the launch traced here: 63.1 us
  starting transfers between devices  23.5 us (37%)
  Pallas kernels  20.5 us (32%)
  waiting for transfers between devices  14.2 us (22%)
  local copies, waits for them, and re-layouts  4.71 us (7%)
    ppermute x11, starting transfers between devices, moved(): lax.ppermute(block, axis, [(i, j) for i, j in pairs if j is not None and...  23.5 us
    ppermute x11, waiting for transfers between devices, moved(): lax.ppermute(block, axis, [(i, j) for i, j in pairs if j is not None and...  14.2 us
    pallas_call x1, Pallas kernels, body(): call(partial(core_kernel, rows, lanes), (answer, answer), [smem, *vmem(12...  12.9 us
    unnamed x26, local copies, waits for them, and re-layouts  3.64 us
    pallas_call x1, Pallas kernels, body(): call(partial(late_kernel, rows, lanes, early, kernels), (shape((2 * rows,...  1.78 us
    pallas_call x1, Pallas kernels, body(): call(partial(early_kernel, rows, lanes, early), (shape((2 * rows, width),...  1.65 us
    pallas_call x1, Pallas kernels, body(): pl.pallas_call(update_kernel, out_shape=(whole, rims), in_specs=vmem(3),...  1.41 us
  transfers between devices with their start and end apart: 11, of which 5 were waited for; matrix products, arithmetic and copies ran while one was open for 0% of the time, Pallas kernels for 9%

profile of v2, /device:TPU:11, one launch (start us, length us, event | category | flops | bytes accessed | tf_op | source)
XLA Modules:
  0.0 63.1 jit_solution(1410314066644852473)
XLA Ops:
  0.0 1.1 %slice.3 = bf16[512,512]{1,0:T(8,128)(2,1)S(1)} slice(bf16[512,1024]{1,0:T(8,128)(2,1)} %goal_ref.1), slice={[0:512], [512:1024]} | slice | bytes 1048576 | tf_op jit(solution)/shard_map/slice | solution.py:395
  1.1 0.2 collective-permute-start.5
  1.3 1.6 %copy-done = f32[512,1024]{1,0:T(8,128)S(1)} copy-done((f32[512,1024]{1,0:T(8,128)S(1)}, f32[512,1024]{1,0:T(8,128)}, u32[]{:S(2)}) %copy-start) | copy-done | bytes 2097176
  2.9 0.0 copy-start.12
  2.9 0.1 shard_map.110
  3.0 4.1 %collective-permute-start = (bf16[128,1024]{1,0:T(8,128)(2,1)S(1)}, bf16[128,1024]{1,0:T(8,128)(2,1)S(1)}, u32[]{:S(2)}, u32[]{:S(2)}) collective-permute-start(bf16[128,1024]{1,0:T(8,128)(2,1)S(1)} %get-tuple-element.23), channel_id=1, source_target_pairs={{0,4},{4,8},{8,12},{12,16},{16,20},{20,24},{24,28},{1,5},{5,9},{9,... | collective-permute-start | bytes 786440 | tf_op jit(solution)/shard_map/ppermute | solution.py:29
  7.1 1.9 %collective-permute-start.1 = (bf16[128,1024]{1,0:T(8,128)(2,1)S(1)}, bf16[128,1024]{1,0:T(8,128)(2,1)S(1)}, u32[]{:S(2)}, u32[]{:S(2)}) collective-permute-start(bf16[128,1024]{1,0:T(8,128)(2,1)S(1)} %get-tuple-element.24), channel_id=1, source_target_pairs={{4,0},{8,4},{12,8},{16,12},{20,16},{24,20},{28,24},{5,1},{9,5},{13... | collective-permute-start | bytes 786440 | tf_op jit(solution)/shard_map/ppermute | solution.py:29
  9.1 0.0 copy-start.3
  9.1 2.0 %copy-done.3 = f32[2,12,144,144]{3,2,1,0:T(8,128)S(1)} copy-done((f32[2,12,144,144]{3,2,1,0:T(8,128)S(1)}, f32[2,12,144,144]{3,2,1,0:T(8,128)}, u32[]{:S(2)}) %copy-start.3) | copy-done | bytes 1990680
  11.1 1.6 %shard_map.109 = (f32[160,1024]{1,0:T(8,128)S(1)}, bf16[6,8,80,128]{3,2,1,0:T(8,128)(2,1)S(1)}) custom-call(f32[512,1024]{1,0:T(8,128)S(1)} %copy-done.1, bf16[160,768]{1,0:T(8,128)(2,1)S(1)} %copy-done.10, f32[2,12,144,144]{3,2,1,0:T(8,128)S(1)} %copy-done.3, f32[12]{0:T(128)S(1)} %copy-done.5, bf16[160,144]{1,0:T(8,128)(2,1)S(1)} %copy-done.11, ...), custom_call_target="tpu_custom_call" | custom-call | flops 2000000000 | bytes 4000000 | tf_op jit(solution)/shard_map/pallas_call | solution.py:396
  12.7 2.9 %collective-permute-done.1.bottom_ref = bf16[128,1024]{1,0:T(8,128)(2,1)S(1)} collective-permute-done((bf16[128,1024]{1,0:T(8,128)(2,1)S(1)}, bf16[128,1024]{1,0:T(8,128)(2,1)S(1)}, u32[]{:S(2)}, u32[]{:S(2)}) %collective-permute-start.1) | collective-permute-done | bytes 262176 | tf_op jit(solution)/shard_map/ppermute | solution.py:29
  15.7 1.1 %shard_map.111 = (bf16[160,640]{1,0:T(8,128)(2,1)S(1)}, bf16[160,128]{1,0:T(8,128)(2,1)S(1)}, bf16[160,128]{1,0:T(8,128)(2,1)S(1)}, bf16[160,256]{1,0:T(8,128)(2,1)S(1)}) custom-call(s32[1,2]{1,0:T(1,128)S(1)} %copy-done.6, f32[160,1024]{1,0:T(8,128)S(1)} %get-tuple-element.22.mid_ref, bf16[128,1024]{1,0:T(8,128)(2,1)S(1)} %collective-permute-done.top_ref, ...), custom_call_target="tpu_custom_call" | custom-call | flops 500000000 | bytes 1000000 | tf_op jit(solution)/shard_map/pallas_call | solution.py:402
  16.8 4.3 %collective-permute-start.2 = (bf16[160,128]{1,0:T(8,128)(2,1)S(1)}, bf16[160,128]{1,0:T(8,128)(2,1)S(1)}, u32[]{:S(2)}, u32[]{:S(2)}) collective-permute-start(bf16[160,128]{1,0:T(8,128)(2,1)S(1)} %get-tuple-element.28), channel_id=1, source_target_pairs={{0,1},{1,2},{2,3},{4,5},{5,6},{6,7},{8,9},{9,10},{10,11},{12,13},{... | collective-permute-start | bytes 122888 | tf_op jit(solution)/shard_map/ppermute | solution.py:29
  21.1 0.7 %collective-permute-start.4 = (bf16[160,128]{1,0:T(8,128)(2,1)S(1)}, bf16[160,128]{1,0:T(8,128)(2,1)S(1)}, u32[]{:S(2)}, u32[]{:S(2)}) collective-permute-start(bf16[160,128]{1,0:T(8,128)(2,1)S(1)} %get-tuple-element.30.low_ref), channel_id=1, source_target_pairs={{2,0},{6,4},{10,8},{14,12},{18,16},{22,20},{26,24},{30,28}} | collective-permute-start | bytes 122888 | tf_op jit(solution)/shard_map/ppermute | solution.py:29
  21.8 0.1 collective-permute-start.3
  21.9 0.0 copy-start.2
  21.9 0.0 copy-start.7
  21.9 0.0 copy-start.8
  21.9 1.8 %shard_map.112 = (f32[160,256]{1,0:T(8,128)S(1)}, bf16[12,8,80,128]{3,2,1,0:T(8,128)(2,1)S(1)}) custom-call(bf16[160,640]{1,0:T(8,128)(2,1)S(1)} %get-tuple-element.25.own_ref, bf16[768,256]{1,0:T(8,128)(2,1)S(1)} %copy-done.9, bf16[6,8,80,128]{3,2,1,0:T(8,128)(2,1)S(1)} %get-tuple-element.26.quads_ref, f32[2,12,144,144]{3,2,1,0:T(8,128)S(1)} %copy-done.4, ...), custom_call_target="tpu_custom_call" | custom-call | flops 2000000000 | bytes 4000000 | tf_op jit(solution)/shard_map/pallas_call | solution.py:415
  23.7 1.4 %collective-permute-done.3.main_ref = bf16[160,256]{1,0:T(8,128)(2,1)S(1)} collective-permute-done((bf16[160,256]{1,0:T(8,128)(2,1)S(1)}, bf16[160,256]{1,0:T(8,128)(2,1)S(1)}, u32[]{:S(2)}, u32[]{:S(2)}) %collective-permute-start.3) | collective-permute-done | bytes 81952 | tf_op jit(solution)/shard_map/ppermute | solution.py:29
  25.2 12.9 %shard_map.113 = (bf16[160,256]{1,0:T(8,128)(2,1)S(1)}, bf16[160,256]{1,0:T(8,128)(2,1)S(1)}) custom-call(s32[1,2]{1,0:T(1,128)S(1)} %copy-done.6, f32[160,256]{1,0:T(8,128)S(1)} %get-tuple-element.27.base_ref, bf16[160,128]{1,0:T(8,128)(2,1)S(1)} %collective-permute-done.2.left_ref, bf16[160,256]{1,0:T(8,128)(2,1)S(1)} %collective-permute-done.3.main_ref, ...), custom_call_target="tpu_custom_call" | custom-call | flops 7500000256 | bytes 15000000 | tf_op jit(solution)/shard_map/pallas_call | solution.py:422
  38.1 2.6 %collective-permute-start.7 = (bf16[160,256]{1,0:T(8,128)(2,1)S(1)}, bf16[160,256]{1,0:T(8,128)(2,1)S(1)}, u32[]{:S(2)}, u32[]{:S(2)}) collective-permute-start(bf16[160,256]{1,0:T(8,128)(2,1)S(1)} %get-tuple-element.32.mine_ref), channel_id=1, source_target_pairs={{1,0},{2,1},{3,2},{5,4},{6,5},{7,6},{9,8},{10,9},{11,10},{13,12},{... | collective-permute-start | bytes 245768 | tf_op jit(solution)/shard_map/ppermute | solution.py:29
  40.7 0.7 %collective-permute-start.8 = (bf16[160,256]{1,0:T(8,128)(2,1)S(1)}, bf16[160,256]{1,0:T(8,128)(2,1)S(1)}, u32[]{:S(2)}, u32[]{:S(2)}) collective-permute-start(bf16[160,256]{1,0:T(8,128)(2,1)S(1)} %get-tuple-element.33.other_ref), channel_id=1, source_target_pairs={{0,2},{4,6},{8,10},{12,14},{16,18},{20,22},{24,26},{28,30}} | collective-permute-start | bytes 245768 | tf_op jit(solution)/shard_map/ppermute | solution.py:29
  41.4 3.3 %collective-permute-start.6 = (bf16[160,256]{1,0:T(8,128)(2,1)S(1)}, bf16[160,256]{1,0:T(8,128)(2,1)S(1)}, u32[]{:S(2)}, u32[]{:S(2)}) collective-permute-start(bf16[160,256]{1,0:T(8,128)(2,1)S(1)} %get-tuple-element.33.other_ref), channel_id=1, source_target_pairs={{0,1},{1,0},{2,3},{3,2},{4,5},{5,4},{6,7},{7,6},{8,9},{9,8},{10,11... | collective-permute-start | bytes 245768 | tf_op jit(solution)/shard_map/ppermute | solution.py:29
  44.7 4.6 %collective-permute-done.6.second_ref = bf16[160,256]{1,0:T(8,128)(2,1)S(1)} collective-permute-done((bf16[160,256]{1,0:T(8,128)(2,1)S(1)}, bf16[160,256]{1,0:T(8,128)(2,1)S(1)}, u32[]{:S(2)}, u32[]{:S(2)}) %collective-permute-start.6) | collective-permute-done | bytes 81952 | tf_op jit(solution)/shard_map/ppermute | solution.py:29
  49.2 0.6 shard_map.114
  49.8 3.7 %collective-permute-start.9 = (bf16[128,1024]{1,0:T(8,128)(2,1)S(1)}, bf16[128,1024]{1,0:T(8,128)(2,1)S(1)}, u32[]{:S(2)}, u32[]{:S(2)}) collective-permute-start(bf16[128,1024]{1,0:T(8,128)(2,1)S(1)} %get-tuple-element.34), channel_id=1, source_target_pairs={{0,4},{4,8},{8,12},{12,16},{16,20},{20,24},{24,28},{1,5},{5,9},{9,... | collective-permute-start | bytes 786440 | tf_op jit(solution)/shard_map/ppermute | solution.py:29
  53.5 1.9 %collective-permute-start.10 = (bf16[128,1024]{1,0:T(8,128)(2,1)S(1)}, bf16[128,1024]{1,0:T(8,128)(2,1)S(1)}, u32[]{:S(2)}, u32[]{:S(2)}) collective-permute-start(bf16[128,1024]{1,0:T(8,128)(2,1)S(1)} %get-tuple-element.35), channel_id=1, source_target_pairs={{4,0},{8,4},{12,8},{16,12},{20,16},{24,20},{28,24},{5,1},{9,5},{13... | collective-permute-start | bytes 786440 | tf_op jit(solution)/shard_map/ppermute | solution.py:29
  55.4 1.4 %shard_map.115 = (f32[512,1024]{1,0:T(8,128)}, f32[256,1024]{1,0:T(8,128)S(1)}) custom-call(f32[512,1024]{1,0:T(8,128)S(1)} %copy-done.1, bf16[160,1024]{1,0:T(8,128)(2,1)S(1)} %get-tuple-element.36.mixed_ref, bf16[768,160]{1,0:T(8,128)(2,1)S(1)} %copy-done.7), custom_call_target="tpu_custom_call" | custom-call | flops 1000000000 | bytes 2000000 | tf_op jit(solution)/shard_map/pallas_call | solution.py:456
  56.8 0.2 collective-permute-done.9.above_ref
  57.1 5.0 %collective-permute-done.10.below_ref = bf16[128,1024]{1,0:T(8,128)(2,1)S(1)} collective-permute-done((bf16[128,1024]{1,0:T(8,128)(2,1)S(1)}, bf16[128,1024]{1,0:T(8,128)(2,1)S(1)}, u32[]{:S(2)}, u32[]{:S(2)}) %collective-permute-start.10) | collective-permute-done | bytes 262176 | tf_op jit(solution)/shard_map/ppermute | solution.py:29
  62.1 1.0 %shard_map.116 = f32[512,1024]{1,0:T(8,128)} custom-call(bf16[128,1024]{1,0:T(8,128)(2,1)S(1)} %collective-permute-done.9.above_ref, bf16[128,1024]{1,0:T(8,128)(2,1)S(1)} %collective-permute-done.10.below_ref, f32[256,1024]{1,0:T(8,128)S(1)} %get-tuple-element.37.rims_ref, f32[512,1024]{1,0:T(8,128)} %get-tuple-element.38.base_ref), custom_call_target="tpu_custom_call", output_to_operand_aliasing={{}: (3, {})} | custom-call | tf_op jit(solution)/shard_map/pallas_call | solution.py:465
  (25 shorter events, 0.1 us)
Async XLA Ops:
  1.1 24.1 %collective-permute-start.5 = (bf16[512,512]{1,0:T(8,128)(2,1)S(1)}, bf16[512,512]{1,0:T(8,128)(2,1)S(1)}, u32[]{:S(2)}, u32[]{:S(2)}) collective-permute-start(bf16[512,512]{1,0:T(8,128)(2,1)S(1)} %slice.3), channel_id=1, source_target_pairs={{0,1},{1,0},{2,3},{3,2},{4,5},{5,4},{6,7},{7,6},{8,9},{9,8},{10,11... | collective-permute-start | bytes 1572872 | tf_op jit(solution)/shard_map/ppermute | solution.py:29
  1.3 1.6 %copy-start = (f32[512,1024]{1,0:T(8,128)S(1)}, f32[512,1024]{1,0:T(8,128)}, u32[]{:S(2)}) copy-start(f32[512,1024]{1,0:T(8,128)} %mask_ref.3) | copy-start | bytes 6291460
  2.9 6.1 %copy-start.1 = (f32[512,1024]{1,0:T(8,128)S(1)}, f32[512,1024]{1,0:T(8,128)}, u32[]{:S(2)}) copy-start(f32[512,1024]{1,0:T(8,128)} %mask_ref.3) | copy-start | bytes 6291460
  2.9 6.1 %copy-start.5 = (f32[12]{0:T(128)S(1)}, f32[12]{0:T(128)}, u32[]{:S(2)}) copy-start(f32[12]{0:T(128)} %weights_ref.3) | copy-start | bytes 148
  2.9 6.1 %copy-start.10 = (bf16[160,768]{1,0:T(8,128)(2,1)S(1)}, bf16[160,768]{1,0:T(8,128)(2,1)}, u32[]{:S(2)}) copy-start(bf16[160,768]{1,0:T(8,128)(2,1)} %constant.14.clone.table_ref.row_ref) | copy-start | bytes 737284
  2.9 6.1 %copy-start.11 = (bf16[160,144]{1,0:T(8,128)(2,1)S(1)}, bf16[160,144]{1,0:T(8,128)(2,1)}, u32[]{:S(2)}) copy-start(bf16[160,144]{1,0:T(8,128)(2,1)} %constant.12.clone.row_ref) | copy-start | bytes 138244
  2.9 6.1 %copy-start.12 = (bf16[144,256]{1,0:T(8,128)(2,1)S(1)}, bf16[144,256]{1,0:T(8,128)(2,1)}, u32[]{:S(2)}) copy-start(bf16[144,256]{1,0:T(8,128)(2,1)} %constant.13.clone.col_ref) | copy-start | bytes 221188
  3.0 9.7 %collective-permute-start = (bf16[128,1024]{1,0:T(8,128)(2,1)S(1)}, bf16[128,1024]{1,0:T(8,128)(2,1)S(1)}, u32[]{:S(2)}, u32[]{:S(2)}) collective-permute-start(bf16[128,1024]{1,0:T(8,128)(2,1)S(1)} %get-tuple-element.23), channel_id=1, source_target_pairs={{0,4},{4,8},{8,12},{12,16},{16,20},{20,24},{24,28},{1,5},{5,9},{9,... | collective-permute-start | bytes 786440 | tf_op jit(solution)/shard_map/ppermute | solution.py:29
  7.1 8.6 %collective-permute-start.1 = (bf16[128,1024]{1,0:T(8,128)(2,1)S(1)}, bf16[128,1024]{1,0:T(8,128)(2,1)S(1)}, u32[]{:S(2)}, u32[]{:S(2)}) collective-permute-start(bf16[128,1024]{1,0:T(8,128)(2,1)S(1)} %get-tuple-element.24), channel_id=1, source_target_pairs={{4,0},{8,4},{12,8},{16,12},{20,16},{24,20},{28,24},{5,1},{9,5},{13... | collective-permute-start | bytes 786440 | tf_op jit(solution)/shard_map/ppermute | solution.py:29
  9.1 2.0 %copy-start.3 = (f32[2,12,144,144]{3,2,1,0:T(8,128)S(1)}, f32[2,12,144,144]{3,2,1,0:T(8,128)}, u32[]{:S(2)}) copy-start(f32[2,12,144,144]{3,2,1,0:T(8,128)} %pupils_ref.3) | copy-start | bytes 5971972
  11.1 4.6 %copy-start.6 = (s32[1,2]{1,0:T(1,128)S(1)}, s32[1,2]{1,0:T(1,128)}, u32[]{:S(2)}) copy-start(s32[1,2]{1,0:T(1,128)} %live_ref.3) | copy-start | bytes 28
  11.1 4.6 %copy-start.9 = (bf16[768,256]{1,0:T(8,128)(2,1)S(1)}, bf16[768,256]{1,0:T(8,128)(2,1)}, u32[]{:S(2)}) copy-start(bf16[768,256]{1,0:T(8,128)(2,1)} %constant.17.clone.col_t_ref) | copy-start | bytes 1179652
  11.1 10.8 %copy-start.4 = (f32[2,12,144,144]{3,2,1,0:T(8,128)S(1)}, f32[2,12,144,144]{3,2,1,0:T(8,128)}, u32[]{:S(2)}) copy-start(f32[2,12,144,144]{3,2,1,0:T(8,128)} %pupils_ref.3) | copy-start | bytes 5971972
  16.8 6.9 %collective-permute-start.2 = (bf16[160,128]{1,0:T(8,128)(2,1)S(1)}, bf16[160,128]{1,0:T(8,128)(2,1)S(1)}, u32[]{:S(2)}, u32[]{:S(2)}) collective-permute-start(bf16[160,128]{1,0:T(8,128)(2,1)S(1)} %get-tuple-element.28), channel_id=1, source_target_pairs={{0,1},{1,2},{2,3},{4,5},{5,6},{6,7},{8,9},{9,10},{10,11},{12,13},{... | collective-permute-start | bytes 122888 | tf_op jit(solution)/shard_map/ppermute | solution.py:29
  21.1 2.6 %collective-permute-start.4 = (bf16[160,128]{1,0:T(8,128)(2,1)S(1)}, bf16[160,128]{1,0:T(8,128)(2,1)S(1)}, u32[]{:S(2)}, u32[]{:S(2)}) collective-permute-start(bf16[160,128]{1,0:T(8,128)(2,1)S(1)} %get-tuple-element.30.low_ref), channel_id=1, source_target_pairs={{2,0},{6,4},{10,8},{14,12},{18,16},{22,20},{26,24},{30,28}} | collective-permute-start | bytes 122888 | tf_op jit(solution)/shard_map/ppermute | solution.py:29
  21.8 3.4 %collective-permute-start.3 = (bf16[160,256]{1,0:T(8,128)(2,1)S(1)}, bf16[160,256]{1,0:T(8,128)(2,1)S(1)}, u32[]{:S(2)}, u32[]{:S(2)}) collective-permute-start(bf16[160,256]{1,0:T(8,128)(2,1)S(1)} %get-tuple-element.29), channel_id=1, source_target_pairs={{0,1},{1,0},{2,3},{3,2},{4,5},{5,4},{6,7},{7,6},{8,9},{9,8},{10,11... | collective-permute-start | bytes 245768 | tf_op jit(solution)/shard_map/ppermute | solution.py:29
  21.9 3.3 %copy-start.2 = (bf16[512,1024]{1,0:T(8,128)(2,1)S(1)}, bf16[512,1024]{1,0:T(8,128)(2,1)}, u32[]{:S(2)}) copy-start(bf16[512,1024]{1,0:T(8,128)(2,1)} %goal_ref.1) | copy-start | bytes 3145732
  21.9 3.3 %copy-start.7 = (bf16[768,160]{1,0:T(8,128)(2,1)S(1)}, bf16[768,160]{1,0:T(8,128)(2,1)}, u32[]{:S(2)}) copy-start(bf16[768,160]{1,0:T(8,128)(2,1)} %constant.15.clone.row_t_ref) | copy-start | bytes 737284
  21.9 3.3 %copy-start.8 = (bf16[256,768]{1,0:T(8,128)(2,1)S(1)}, bf16[256,768]{1,0:T(8,128)(2,1)}, u32[]{:S(2)}) copy-start(bf16[256,768]{1,0:T(8,128)(2,1)} %constant.16.clone.col_ref) | copy-start | bytes 1179652
  38.1 6.5 %collective-permute-start.7 = (bf16[160,256]{1,0:T(8,128)(2,1)S(1)}, bf16[160,256]{1,0:T(8,128)(2,1)S(1)}, u32[]{:S(2)}, u32[]{:S(2)}) collective-permute-start(bf16[160,256]{1,0:T(8,128)(2,1)S(1)} %get-tuple-element.32.mine_ref), channel_id=1, source_target_pairs={{1,0},{2,1},{3,2},{5,4},{6,5},{7,6},{9,8},{10,9},{11,10},{13,12},{... | collective-permute-start | bytes 245768 | tf_op jit(solution)/shard_map/ppermute | solution.py:29
  40.7 4.0 %collective-permute-start.8 = (bf16[160,256]{1,0:T(8,128)(2,1)S(1)}, bf16[160,256]{1,0:T(8,128)(2,1)S(1)}, u32[]{:S(2)}, u32[]{:S(2)}) collective-permute-start(bf16[160,256]{1,0:T(8,128)(2,1)S(1)} %get-tuple-element.33.other_ref), channel_id=1, source_target_pairs={{0,2},{4,6},{8,10},{12,14},{16,18},{20,22},{24,26},{28,30}} | collective-permute-start | bytes 245768 | tf_op jit(solution)/shard_map/ppermute | solution.py:29
  41.4 7.9 %collective-permute-start.6 = (bf16[160,256]{1,0:T(8,128)(2,1)S(1)}, bf16[160,256]{1,0:T(8,128)(2,1)S(1)}, u32[]{:S(2)}, u32[]{:S(2)}) collective-permute-start(bf16[160,256]{1,0:T(8,128)(2,1)S(1)} %get-tuple-element.33.other_ref), channel_id=1, source_target_pairs={{0,1},{1,0},{2,3},{3,2},{4,5},{5,4},{6,7},{7,6},{8,9},{9,8},{10,11... | collective-permute-start | bytes 245768 | tf_op jit(solution)/shard_map/ppermute | solution.py:29
  49.8 7.3 %collective-permute-start.9 = (bf16[128,1024]{1,0:T(8,128)(2,1)S(1)}, bf16[128,1024]{1,0:T(8,128)(2,1)S(1)}, u32[]{:S(2)}, u32[]{:S(2)}) collective-permute-start(bf16[128,1024]{1,0:T(8,128)(2,1)S(1)} %get-tuple-element.34), channel_id=1, source_target_pairs={{0,4},{4,8},{8,12},{12,16},{16,20},{20,24},{24,28},{1,5},{5,9},{9,... | collective-permute-start | bytes 786440 | tf_op jit(solution)/shard_map/ppermute | solution.py:29
  53.5 8.6 %collective-permute-start.10 = (bf16[128,1024]{1,0:T(8,128)(2,1)S(1)}, bf16[128,1024]{1,0:T(8,128)(2,1)S(1)}, u32[]{:S(2)}, u32[]{:S(2)}) collective-permute-start(bf16[128,1024]{1,0:T(8,128)(2,1)S(1)} %get-tuple-element.35), channel_id=1, source_target_pairs={{4,0},{8,4},{12,8},{16,12},{20,16},{24,20},{28,24},{5,1},{9,5},{13... | collective-permute-start | bytes 786440 | tf_op jit(solution)/shard_map/ppermute | solution.py:29

commit v3 on v2

--- a/solution.py
+++ b/solution.py
@@ -9,6 +9,7 @@
 from jax.experimental.pallas import tpu as pltpu
 from jax.sharding import PartitionSpec as P
 
+
 AMBIT = 128
 LANE = 128
 
@@ -23,10 +24,15 @@
     return -(-value // unit) * unit
 
 
-def moved(block, axis, target_of):
+def stepped(block, axis, step):
     count = lax.axis_size(axis)
-    pairs = [(i, target_of(i)) for i in range(count)]
-    return lax.ppermute(block, axis, [(i, j) for i, j in pairs if j is not None and 0 <= j < count])
+    pairs = [(i, i + step) for i in range(count) if 0 <= i + step < count]
+    return lax.ppermute(block, axis, pairs)
+
+
+def turned(block, axis, step):
+    count = lax.axis_size(axis)
+    return lax.ppermute(block, axis, [(i, (i + step) % count) for i in range(count)])
 
 
 def dot(leading, trailing):
@@ -80,7 +86,7 @@
     for k in range(first, last):
         scale = jnp.sqrt(jnp.full((1, 1), weights_ref[k] * (0.5 * steepness), jnp.float32))
         for part in range(2):
-            values = (pupils_ref[part, k] * scale).astype(jnp.bfloat16)
+            values = (pupils_ref[part, k - first] * scale).astype(jnp.bfloat16)
             columns = dot(values, col_ref[...]).astype(jnp.bfloat16)
             full = dot(row_ref[...], columns)
             pos_pos, pos_neg = full[:rows, :lanes], full[:rows, lanes:]
@@ -91,23 +97,42 @@
             out_ref[k, 6 + part] = (pos_neg - neg_pos).astype(jnp.bfloat16)
 
 
-def edges_kernel(low_ref, high_ref, first_ref, last_ref):
-    first_ref[...] = low_ref[...].astype(jnp.bfloat16)
-    last_ref[...] = high_ref[...].astype(jnp.bfloat16)
+def edges_kernel(mask_ref, target_ref, first_ref, last_ref, goal_ref, stage_ref, sems):
+    tile = mask_ref.shape[0]
+    whole = pltpu.make_async_copy(target_ref.at[:, tile:], goal_ref, sems.at[2])
+    copies = []
+    for index, start in enumerate((0, tile - AMBIT)):
+        copy = pltpu.make_async_copy(
+            mask_ref.at[pl.ds(start, AMBIT)], stage_ref.at[index], sems.at[index]
+        )
+        copy.start()
+        copies.append(copy)
+    whole.start()
+    for index, out_ref in enumerate((first_ref, last_ref)):
+        copies[index].wait()
+        out_ref[...] = stage_ref[index].astype(jnp.bfloat16)
+    whole.wait()
 
 
 def early_kernel(
-    rows, lanes, count, mask_ref, table_ref, pupils_ref, weights_ref, row_ref, col_ref, mid_ref, out_ref
+    rows, lanes, count, mask_ref, pupils_ref, table_ref, weights_ref, row_ref, col_ref,
+    mid_ref, out_ref, mask_stage, pupil_stage, sems,
 ):
     tile = mask_ref.shape[0]
+    mask_copy = pltpu.make_async_copy(mask_ref, mask_stage, sems.at[0])
+    mask_copy.start()
+    pupil_copy = pltpu.make_async_copy(pupils_ref.at[:, pl.ds(0, count)], pupil_stage, sems.at[1])
+    pupil_copy.start()
+    mask_copy.wait()
     mid_ref[...] = dot(
-        table_ref[:, AMBIT : AMBIT + tile], mask_ref[...].astype(jnp.bfloat16)
-    )
-    pupil_steps(rows, lanes, 0, count, pupils_ref, weights_ref, row_ref, col_ref, out_ref)
+        table_ref[:, AMBIT : AMBIT + tile], mask_stage[...].astype(jnp.bfloat16)
+    )
+    pupil_copy.wait()
+    pupil_steps(rows, lanes, 0, count, pupil_stage, weights_ref, row_ref, col_ref, out_ref)
 
 
 def partial_kernel(
-    rows, lanes, live_ref, mid_ref, top_ref, bottom_ref, table_ref, col_t_ref, own_ref, low_ref, high_ref, main_ref
+    live_ref, mid_ref, top_ref, bottom_ref, table_ref, col_t_ref, own_ref, low_ref, sent_ref
 ):
     extent = table_ref.shape[1]
     width = mid_ref.shape[1]
@@ -117,22 +142,26 @@
     total = total.astype(jnp.bfloat16)
     own_ref[...] = total[:, : tile + AMBIT]
     low_ref[...] = total[:, :AMBIT]
-    high_ref[...] = total[:, width - AMBIT :]
+    sent_ref[:, :AMBIT] = total[:, width - AMBIT :]
     main = dot(total[:, tile - AMBIT :], col_t_ref[: tile + AMBIT])
     shape = main.shape
     flag = (lax.broadcasted_iota(jnp.int32, shape, 0) == shape[0] - 1) & (
         lax.broadcasted_iota(jnp.int32, shape, 1) == shape[1] - 1
     )
     live = live_ref[0, live_ref.shape[1] - 1].astype(jnp.float32)
-    main_ref[...] = jnp.where(flag, live, main).astype(jnp.bfloat16)
+    sent_ref[:, AMBIT:] = jnp.where(flag, live, main).astype(jnp.bfloat16)
 
 
 def late_kernel(
-    rows, lanes, first, last, own_ref, col_t_ref, quads_ref, pupils_ref, weights_ref, row_ref, col_ref, base_ref, out_ref
+    rows, lanes, first, last, pupils_ref, own_ref, col_t_ref, quads_ref, weights_ref, row_ref, col_ref,
+    base_ref, out_ref, pupil_stage, sem,
 ):
+    copy = pltpu.make_async_copy(pupils_ref.at[:, pl.ds(first, last - first)], pupil_stage, sem)
+    copy.start()
     out_ref[:first] = quads_ref[...]
     base_ref[...] = dot(own_ref[...], col_t_ref[AMBIT:])
-    pupil_steps(rows, lanes, first, last, pupils_ref, weights_ref, row_ref, col_ref, out_ref)
+    copy.wait()
+    pupil_steps(rows, lanes, first, last, pupil_stage, weights_ref, row_ref, col_ref, out_ref)
 
 
 def core_kernel(
@@ -140,10 +169,8 @@
     lanes,
     live_ref,
     base_ref,
-    left_ref,
-    main_ref,
+    sent_ref,
     low_ref,
-    right_ref,
     goal_ref,
     other_ref,
     pupil_ref,
@@ -152,7 +179,6 @@
     col_ref,
     col_t_ref,
     out_ref,
-    other_out_ref,
     spec_ref,
     amp_ref,
     sec_ref,
@@ -168,13 +194,16 @@
     kernels = pupil_ref.shape[0]
     halves = [slice(start, start + 2 * LANE) for start in range(0, tile, 2 * LANE)]
     inner = slice(AMBIT, AMBIT + tile)
-    odd = lax.rem(lax.axis_index("col"), 2) == 1
-    spec_ref[0] = base_ref[...] + dot(left_ref[...], col_t_ref[:AMBIT])
-    rim = jnp.where(odd, low_ref[...], right_ref[...])
-    spec_ref[1] = main_ref[...].astype(jnp.float32) + dot(rim, col_t_ref[extent - AMBIT :])
-    other_live = jnp.max(main_ref[2 * rows - 16 :, 2 * lanes - LANE :].astype(jnp.float32)[15:, LANE - 1 :])
+    outer = lax.axis_index("col") == 0
+    left = sent_ref[:, :AMBIT]
+    left = jnp.where(outer, jnp.zeros_like(left), left)
+    spec_ref[0] = base_ref[...] + dot(left, col_t_ref[:AMBIT])
+    right = low_ref[...]
+    right = jnp.where(outer, jnp.zeros_like(right), right)
+    spec_ref[1] = sent_ref[:, AMBIT:].astype(jnp.float32) + dot(right, col_t_ref[extent - AMBIT :])
+    corner = sent_ref[2 * rows - 16 :, AMBIT + 2 * lanes - LANE :].astype(jnp.float32)
+    other_live = jnp.max(corner[15:, LANE - 1 :])
     out_ref[...] = jnp.zeros_like(out_ref)
-    other_out_ref[...] = jnp.zeros_like(other_out_ref)
 
     def work(item, carry):
         live = jnp.where(item == 0, live_ref[0, 0].astype(jnp.float32), other_live) > 0.0
@@ -292,34 +321,36 @@
 
             lax.fori_loop(0, kernels // 2, backward, 0)
 
-            def answer(ref):
-                ref[:rows, :lanes] = (ans_ref[0] + ans_ref[2]).astype(jnp.bfloat16)
-                ref[:rows, lanes:] = (ans_ref[3] - ans_ref[1]).astype(jnp.bfloat16)
-                ref[rows:, :lanes] = (-(ans_ref[1] + ans_ref[3])).astype(jnp.bfloat16)
-                ref[rows:, lanes:] = (ans_ref[2] - ans_ref[0]).astype(jnp.bfloat16)
+            def answer(first):
+                left, right = slice(first, first + lanes), slice(first + lanes, first + 2 * lanes)
+                out_ref[:rows, left] = (ans_ref[0] + ans_ref[2]).astype(jnp.bfloat16)
+                out_ref[:rows, right] = (ans_ref[3] - ans_ref[1]).astype(jnp.bfloat16)
+                out_ref[rows:, left] = (-(ans_ref[1] + ans_ref[3])).astype(jnp.bfloat16)
+                out_ref[rows:, right] = (ans_ref[2] - ans_ref[0]).astype(jnp.bfloat16)
 
             @pl.when(item == 0)
             def _():
-                answer(out_ref)
+                answer(0)
 
             @pl.when(item > 0)
             def _():
-                answer(other_out_ref)
+                answer(2 * lanes)
 
         return carry
 
     lax.fori_loop(0, 2, work, 0)
 
 
-def returned_kernel(
-    tile, mine_ref, second_ref, after_ref, before_ref, other_ref, row_t_ref, col_ref, out_ref, up_ref, down_ref, sum_ref
-):
+def returned_kernel(tile, mine_ref, sent_ref, row_t_ref, col_ref, out_ref, up_ref, down_ref, sum_ref):
     width = out_ref.shape[1]
     extent = row_t_ref.shape[0]
-    odd = lax.rem(lax.axis_index("col"), 2) == 1
-    before = jnp.where(odd, other_ref[...], before_ref[...])
+    lanes = mine_ref.shape[1] // 2
+    place = lax.axis_index("col")
+    before, after = mine_ref[:, lanes:], sent_ref[:, :lanes]
+    before = jnp.where(place == 0, jnp.zeros_like(before), before)
+    after = jnp.where(place == lax.axis_size("col") - 1, jnp.zeros_like(after), after)
     sum_ref[...] = jnp.zeros_like(sum_ref)
-    for place, value in zip(range(-1, 3), (before, mine_ref[...], second_ref[...], after_ref[...])):
+    for place, value in zip(range(-1, 3), (before, mine_ref[:, :lanes], sent_ref[:, lanes:], after)):
         start = place * tile - AMBIT
         low, high = max(0, start), min(width, start + extent)
         sum_ref[:, low:high] += dot(value, col_ref[:, low - start : high - start])
@@ -329,13 +360,16 @@
     down_ref[...] = dot(row_t_ref[extent - AMBIT :], mixed).astype(jnp.bfloat16)
 
 
-def update_kernel(mask_ref, mixed_ref, row_t_ref, out_ref, rims_ref, stage_ref, sem):
+def update_kernel(mask_ref, mixed_ref, row_t_ref, out_ref, rims_ref, stage_ref, sems):
     tile = mask_ref.shape[0]
-    stage_ref[...] = mask_ref[...] - step_rate * dot(
+    copy = pltpu.make_async_copy(mask_ref, stage_ref, sems.at[0])
+    copy.start()
+    copy.wait()
+    stage_ref[...] = stage_ref[...] - step_rate * dot(
         row_t_ref[AMBIT : AMBIT + tile], mixed_ref[...]
     )
     inner = pl.ds(AMBIT, tile - 2 * AMBIT)
-    copy = pltpu.make_async_copy(stage_ref.at[inner], out_ref.at[inner], sem)
+    copy = pltpu.make_async_copy(stage_ref.at[inner], out_ref.at[inner], sems.at[1])
     copy.start()
     rims_ref[:AMBIT] = stage_ref[:AMBIT]
     rims_ref[AMBIT:] = stage_ref[tile - AMBIT :]
@@ -375,54 +409,51 @@
     smem = pl.BlockSpec(memory_space=pltpu.SMEM)
     early = kernels // 2
 
-    def paired(index):
-        return index + 1 - 2 * (index % 2)
-
+    hbm = pl.BlockSpec(memory_space=pltpu.HBM)
+    dma = pltpu.SemaphoreType.DMA
     edge = shape((AMBIT, width), bf16)
-    first, last = pl.pallas_call(
+    first, last, goal = call(
         edges_kernel,
-        out_shape=(edge, edge),
-        grid=(1,),
-        in_specs=[
-            pl.BlockSpec((AMBIT, width), lambda i: (0, 0)),
-            pl.BlockSpec((AMBIT, width), lambda i: (tile // AMBIT - 1, 0)),
-        ],
-        out_specs=(pl.BlockSpec(memory_space=pltpu.VMEM), pl.BlockSpec(memory_space=pltpu.VMEM)),
-        compiler_params=pltpu.CompilerParams(vmem_limit_bytes=8 * MIB),
-    )(mask, mask)
-    top = moved(last, "row", lambda i: i + 1)
-    bottom = moved(first, "row", lambda i: i - 1)
-    other_goal = moved(target[:, tile:], "col", paired)
+        (edge, edge, shape((tile, tile), bf16)),
+        [hbm, hbm],
+        scratch=[pltpu.VMEM((2, AMBIT, width), f32), dma((3,))],
+        limit=52,
+    )(mask, target)
+    top = stepped(last, "row", 1)
+    bottom = stepped(first, "row", -1)
+    other_goal = turned(goal, "col", 1)
     middle, quads = call(
         partial(early_kernel, rows, lanes, early),
         (shape((2 * rows, width), f32), shape((early, 8, rows, lanes), bf16)),
-        [*vmem(3), smem, *vmem(2)],
+        [hbm, hbm, *vmem(1), smem, *vmem(2)],
+        scratch=[
+            pltpu.VMEM((tile, width), f32), pltpu.VMEM((2, early, size, size), f32), dma((2,)),
+        ],
+        limit=50,
         us=4,
-    )(mask, row_table, pupils, weights, row_pick, col_pick)
-    own, low, high, main = call(
-        partial(partial_kernel, rows, lanes),
+    )(mask, pupils, row_table, weights, row_pick, col_pick)
+    own, low, sending = call(
+        partial_kernel,
         (
             shape((2 * rows, tile + AMBIT), bf16),
             shape((2 * rows, AMBIT), bf16),
-            shape((2 * rows, AMBIT), bf16),
-            shape((2 * rows, 2 * lanes), bf16),
+            shape((2 * rows, AMBIT + 2 * lanes), bf16),
         ),
         [smem, *vmem(5)],
     )(live, middle, top, bottom, row_table, col_table_t)
-    left = moved(high, "col", lambda i: i + 1)
-    other_main = moved(main, "col", paired)
-    right = moved(low, "col", lambda i: i - 2 if i % 2 == 0 else None)
+    sent = turned(sending, "col", 1)
     base, all_quads = call(
         partial(late_kernel, rows, lanes, early, kernels),
         (shape((2 * rows, 2 * lanes), f32), shape((kernels, 8, rows, lanes), bf16)),
-        [*vmem(4), smem, *vmem(2)],
+        [hbm, *vmem(3), smem, *vmem(2)],
+        scratch=[pltpu.VMEM((2, kernels - early, size, size), f32), dma],
+        limit=48,
         us=4,
-    )(own, col_table_t, quads, pupils, weights, row_pick, col_pick)
-    answer = shape((2 * rows, 2 * lanes), bf16)
-    mine, other = call(
+    )(pupils, own, col_table_t, quads, weights, row_pick, col_pick)
+    answers = call(
         partial(core_kernel, rows, lanes),
-        (answer, answer),
-        [smem, *vmem(12)],
+        shape((2 * rows, 4 * lanes), bf16),
+        [smem, *vmem(10)],
         scratch=[
             pltpu.VMEM((2, 2 * rows, 2 * lanes), f32),
             pltpu.VMEM((2, 4 * rows, 2 * lanes), bf16),
@@ -437,28 +468,26 @@
         limit=36,
         us=15,
     )(
-        live, base, left, other_main, low, right, target, other_goal, all_quads,
+        live, base, sent, low, target, other_goal, all_quads,
         row_table, row_table_t, col_table, col_table_t,
     )
-    second = moved(other, "col", paired)
-    after = moved(mine, "col", lambda i: i - 1)
-    before = moved(other, "col", lambda i: i + 2 if i % 2 == 0 else None)
+    returned = turned(answers, "col", -1)
     mixed, up, down = call(
         partial(returned_kernel, tile),
         (shape((2 * rows, width), bf16), shape((AMBIT, width), bf16), shape((AMBIT, width), bf16)),
-        vmem(7),
+        vmem(4),
         scratch=[pltpu.VMEM((2 * rows, width), f32)],
-    )(mine, second, after, before, other, row_table_t, col_table)
-    from_above = moved(down, "row", lambda i: i + 1)
-    from_below = moved(up, "row", lambda i: i - 1)
+    )(answers, returned, row_table_t, col_table)
+    from_above = stepped(down, "row", 1)
+    from_below = stepped(up, "row", -1)
     anywhere = pl.BlockSpec(memory_space=pl.ANY)
     whole, rims = shape((tile, width), f32), shape((2 * AMBIT, width), f32)
     updated, edges = pl.pallas_call(
         update_kernel,
         out_shape=(whole, rims),
-        in_specs=vmem(3),
+        in_specs=[hbm, *vmem(2)],
         out_specs=(anywhere, *vmem(1)),
-        scratch_shapes=[pltpu.VMEM((tile, width), f32), pltpu.SemaphoreType.DMA],
+        scratch_shapes=[pltpu.VMEM((tile, width), f32), dma((2,))],
         cost_estimate=pl.CostEstimate(flops=10**9, bytes_accessed=2 * 10**6, transcendentals=0),
         compiler_params=pltpu.CompilerParams(vmem_limit_bytes=16 * MIB),
     )(mask, mixed, row_table_t)

time: 63.7 us -> 54.1 us (0.85)
  Pallas kernels: 20.5 us -> 13.3 us
  starting transfers between devices: 23.5 us -> 28.4 us
  local copies, waits for them, and re-layouts: 4.71 us -> 0.05 us
  waiting for transfers between devices: 14.2 us -> 11.3 us
    pallas_call x4, Pallas kernels: 15.5 us -> 4.85 us  [the longest x1 1.56 us: body(): pl.pallas_call(update_kernel, out_shape=(whole, rims), in_specs=[hbm, *vm...]
    ppermute x11 -> x7, starting transfers between devices: 23.5 us -> 28.4 us  [the longest x3 16.5 us: turned(): lax.ppermute(block, axis, [(i, (i + step) % count) for i in range(count)])]
    unnamed x26 -> x20, local copies, waits for them, and re-layouts: 3.64 us -> 0.05 us
    ppermute x11 -> x7, waiting for transfers between devices: 14.2 us -> 11.3 us  [the longest x4 8.11 us: stepped(): return lax.ppermute(block, axis, pairs)]
    pallas_call x1, Pallas kernels: 1.65 us -> 3.57 us  [body(): call(partial(early_kernel, rows, lanes, early), (shape((2 * rows, width),...]
    pallas_call x1, Pallas kernels: 1.78 us -> 3.33 us  [body(): call(partial(late_kernel, rows, lanes, early, kernels), (shape((2 * rows,...]
    slice x1 -> x0, local copies, waits for them, and re-layouts: 1.08 us -> none  [body(): other_goal = moved(target[:, tile:], 'col', paired)]
  transfers between devices with their start and end apart: 11 -> 7, of which waited for: 5 -> 4; matrix products, arithmetic and copies ran while one was open for 0% -> 0% of each run, Pallas kernels for 9% -> 18%
where the time goes in v3:
time: 54.1 us; the launch traced here: 53.3 us
  starting transfers between devices  28.4 us (52%)
  Pallas kernels  13.3 us (25%)
  waiting for transfers between devices  11.3 us (21%)
    ppermute x3, starting transfers between devices, turned(): lax.ppermute(block, axis, [(i, (i + step) % count) for i in range(count)])  16.5 us
    ppermute x4, starting transfers between devices, stepped(): return lax.ppermute(block, axis, pairs)  11.8 us
    ppermute x4, waiting for transfers between devices, stepped(): return lax.ppermute(block, axis, pairs)  8.11 us
    pallas_call x1, Pallas kernels, body(): call(partial(early_kernel, rows, lanes, early), (shape((2 * rows, width),...  3.57 us
    pallas_call x1, Pallas kernels, body(): call(partial(late_kernel, rows, lanes, early, kernels), (shape((2 * rows,...  3.33 us
    ppermute x3, waiting for transfers between devices, turned(): lax.ppermute(block, axis, [(i, (i + step) % count) for i in range(count)])  3.2 us
    pallas_call x1, Pallas kernels, body(): pl.pallas_call(update_kernel, out_shape=(whole, rims), in_specs=[hbm, *vm...  1.56 us
    pallas_call x1, Pallas kernels, body(): call(edges_kernel, (edge, edge, shape((tile, tile), bf16)), [hbm, hbm], s...  1.44 us
  transfers between devices with their start and end apart: 7, of which 4 were waited for; matrix products, arithmetic and copies ran while one was open for 0% of the time, Pallas kernels for 18%

profile of v3, /device:TPU:11, one launch (start us, length us, event | category | flops | bytes accessed | tf_op | source)
XLA Modules:
  0.0 53.3 jit_solution(5992130144970553187)
XLA Ops:
  0.0 0.0 copy-start.2
  0.0 1.4 %shard_map.110 = (bf16[128,1024]{1,0:T(8,128)(2,1)S(1)}, bf16[128,1024]{1,0:T(8,128)(2,1)S(1)}, bf16[512,512]{1,0:T(8,128)(2,1)S(1)}) custom-call(f32[512,1024]{1,0:T(8,128)} %mask_ref.5, bf16[512,1024]{1,0:T(8,128)(2,1)} %goal_ref.1), custom_call_target="tpu_custom_call" | custom-call | flops 500000000 | bytes 1000000 | tf_op jit(solution)/shard_map/pallas_call | solution.py:415
  1.5 1.3 %collective-permute-start.3 = (bf16[512,512]{1,0:T(8,128)(2,1)S(1)}, bf16[512,512]{1,0:T(8,128)(2,1)S(1)}, u32[]{:S(2)}, u32[]{:S(2)}) collective-permute-start(bf16[512,512]{1,0:T(8,128)(2,1)S(1)} %get-tuple-element.28), channel_id=1, source_target_pairs={{0,1},{1,2},{2,3},{3,0},{4,5},{5,6},{6,7},{7,4},{8,9},{9,10},{10,1... | collective-permute-start | bytes 1572872 | tf_op jit(solution)/shard_map/ppermute | solution.py:35
  2.8 3.9 %collective-permute-start = (bf16[128,1024]{1,0:T(8,128)(2,1)S(1)}, bf16[128,1024]{1,0:T(8,128)(2,1)S(1)}, u32[]{:S(2)}, u32[]{:S(2)}) collective-permute-start(bf16[128,1024]{1,0:T(8,128)(2,1)S(1)} %get-tuple-element.21), channel_id=1, source_target_pairs={{0,4},{4,8},{8,12},{12,16},{16,20},{20,24},{24,28},{1,5},{5,9},{9,... | collective-permute-start | bytes 786440 | tf_op jit(solution)/shard_map/ppermute | solution.py:30
  6.8 0.0 copy-start.3
  6.8 0.0 copy-start.6
  6.8 2.1 %collective-permute-start.1 = (bf16[128,1024]{1,0:T(8,128)(2,1)S(1)}, bf16[128,1024]{1,0:T(8,128)(2,1)S(1)}, u32[]{:S(2)}, u32[]{:S(2)}) collective-permute-start(bf16[128,1024]{1,0:T(8,128)(2,1)S(1)} %get-tuple-element.22), channel_id=1, source_target_pairs={{4,0},{8,4},{12,8},{16,12},{20,16},{24,20},{28,24},{5,1},{9,5},{13... | collective-permute-start | bytes 786440 | tf_op jit(solution)/shard_map/ppermute | solution.py:30
  8.9 0.0 copy-done.7
  8.9 0.0 copy-done.9
  8.9 3.6 %shard_map.109 = (f32[160,1024]{1,0:T(8,128)S(1)}, bf16[6,8,80,128]{3,2,1,0:T(8,128)(2,1)S(1)}) custom-call(f32[512,1024]{1,0:T(8,128)} %mask_ref.5, f32[2,12,144,144]{3,2,1,0:T(8,128)} %pupils_ref.3, bf16[160,768]{1,0:T(8,128)(2,1)S(1)} %copy-done.7, f32[12]{0:T(128)S(1)} %copy-done.2, bf16[160,144]{1,0:T(8,128)(2,1)S(1)} %copy-done.8, ...), custom_call_target="tpu_custom_call" | custom-call | flops 2000000000 | bytes 4000000 | tf_op jit(solution)/shard_map/pallas_call | solution.py:425
  12.5 0.0 collective-permute-done.top_ref
  12.5 3.0 %collective-permute-done.1.bottom_ref = bf16[128,1024]{1,0:T(8,128)(2,1)S(1)} collective-permute-done((bf16[128,1024]{1,0:T(8,128)(2,1)S(1)}, bf16[128,1024]{1,0:T(8,128)(2,1)S(1)}, u32[]{:S(2)}, u32[]{:S(2)}) %collective-permute-start.1) | collective-permute-done | bytes 262176 | tf_op jit(solution)/shard_map/ppermute | solution.py:30
  15.5 0.0 copy-done.3
  15.5 1.1 %shard_map.111 = (bf16[160,640]{1,0:T(8,128)(2,1)S(1)}, bf16[160,128]{1,0:T(8,128)(2,1)S(1)}, bf16[160,384]{1,0:T(8,128)(2,1)S(1)}) custom-call(s32[1,2]{1,0:T(1,128)S(1)} %copy-done.3, f32[160,1024]{1,0:T(8,128)S(1)} %get-tuple-element.20.mid_ref, bf16[128,1024]{1,0:T(8,128)(2,1)S(1)} %collective-permute-done.top_ref, ...), custom_call_target="tpu_custom_call" | custom-call | flops 500000000 | bytes 1000000 | tf_op jit(solution)/shard_map/pallas_call | solution.py:435
  16.6 1.3 %collective-permute-start.2 = (bf16[160,384]{1,0:T(8,128)(2,1)S(1)}, bf16[160,384]{1,0:T(8,128)(2,1)S(1)}, u32[]{:S(2)}, u32[]{:S(2)}) collective-permute-start(bf16[160,384]{1,0:T(8,128)(2,1)S(1)} %get-tuple-element.26), channel_id=1, source_target_pairs={{0,1},{1,2},{2,3},{3,0},{4,5},{5,6},{6,7},{7,4},{8,9},{9,10},{10,1... | collective-permute-start | bytes 368648 | tf_op jit(solution)/shard_map/ppermute | solution.py:35
  18.0 3.3 %shard_map.112 = (f32[160,256]{1,0:T(8,128)S(1)}, bf16[12,8,80,128]{3,2,1,0:T(8,128)(2,1)S(1)}) custom-call(f32[2,12,144,144]{3,2,1,0:T(8,128)} %pupils_ref.3, bf16[160,640]{1,0:T(8,128)(2,1)S(1)} %get-tuple-element.23.own_ref, bf16[768,256]{1,0:T(8,128)(2,1)S(1)} %copy-done.6, bf16[6,8,80,128]{3,2,1,0:T(8,128)(2,1)S(1)} %get-tuple-element.24.quads_ref, ...), custom_call_target="tpu_custom_call" | custom-call | flops 2000000000 | bytes 4000000 | tf_op jit(solution)/shard_map/pallas_call | solution.py:445
  21.3 0.0 collective-permute-done.2.sent_ref
  21.3 0.0 collective-permute-done.3.other_ref
  21.3 0.0 copy-done.1
  21.4 0.0 copy-done.4
  21.4 0.0 copy-done.5
  21.4 0.0 copy-start
  21.4 0.8 %shard_map.113.mine_ref = bf16[160,512]{1,0:T(8,128)(2,1)S(1)} custom-call(s32[1,2]{1,0:T(1,128)S(1)} %copy-done.3, f32[160,256]{1,0:T(8,128)S(1)} %get-tuple-element.25.base_ref, bf16[160,384]{1,0:T(8,128)(2,1)S(1)} %collective-permute-done.2.sent_ref, bf16[160,128]{1,0:T(8,128)(2,1)S(1)} %get-tuple-element.27.low_ref, bf16[512,1024]{1,0:T(8,128)(2,1)S(1)} %copy-done.1, ...), custom_call_target="tpu_custom_call" | custom-call | flops 7500000256 | bytes 15000000 | tf_op jit(solution)/shard_map/pallas_call | solution.py:453
  22.1 13.8 %collective-permute-start.4 = (bf16[160,512]{1,0:T(8,128)(2,1)S(1)}, bf16[160,512]{1,0:T(8,128)(2,1)S(1)}, u32[]{:S(2)}, u32[]{:S(2)}) collective-permute-start(bf16[160,512]{1,0:T(8,128)(2,1)S(1)} %shard_map.113.mine_ref), channel_id=1, source_target_pairs={{0,3},{1,0},{2,1},{3,2},{4,7},{5,4},{6,5},{7,6},{8,11},{9,8},{10,9... | collective-permute-start | bytes 491528 | tf_op jit(solution)/shard_map/ppermute | solution.py:35
  36.0 3.2 %collective-permute-done.4.sent_ref = bf16[160,512]{1,0:T(8,128)(2,1)S(1)} collective-permute-done((bf16[160,512]{1,0:T(8,128)(2,1)S(1)}, bf16[160,512]{1,0:T(8,128)(2,1)S(1)}, u32[]{:S(2)}, u32[]{:S(2)}) %collective-permute-start.4) | collective-permute-done | bytes 163872 | tf_op jit(solution)/shard_map/ppermute | solution.py:35
  39.2 0.6 %shard_map.114 = (bf16[160,1024]{1,0:T(8,128)(2,1)S(1)}, bf16[128,1024]{1,0:T(8,128)(2,1)S(1)}, bf16[128,1024]{1,0:T(8,128)(2,1)S(1)}) custom-call(bf16[160,512]{1,0:T(8,128)(2,1)S(1)} %shard_map.113.mine_ref, bf16[160,512]{1,0:T(8,128)(2,1)S(1)} %collective-permute-done.4.sent_ref, bf16[768,160]{1,0:T(8,128)(2,1)S(1)} %copy-done.4, ...), custom_call_target="tpu_custom_call" | custom-call | flops 500000000 | bytes 1000000 | tf_op jit(solution)/shard_map/pallas_call | solution.py:475
  39.7 3.9 %collective-permute-start.5 = (bf16[128,1024]{1,0:T(8,128)(2,1)S(1)}, bf16[128,1024]{1,0:T(8,128)(2,1)S(1)}, u32[]{:S(2)}, u32[]{:S(2)}) collective-permute-start(bf16[128,1024]{1,0:T(8,128)(2,1)S(1)} %get-tuple-element.30), channel_id=1, source_target_pairs={{0,4},{4,8},{8,12},{12,16},{16,20},{20,24},{24,28},{1,5},{5,9},{9,... | collective-permute-start | bytes 786440 | tf_op jit(solution)/shard_map/ppermute | solution.py:30
  43.7 1.9 %collective-permute-start.6 = (bf16[128,1024]{1,0:T(8,128)(2,1)S(1)}, bf16[128,1024]{1,0:T(8,128)(2,1)S(1)}, u32[]{:S(2)}, u32[]{:S(2)}) collective-permute-start(bf16[128,1024]{1,0:T(8,128)(2,1)S(1)} %get-tuple-element.31), channel_id=1, source_target_pairs={{4,0},{8,4},{12,8},{16,12},{20,16},{24,20},{28,24},{5,1},{9,5},{13... | collective-permute-start | bytes 786440 | tf_op jit(solution)/shard_map/ppermute | solution.py:30
  45.6 1.6 %shard_map.115 = (f32[512,1024]{1,0:T(8,128)}, f32[256,1024]{1,0:T(8,128)S(1)}) custom-call(f32[512,1024]{1,0:T(8,128)S(1)} %copy-done, bf16[160,1024]{1,0:T(8,128)(2,1)S(1)} %get-tuple-element.32.mixed_ref, bf16[768,160]{1,0:T(8,128)(2,1)S(1)} %copy-done.4), custom_call_target="tpu_custom_call" | custom-call | flops 1000000000 | bytes 2000000 | tf_op jit(solution)/shard_map/pallas_call | solution.py:485
  47.2 1.2 %collective-permute-done.5.above_ref = bf16[128,1024]{1,0:T(8,128)(2,1)S(1)} collective-permute-done((bf16[128,1024]{1,0:T(8,128)(2,1)S(1)}, bf16[128,1024]{1,0:T(8,128)(2,1)S(1)}, u32[]{:S(2)}, u32[]{:S(2)}) %collective-permute-start.5) | collective-permute-done | bytes 262176 | tf_op jit(solution)/shard_map/ppermute | solution.py:30
  48.3 3.9 %collective-permute-done.6.below_ref = bf16[128,1024]{1,0:T(8,128)(2,1)S(1)} collective-permute-done((bf16[128,1024]{1,0:T(8,128)(2,1)S(1)}, bf16[128,1024]{1,0:T(8,128)(2,1)S(1)}, u32[]{:S(2)}, u32[]{:S(2)}) %collective-permute-start.6) | collective-permute-done | bytes 262176 | tf_op jit(solution)/shard_map/ppermute | solution.py:30
  52.2 1.0 %shard_map.116 = f32[512,1024]{1,0:T(8,128)} custom-call(bf16[128,1024]{1,0:T(8,128)(2,1)S(1)} %collective-permute-done.5.above_ref, bf16[128,1024]{1,0:T(8,128)(2,1)S(1)} %collective-permute-done.6.below_ref, f32[256,1024]{1,0:T(8,128)S(1)} %get-tuple-element.33.rims_ref, f32[512,1024]{1,0:T(8,128)} %get-tuple-element.34.base_ref), custom_call_target="tpu_custom_call", output_to_operand_aliasing={{}: (3, {})} | custom-call | tf_op jit(solution)/shard_map/pallas_call | solution.py:494
  (10 shorter events, 0.0 us)
Async XLA Ops:
  0.0 8.9 %copy-start.7 = (bf16[160,768]{1,0:T(8,128)(2,1)S(1)}, bf16[160,768]{1,0:T(8,128)(2,1)}, u32[]{:S(2)}) copy-start(bf16[160,768]{1,0:T(8,128)(2,1)} %constant.14.clone.table_ref.row_ref) | copy-start | bytes 737284
  0.0 8.9 %copy-start.9 = (bf16[144,256]{1,0:T(8,128)(2,1)S(1)}, bf16[144,256]{1,0:T(8,128)(2,1)}, u32[]{:S(2)}) copy-start(bf16[144,256]{1,0:T(8,128)(2,1)} %constant.13.clone.col_ref) | copy-start | bytes 221188
  0.0 8.9 %copy-start.8 = (bf16[160,144]{1,0:T(8,128)(2,1)S(1)}, bf16[160,144]{1,0:T(8,128)(2,1)}, u32[]{:S(2)}) copy-start(bf16[160,144]{1,0:T(8,128)(2,1)} %constant.12.clone.row_ref) | copy-start | bytes 138244
  0.0 8.9 %copy-start.2 = (f32[12]{0:T(128)S(1)}, f32[12]{0:T(128)}, u32[]{:S(2)}) copy-start(f32[12]{0:T(128)} %weights_ref.3) | copy-start | bytes 148
  1.5 19.9 %collective-permute-start.3 = (bf16[512,512]{1,0:T(8,128)(2,1)S(1)}, bf16[512,512]{1,0:T(8,128)(2,1)S(1)}, u32[]{:S(2)}, u32[]{:S(2)}) collective-permute-start(bf16[512,512]{1,0:T(8,128)(2,1)S(1)} %get-tuple-element.28), channel_id=1, source_target_pairs={{0,1},{1,2},{2,3},{3,0},{4,5},{5,6},{6,7},{7,4},{8,9},{9,10},{10,1... | collective-permute-start | bytes 1572872 | tf_op jit(solution)/shard_map/ppermute | solution.py:35
  2.8 9.7 %collective-permute-start = (bf16[128,1024]{1,0:T(8,128)(2,1)S(1)}, bf16[128,1024]{1,0:T(8,128)(2,1)S(1)}, u32[]{:S(2)}, u32[]{:S(2)}) collective-permute-start(bf16[128,1024]{1,0:T(8,128)(2,1)S(1)} %get-tuple-element.21), channel_id=1, source_target_pairs={{0,4},{4,8},{8,12},{12,16},{16,20},{20,24},{24,28},{1,5},{5,9},{9,... | collective-permute-start | bytes 786440 | tf_op jit(solution)/shard_map/ppermute | solution.py:30
  6.8 8.7 %copy-start.3 = (s32[1,2]{1,0:T(1,128)S(1)}, s32[1,2]{1,0:T(1,128)}, u32[]{:S(2)}) copy-start(s32[1,2]{1,0:T(1,128)} %live_ref.3) | copy-start | bytes 28
  6.8 8.7 %copy-start.6 = (bf16[768,256]{1,0:T(8,128)(2,1)S(1)}, bf16[768,256]{1,0:T(8,128)(2,1)}, u32[]{:S(2)}) copy-start(bf16[768,256]{1,0:T(8,128)(2,1)} %constant.17.clone.col_t_ref) | copy-start | bytes 1179652
  6.8 8.7 %collective-permute-start.1 = (bf16[128,1024]{1,0:T(8,128)(2,1)S(1)}, bf16[128,1024]{1,0:T(8,128)(2,1)S(1)}, u32[]{:S(2)}, u32[]{:S(2)}) collective-permute-start(bf16[128,1024]{1,0:T(8,128)(2,1)S(1)} %get-tuple-element.22), channel_id=1, source_target_pairs={{4,0},{8,4},{12,8},{16,12},{20,16},{24,20},{28,24},{5,1},{9,5},{13... | collective-permute-start | bytes 786440 | tf_op jit(solution)/shard_map/ppermute | solution.py:30
  16.6 4.7 %collective-permute-start.2 = (bf16[160,384]{1,0:T(8,128)(2,1)S(1)}, bf16[160,384]{1,0:T(8,128)(2,1)S(1)}, u32[]{:S(2)}, u32[]{:S(2)}) collective-permute-start(bf16[160,384]{1,0:T(8,128)(2,1)S(1)} %get-tuple-element.26), channel_id=1, source_target_pairs={{0,1},{1,2},{2,3},{3,0},{4,5},{5,6},{6,7},{7,4},{8,9},{9,10},{10,1... | collective-permute-start | bytes 368648 | tf_op jit(solution)/shard_map/ppermute | solution.py:35
  18.0 3.4 %copy-start.1 = (bf16[512,1024]{1,0:T(8,128)(2,1)S(1)}, bf16[512,1024]{1,0:T(8,128)(2,1)}, u32[]{:S(2)}) copy-start(bf16[512,1024]{1,0:T(8,128)(2,1)} %goal_ref.1) | copy-start | bytes 3145732
  18.0 3.4 %copy-start.4 = (bf16[768,160]{1,0:T(8,128)(2,1)S(1)}, bf16[768,160]{1,0:T(8,128)(2,1)}, u32[]{:S(2)}) copy-start(bf16[768,160]{1,0:T(8,128)(2,1)} %constant.15.clone.row_t_ref) | copy-start | bytes 737284
  18.0 3.4 %copy-start.5 = (bf16[256,768]{1,0:T(8,128)(2,1)S(1)}, bf16[256,768]{1,0:T(8,128)(2,1)}, u32[]{:S(2)}) copy-start(bf16[256,768]{1,0:T(8,128)(2,1)} %constant.16.clone.col_ref) | copy-start | bytes 1179652
  21.4 24.2 %copy-start = (f32[512,1024]{1,0:T(8,128)S(1)}, f32[512,1024]{1,0:T(8,128)}, u32[]{:S(2)}) copy-start(f32[512,1024]{1,0:T(8,128)} %mask_ref.5) | copy-start | bytes 6291460
  22.1 17.0 %collective-permute-start.4 = (bf16[160,512]{1,0:T(8,128)(2,1)S(1)}, bf16[160,512]{1,0:T(8,128)(2,1)S(1)}, u32[]{:S(2)}, u32[]{:S(2)}) collective-permute-start(bf16[160,512]{1,0:T(8,128)(2,1)S(1)} %shard_map.113.mine_ref), channel_id=1, source_target_pairs={{0,3},{1,0},{2,1},{3,2},{4,7},{5,4},{6,5},{7,6},{8,11},{9,8},{10,9... | collective-permute-start | bytes 491528 | tf_op jit(solution)/shard_map/ppermute | solution.py:35
  39.7 8.6 %collective-permute-start.5 = (bf16[128,1024]{1,0:T(8,128)(2,1)S(1)}, bf16[128,1024]{1,0:T(8,128)(2,1)S(1)}, u32[]{:S(2)}, u32[]{:S(2)}) collective-permute-start(bf16[128,1024]{1,0:T(8,128)(2,1)S(1)} %get-tuple-element.30), channel_id=1, source_target_pairs={{0,4},{4,8},{8,12},{12,16},{16,20},{20,24},{24,28},{1,5},{5,9},{9,... | collective-permute-start | bytes 786440 | tf_op jit(solution)/shard_map/ppermute | solution.py:30
  43.7 8.6 %collective-permute-start.6 = (bf16[128,1024]{1,0:T(8,128)(2,1)S(1)}, bf16[128,1024]{1,0:T(8,128)(2,1)S(1)}, u32[]{:S(2)}, u32[]{:S(2)}) collective-permute-start(bf16[128,1024]{1,0:T(8,128)(2,1)S(1)} %get-tuple-element.31), channel_id=1, source_target_pairs={{4,0},{8,4},{12,8},{16,12},{20,16},{24,20},{28,24},{5,1},{9,5},{13... | collective-permute-start | bytes 786440 | tf_op jit(solution)/shard_map/ppermute | solution.py:30

commit v4 on v3

--- a/solution.py
+++ b/solution.py
@@ -30,9 +30,18 @@
     return lax.ppermute(block, axis, pairs)
 
 
-def turned(block, axis, step):
-    count = lax.axis_size(axis)
-    return lax.ppermute(block, axis, [(i, (i + step) % count) for i in range(count)])
+def turned(block, step):
+    height, count = lax.axis_size("row"), lax.axis_size("col")
+    pairs = [
+        (row * count + col, row * count + (col + (step if row % 2 == 0 else -step)) % count)
+        for row in range(height)
+        for col in range(count)
+    ]
+    return lax.ppermute(block, ("row", "col"), pairs)
+
+
+def row_parity():
+    return lax.rem(lax.axis_index("row"), 2)
 
 
 def dot(leading, trailing):
@@ -99,7 +108,8 @@
 
 def edges_kernel(mask_ref, target_ref, first_ref, last_ref, goal_ref, stage_ref, sems):
     tile = mask_ref.shape[0]
-    whole = pltpu.make_async_copy(target_ref.at[:, tile:], goal_ref, sems.at[2])
+    far = pl.multiple_of((1 - row_parity()) * tile, LANE)
+    whole = pltpu.make_async_copy(target_ref.at[:, pl.ds(far, tile)], goal_ref, sems.at[2])
     copies = []
     for index, start in enumerate((0, tile - AMBIT)):
         copy = pltpu.make_async_copy(
@@ -132,7 +142,7 @@
 
 
 def partial_kernel(
-    live_ref, mid_ref, top_ref, bottom_ref, table_ref, col_t_ref, own_ref, low_ref, sent_ref
+    live_ref, mid_ref, top_ref, bottom_ref, table_ref, col_t_ref, own_ref, kept_ref, sent_ref
 ):
     extent = table_ref.shape[1]
     width = mid_ref.shape[1]
@@ -140,16 +150,31 @@
     total = mid_ref[...] + dot(table_ref[:, :AMBIT], top_ref[...])
     total = total + dot(table_ref[:, extent - AMBIT :], bottom_ref[...])
     total = total.astype(jnp.bfloat16)
-    own_ref[...] = total[:, : tile + AMBIT]
-    low_ref[...] = total[:, :AMBIT]
-    sent_ref[:, :AMBIT] = total[:, width - AMBIT :]
-    main = dot(total[:, tile - AMBIT :], col_t_ref[: tile + AMBIT])
-    shape = main.shape
-    flag = (lax.broadcasted_iota(jnp.int32, shape, 0) == shape[0] - 1) & (
-        lax.broadcasted_iota(jnp.int32, shape, 1) == shape[1] - 1
-    )
-    live = live_ref[0, live_ref.shape[1] - 1].astype(jnp.float32)
-    sent_ref[:, AMBIT:] = jnp.where(flag, live, main).astype(jnp.bfloat16)
+    parity = row_parity()
+    live = live_ref[0, 1 - parity].astype(jnp.float32)
+
+    def store(near, far, far_table, facing, kept):
+        own_ref[...] = total[:, near]
+        kept_ref[...] = total[:, kept]
+        sent_ref[:, :AMBIT] = total[:, facing]
+        main = dot(total[:, far], col_t_ref[far_table])
+        shape = main.shape
+        flag = (lax.broadcasted_iota(jnp.int32, shape, 0) == shape[0] - 1) & (
+            lax.broadcasted_iota(jnp.int32, shape, 1) == shape[1] - 1
+        )
+        sent_ref[:, AMBIT:] = jnp.where(flag, live, main).astype(jnp.bfloat16)
+
+    reach = tile + AMBIT
+    first, last = slice(0, reach), slice(width - reach, width)
+    low, high = slice(0, AMBIT), slice(width - AMBIT, width)
+
+    @pl.when(parity == 0)
+    def _():
+        store(first, last, slice(0, reach), high, low)
+
+    @pl.when(parity > 0)
+    def _():
+        store(last, first, slice(AMBIT, extent), low, high)
 
 
 def late_kernel(
@@ -159,7 +184,9 @@
     copy = pltpu.make_async_copy(pupils_ref.at[:, pl.ds(first, last - first)], pupil_stage, sem)
     copy.start()
     out_ref[:first] = quads_ref[...]
-    base_ref[...] = dot(own_ref[...], col_t_ref[AMBIT:])
+    reach = own_ref.shape[1]
+    start = pl.multiple_of((1 - row_parity()) * AMBIT, AMBIT)
+    base_ref[...] = dot(own_ref[...], col_t_ref[pl.ds(start, reach)])
     copy.wait()
     pupil_steps(rows, lanes, first, last, pupil_stage, weights_ref, row_ref, col_ref, out_ref)
 
@@ -170,7 +197,7 @@
     live_ref,
     base_ref,
     sent_ref,
-    low_ref,
+    kept_ref,
     goal_ref,
     other_ref,
     pupil_ref,
@@ -194,19 +221,25 @@
     kernels = pupil_ref.shape[0]
     halves = [slice(start, start + 2 * LANE) for start in range(0, tile, 2 * LANE)]
     inner = slice(AMBIT, AMBIT + tile)
-    outer = lax.axis_index("col") == 0
-    left = sent_ref[:, :AMBIT]
-    left = jnp.where(outer, jnp.zeros_like(left), left)
-    spec_ref[0] = base_ref[...] + dot(left, col_t_ref[:AMBIT])
-    right = low_ref[...]
-    right = jnp.where(outer, jnp.zeros_like(right), right)
-    spec_ref[1] = sent_ref[:, AMBIT:].astype(jnp.float32) + dot(right, col_t_ref[extent - AMBIT :])
+    parity = row_parity()
+    outer = lax.axis_index("col") == parity * (lax.axis_size("col") - 1)
+    ends = [
+        pl.multiple_of(side * (extent - AMBIT), AMBIT) for side in (parity, 1 - parity)
+    ]
+    facing = sent_ref[:, :AMBIT]
+    facing = jnp.where(outer, jnp.zeros_like(facing), facing)
+    spec_ref[0] = base_ref[...] + dot(facing, col_t_ref[pl.ds(ends[0], AMBIT)])
+    kept = kept_ref[...]
+    kept = jnp.where(outer, jnp.zeros_like(kept), kept)
+    spec_ref[1] = sent_ref[:, AMBIT:].astype(jnp.float32) + dot(
+        kept, col_t_ref[pl.ds(ends[1], AMBIT)]
+    )
     corner = sent_ref[2 * rows - 16 :, AMBIT + 2 * lanes - LANE :].astype(jnp.float32)
     other_live = jnp.max(corner[15:, LANE - 1 :])
     out_ref[...] = jnp.zeros_like(out_ref)
 
     def work(item, carry):
-        live = jnp.where(item == 0, live_ref[0, 0].astype(jnp.float32), other_live) > 0.0
+        live = jnp.where(item == 0, live_ref[0, parity].astype(jnp.float32), other_live) > 0.0
 
         @pl.when(live)
         def _():
@@ -270,19 +303,20 @@
 
             lax.fori_loop(0, kernels // 2, forward, 0)
 
-            def slopes(ref):
+            def slopes(ref, first):
                 for where in halves:
+                    place = pl.ds(pl.multiple_of(first + where.start, LANE), 2 * LANE)
                     level = jnp.tanh(total_ref[:, where] - 0.5 * steepness * threshold_level)
-                    excess = 0.5 * level + 0.5 - ref[:, where].astype(jnp.float32)
+                    excess = 0.5 * level + 0.5 - ref[:, place].astype(jnp.float32)
                     slope_ref[:, where] = (excess * (1.0 - level * level)).astype(jnp.bfloat16)
 
             @pl.when(item == 0)
             def _():
-                slopes(goal_ref)
+                slopes(goal_ref, parity * tile)
 
             @pl.when(item > 0)
             def _():
-                slopes(other_ref)
+                slopes(other_ref, 0)
 
             def back(k, buf):
                 for where in halves:
@@ -345,12 +379,18 @@
     width = out_ref.shape[1]
     extent = row_t_ref.shape[0]
     lanes = mine_ref.shape[1] // 2
-    place = lax.axis_index("col")
-    before, after = mine_ref[:, lanes:], sent_ref[:, :lanes]
-    before = jnp.where(place == 0, jnp.zeros_like(before), before)
-    after = jnp.where(place == lax.axis_size("col") - 1, jnp.zeros_like(after), after)
+    column = lax.axis_index("col")
+    odd = row_parity() > 0
+    mine, my_other = mine_ref[:, :lanes], mine_ref[:, lanes:]
+    theirs, their_other = sent_ref[:, :lanes], sent_ref[:, lanes:]
+    before = jnp.where(odd, theirs, my_other)
+    before = jnp.where(column == 0, jnp.zeros_like(before), before)
+    first = jnp.where(odd, their_other, mine)
+    second = jnp.where(odd, mine, their_other)
+    after = jnp.where(odd, my_other, theirs)
+    after = jnp.where(column == lax.axis_size("col") - 1, jnp.zeros_like(after), after)
     sum_ref[...] = jnp.zeros_like(sum_ref)
-    for place, value in zip(range(-1, 3), (before, mine_ref[:, :lanes], sent_ref[:, lanes:], after)):
+    for place, value in zip(range(-1, 3), (before, first, second, after)):
         start = place * tile - AMBIT
         low, high = max(0, start), min(width, start + extent)
         sum_ref[:, low:high] += dot(value, col_ref[:, low - start : high - start])
@@ -421,7 +461,7 @@
     )(mask, target)
     top = stepped(last, "row", 1)
     bottom = stepped(first, "row", -1)
-    other_goal = turned(goal, "col", 1)
+    other_goal = turned(goal, 1)
     middle, quads = call(
         partial(early_kernel, rows, lanes, early),
         (shape((2 * rows, width), f32), shape((early, 8, rows, lanes), bf16)),
@@ -432,7 +472,7 @@
         limit=50,
         us=4,
     )(mask, pupils, row_table, weights, row_pick, col_pick)
-    own, low, sending = call(
+    own, kept, sending = call(
         partial_kernel,
         (
             shape((2 * rows, tile + AMBIT), bf16),
@@ -441,7 +481,7 @@
         ),
         [smem, *vmem(5)],
     )(live, middle, top, bottom, row_table, col_table_t)
-    sent = turned(sending, "col", 1)
+    sent = turned(sending, 1)
     base, all_quads = call(
         partial(late_kernel, rows, lanes, early, kernels),
         (shape((2 * rows, 2 * lanes), f32), shape((kernels, 8, rows, lanes), bf16)),
@@ -468,10 +508,10 @@
         limit=36,
         us=15,
     )(
-        live, base, sent, low, target, other_goal, all_quads,
+        live, base, sent, kept, target, other_goal, all_quads,
         row_table, row_table_t, col_table, col_table_t,
     )
-    returned = turned(answers, "col", -1)
+    returned = turned(answers, -1)
     mixed, up, down = call(
         partial(returned_kernel, tile),
         (shape((2 * rows, width), bf16), shape((AMBIT, width), bf16), shape((AMBIT, width), bf16)),

time: 54.1 us -> 55.1 us (1.018)
  waiting for transfers between devices: 11.3 us -> 12.1 us
  starting transfers between devices: 28.4 us -> 29 us
    ppermute x4, starting transfers between devices: 11.8 us -> 14.9 us  [stepped(): return lax.ppermute(block, axis, pairs)]
    ppermute x3, starting transfers between devices: 16.5 us -> 14.2 us  [turned(): return lax.ppermute(block, ('row', 'col'), pairs)]
    ppermute x3, waiting for transfers between devices: 3.2 us -> 4.03 us  [turned(): return lax.ppermute(block, ('row', 'col'), pairs)]
  transfers between devices with their start and end apart: 7 -> 7, of which waited for: 4 -> 5; matrix products, arithmetic and copies ran while one was open for 0% -> 0% of each run, Pallas kernels for 18% -> 17%
where the time goes in v4:
time: 55.1 us; the launch traced here: 54.8 us
  starting transfers between devices  29 us (53%)
  Pallas kernels  13.4 us (24%)
  waiting for transfers between devices  12.1 us (22%)
    ppermute x4, starting transfers between devices, stepped(): return lax.ppermute(block, axis, pairs)  14.9 us
    ppermute x3, starting transfers between devices, turned(): return lax.ppermute(block, ('row', 'col'), pairs)  14.2 us
    ppermute x4, waiting for transfers between devices, stepped(): return lax.ppermute(block, axis, pairs)  8.11 us
    ppermute x3, waiting for transfers between devices, turned(): return lax.ppermute(block, ('row', 'col'), pairs)  4.03 us
    pallas_call x1, Pallas kernels, body(): call(partial(early_kernel, rows, lanes, early), (shape((2 * rows, width),...  3.57 us
    pallas_call x1, Pallas kernels, body(): call(partial(late_kernel, rows, lanes, early, kernels), (shape((2 * rows,...  3.33 us
    pallas_call x1, Pallas kernels, body(): pl.pallas_call(update_kernel, out_shape=(whole, rims), in_specs=[hbm, *vm...  1.57 us
    pallas_call x1, Pallas kernels, body(): call(edges_kernel, (edge, edge, shape((tile, tile), bf16)), [hbm, hbm], s...  1.44 us
  transfers between devices with their start and end apart: 7, of which 5 were waited for; matrix products, arithmetic and copies ran while one was open for 0% of the time, Pallas kernels for 17%

profile of v4, /device:TPU:11, one launch (start us, length us, event | category | flops | bytes accessed | tf_op | source)
XLA Modules:
  0.0 54.8 jit_solution(13617546527123322207)
XLA Ops:
  0.0 0.0 copy-start.2
  0.0 1.4 %shard_map.110 = (bf16[128,1024]{1,0:T(8,128)(2,1)S(1)}, bf16[128,1024]{1,0:T(8,128)(2,1)S(1)}, bf16[512,512]{1,0:T(8,128)(2,1)S(1)}) custom-call(f32[512,1024]{1,0:T(8,128)} %mask_ref.5, bf16[512,1024]{1,0:T(8,128)(2,1)} %goal_ref.1), custom_call_target="tpu_custom_call" | custom-call | flops 500000000 | bytes 1000000 | tf_op jit(solution)/shard_map/pallas_call | solution.py:455
  1.5 0.2 collective-permute-start.3
  1.7 5.1 %collective-permute-start = (bf16[128,1024]{1,0:T(8,128)(2,1)S(1)}, bf16[128,1024]{1,0:T(8,128)(2,1)S(1)}, u32[]{:S(2)}, u32[]{:S(2)}) collective-permute-start(bf16[128,1024]{1,0:T(8,128)(2,1)S(1)} %get-tuple-element.21), channel_id=1, source_target_pairs={{0,4},{4,8},{8,12},{12,16},{16,20},{20,24},{24,28},{1,5},{5,9},{9,... | collective-permute-start | bytes 786440 | tf_op jit(solution)/shard_map/ppermute | solution.py:30
  6.8 0.0 copy-start.3
  6.8 0.0 copy-start.6
  6.8 2.1 %collective-permute-start.1 = (bf16[128,1024]{1,0:T(8,128)(2,1)S(1)}, bf16[128,1024]{1,0:T(8,128)(2,1)S(1)}, u32[]{:S(2)}, u32[]{:S(2)}) collective-permute-start(bf16[128,1024]{1,0:T(8,128)(2,1)S(1)} %get-tuple-element.22), channel_id=1, source_target_pairs={{4,0},{8,4},{12,8},{16,12},{20,16},{24,20},{28,24},{5,1},{9,5},{13... | collective-permute-start | bytes 786440 | tf_op jit(solution)/shard_map/ppermute | solution.py:30
  8.9 0.0 copy-done.7
  8.9 0.0 copy-done.9
  8.9 0.0 copy-done.8
  8.9 0.0 copy-done.2
  8.9 3.6 %shard_map.109 = (f32[160,1024]{1,0:T(8,128)S(1)}, bf16[6,8,80,128]{3,2,1,0:T(8,128)(2,1)S(1)}) custom-call(f32[512,1024]{1,0:T(8,128)} %mask_ref.5, f32[2,12,144,144]{3,2,1,0:T(8,128)} %pupils_ref.3, bf16[160,768]{1,0:T(8,128)(2,1)S(1)} %copy-done.7, f32[12]{0:T(128)S(1)} %copy-done.2, bf16[160,144]{1,0:T(8,128)(2,1)S(1)} %copy-done.8, ...), custom_call_target="tpu_custom_call" | custom-call | flops 2000000000 | bytes 4000000 | tf_op jit(solution)/shard_map/pallas_call | solution.py:465
  12.5 0.0 collective-permute-done.top_ref
  12.5 3.0 %collective-permute-done.1.bottom_ref = bf16[128,1024]{1,0:T(8,128)(2,1)S(1)} collective-permute-done((bf16[128,1024]{1,0:T(8,128)(2,1)S(1)}, bf16[128,1024]{1,0:T(8,128)(2,1)S(1)}, u32[]{:S(2)}, u32[]{:S(2)}) %collective-permute-start.1) | collective-permute-done | bytes 262176 | tf_op jit(solution)/shard_map/ppermute | solution.py:30
  15.5 0.0 copy-done.3
  15.5 1.1 %shard_map.111 = (bf16[160,640]{1,0:T(8,128)(2,1)S(1)}, bf16[160,128]{1,0:T(8,128)(2,1)S(1)}, bf16[160,384]{1,0:T(8,128)(2,1)S(1)}) custom-call(s32[1,2]{1,0:T(1,128)S(1)} %copy-done.3, f32[160,1024]{1,0:T(8,128)S(1)} %get-tuple-element.20.mid_ref, bf16[128,1024]{1,0:T(8,128)(2,1)S(1)} %collective-permute-done.top_ref, ...), custom_call_target="tpu_custom_call" | custom-call | flops 500000000 | bytes 1000000 | tf_op jit(solution)/shard_map/pallas_call | solution.py:475
  16.6 0.5 collective-permute-start.2
  17.2 3.3 %shard_map.112 = (f32[160,256]{1,0:T(8,128)S(1)}, bf16[12,8,80,128]{3,2,1,0:T(8,128)(2,1)S(1)}) custom-call(f32[2,12,144,144]{3,2,1,0:T(8,128)} %pupils_ref.3, bf16[160,640]{1,0:T(8,128)(2,1)S(1)} %get-tuple-element.23.own_ref, bf16[768,256]{1,0:T(8,128)(2,1)S(1)} %copy-done.6, bf16[6,8,80,128]{3,2,1,0:T(8,128)(2,1)S(1)} %get-tuple-element.24.quads_ref, ...), custom_call_target="tpu_custom_call" | custom-call | flops 2000000000 | bytes 4000000 | tf_op jit(solution)/shard_map/pallas_call | solution.py:485
  20.5 0.3 collective-permute-done.2.sent_ref
  20.8 0.0 collective-permute-done.3.other_ref
  20.8 0.0 copy-done.5
  20.8 0.0 copy-start
  20.9 0.8 %shard_map.113.mine_ref = bf16[160,512]{1,0:T(8,128)(2,1)S(1)} custom-call(s32[1,2]{1,0:T(1,128)S(1)} %copy-done.3, f32[160,256]{1,0:T(8,128)S(1)} %get-tuple-element.25.base_ref, bf16[160,384]{1,0:T(8,128)(2,1)S(1)} %collective-permute-done.2.sent_ref, bf16[160,128]{1,0:T(8,128)(2,1)S(1)} %get-tuple-element.27.kept_ref, bf16[512,1024]{1,0:T(8,128)(2,1)S(1)} %copy-done.1, ...), custom_call_target="tpu_custom_call" | custom-call | flops 7500000256 | bytes 15000000 | tf_op jit(solution)/shard_map/pallas_call | solution.py:493
  21.6 13.4 %collective-permute-start.4 = (bf16[160,512]{1,0:T(8,128)(2,1)S(1)}, bf16[160,512]{1,0:T(8,128)(2,1)S(1)}, u32[]{:S(2)}, u32[]{:S(2)}) collective-permute-start(bf16[160,512]{1,0:T(8,128)(2,1)S(1)} %shard_map.113.mine_ref), channel_id=1, source_target_pairs={{0,3},{1,0},{2,1},{3,2},{4,5},{5,6},{6,7},{7,4},{8,11},{9,8},{10,9... | collective-permute-start | bytes 491528 | tf_op jit(solution)/shard_map/ppermute | solution.py:40
  35.1 3.7 %collective-permute-done.4.sent_ref = bf16[160,512]{1,0:T(8,128)(2,1)S(1)} collective-permute-done((bf16[160,512]{1,0:T(8,128)(2,1)S(1)}, bf16[160,512]{1,0:T(8,128)(2,1)S(1)}, u32[]{:S(2)}, u32[]{:S(2)}) %collective-permute-start.4) | collective-permute-done | bytes 163872 | tf_op jit(solution)/shard_map/ppermute | solution.py:40
  38.8 0.6 %shard_map.114 = (bf16[160,1024]{1,0:T(8,128)(2,1)S(1)}, bf16[128,1024]{1,0:T(8,128)(2,1)S(1)}, bf16[128,1024]{1,0:T(8,128)(2,1)S(1)}) custom-call(bf16[160,512]{1,0:T(8,128)(2,1)S(1)} %shard_map.113.mine_ref, bf16[160,512]{1,0:T(8,128)(2,1)S(1)} %collective-permute-done.4.sent_ref, bf16[768,160]{1,0:T(8,128)(2,1)S(1)} %copy-done.4, ...), custom_call_target="tpu_custom_call" | custom-call | flops 500000000 | bytes 1000000 | tf_op jit(solution)/shard_map/pallas_call | solution.py:515
  39.3 5.8 %collective-permute-start.5 = (bf16[128,1024]{1,0:T(8,128)(2,1)S(1)}, bf16[128,1024]{1,0:T(8,128)(2,1)S(1)}, u32[]{:S(2)}, u32[]{:S(2)}) collective-permute-start(bf16[128,1024]{1,0:T(8,128)(2,1)S(1)} %get-tuple-element.30), channel_id=1, source_target_pairs={{0,4},{4,8},{8,12},{12,16},{16,20},{20,24},{24,28},{1,5},{5,9},{9,... | collective-permute-start | bytes 786440 | tf_op jit(solution)/shard_map/ppermute | solution.py:30
  45.2 1.9 %collective-permute-start.6 = (bf16[128,1024]{1,0:T(8,128)(2,1)S(1)}, bf16[128,1024]{1,0:T(8,128)(2,1)S(1)}, u32[]{:S(2)}, u32[]{:S(2)}) collective-permute-start(bf16[128,1024]{1,0:T(8,128)(2,1)S(1)} %get-tuple-element.31), channel_id=1, source_target_pairs={{4,0},{8,4},{12,8},{16,12},{20,16},{24,20},{28,24},{5,1},{9,5},{13... | collective-permute-start | bytes 786440 | tf_op jit(solution)/shard_map/ppermute | solution.py:30
  47.1 1.6 %shard_map.115 = (f32[512,1024]{1,0:T(8,128)}, f32[256,1024]{1,0:T(8,128)S(1)}) custom-call(f32[512,1024]{1,0:T(8,128)S(1)} %copy-done, bf16[160,1024]{1,0:T(8,128)(2,1)S(1)} %get-tuple-element.32.mixed_ref, bf16[768,160]{1,0:T(8,128)(2,1)S(1)} %copy-done.4), custom_call_target="tpu_custom_call" | custom-call | flops 1000000000 | bytes 2000000 | tf_op jit(solution)/shard_map/pallas_call | solution.py:525
  48.7 1.7 %collective-permute-done.5.above_ref = bf16[128,1024]{1,0:T(8,128)(2,1)S(1)} collective-permute-done((bf16[128,1024]{1,0:T(8,128)(2,1)S(1)}, bf16[128,1024]{1,0:T(8,128)(2,1)S(1)}, u32[]{:S(2)}, u32[]{:S(2)}) %collective-permute-start.5) | collective-permute-done | bytes 262176 | tf_op jit(solution)/shard_map/ppermute | solution.py:30
  50.4 3.3 %collective-permute-done.6.below_ref = bf16[128,1024]{1,0:T(8,128)(2,1)S(1)} collective-permute-done((bf16[128,1024]{1,0:T(8,128)(2,1)S(1)}, bf16[128,1024]{1,0:T(8,128)(2,1)S(1)}, u32[]{:S(2)}, u32[]{:S(2)}) %collective-permute-start.6) | collective-permute-done | bytes 262176 | tf_op jit(solution)/shard_map/ppermute | solution.py:30
  53.8 1.0 %shard_map.116 = f32[512,1024]{1,0:T(8,128)} custom-call(bf16[128,1024]{1,0:T(8,128)(2,1)S(1)} %collective-permute-done.5.above_ref, bf16[128,1024]{1,0:T(8,128)(2,1)S(1)} %collective-permute-done.6.below_ref, f32[256,1024]{1,0:T(8,128)S(1)} %get-tuple-element.33.rims_ref, f32[512,1024]{1,0:T(8,128)} %get-tuple-element.34.base_ref), custom_call_target="tpu_custom_call", output_to_operand_aliasing={{}: (3, {})} | custom-call | tf_op jit(solution)/shard_map/pallas_call | solution.py:534
  (10 shorter events, 0.0 us)
Async XLA Ops:
  0.0 8.9 %copy-start.7 = (bf16[160,768]{1,0:T(8,128)(2,1)S(1)}, bf16[160,768]{1,0:T(8,128)(2,1)}, u32[]{:S(2)}) copy-start(bf16[160,768]{1,0:T(8,128)(2,1)} %constant.14.clone.table_ref.row_ref) | copy-start | bytes 737284
  0.0 8.9 %copy-start.9 = (bf16[144,256]{1,0:T(8,128)(2,1)S(1)}, bf16[144,256]{1,0:T(8,128)(2,1)}, u32[]{:S(2)}) copy-start(bf16[144,256]{1,0:T(8,128)(2,1)} %constant.13.clone.col_ref) | copy-start | bytes 221188
  0.0 8.9 %copy-start.8 = (bf16[160,144]{1,0:T(8,128)(2,1)S(1)}, bf16[160,144]{1,0:T(8,128)(2,1)}, u32[]{:S(2)}) copy-start(bf16[160,144]{1,0:T(8,128)(2,1)} %constant.12.clone.row_ref) | copy-start | bytes 138244
  0.0 8.9 %copy-start.2 = (f32[12]{0:T(128)S(1)}, f32[12]{0:T(128)}, u32[]{:S(2)}) copy-start(f32[12]{0:T(128)} %weights_ref.3) | copy-start | bytes 148
  1.5 19.4 %collective-permute-start.3 = (bf16[512,512]{1,0:T(8,128)(2,1)S(1)}, bf16[512,512]{1,0:T(8,128)(2,1)S(1)}, u32[]{:S(2)}, u32[]{:S(2)}) collective-permute-start(bf16[512,512]{1,0:T(8,128)(2,1)S(1)} %get-tuple-element.28), channel_id=1, source_target_pairs={{0,1},{1,2},{2,3},{3,0},{4,7},{5,4},{6,5},{7,6},{8,9},{9,10},{10,1... | collective-permute-start | bytes 1572872 | tf_op jit(solution)/shard_map/ppermute | solution.py:40
  1.7 10.8 %collective-permute-start = (bf16[128,1024]{1,0:T(8,128)(2,1)S(1)}, bf16[128,1024]{1,0:T(8,128)(2,1)S(1)}, u32[]{:S(2)}, u32[]{:S(2)}) collective-permute-start(bf16[128,1024]{1,0:T(8,128)(2,1)S(1)} %get-tuple-element.21), channel_id=1, source_target_pairs={{0,4},{4,8},{8,12},{12,16},{16,20},{20,24},{24,28},{1,5},{5,9},{9,... | collective-permute-start | bytes 786440 | tf_op jit(solution)/shard_map/ppermute | solution.py:30
  6.8 8.7 %copy-start.3 = (s32[1,2]{1,0:T(1,128)S(1)}, s32[1,2]{1,0:T(1,128)}, u32[]{:S(2)}) copy-start(s32[1,2]{1,0:T(1,128)} %live_ref.3) | copy-start | bytes 28
  6.8 8.7 %copy-start.6 = (bf16[768,256]{1,0:T(8,128)(2,1)S(1)}, bf16[768,256]{1,0:T(8,128)(2,1)}, u32[]{:S(2)}) copy-start(bf16[768,256]{1,0:T(8,128)(2,1)} %constant.17.clone.col_t_ref) | copy-start | bytes 1179652
  6.8 8.7 %collective-permute-start.1 = (bf16[128,1024]{1,0:T(8,128)(2,1)S(1)}, bf16[128,1024]{1,0:T(8,128)(2,1)S(1)}, u32[]{:S(2)}, u32[]{:S(2)}) collective-permute-start(bf16[128,1024]{1,0:T(8,128)(2,1)S(1)} %get-tuple-element.22), channel_id=1, source_target_pairs={{4,0},{8,4},{12,8},{16,12},{20,16},{24,20},{28,24},{5,1},{9,5},{13... | collective-permute-start | bytes 786440 | tf_op jit(solution)/shard_map/ppermute | solution.py:30
  16.6 4.2 %collective-permute-start.2 = (bf16[160,384]{1,0:T(8,128)(2,1)S(1)}, bf16[160,384]{1,0:T(8,128)(2,1)S(1)}, u32[]{:S(2)}, u32[]{:S(2)}) collective-permute-start(bf16[160,384]{1,0:T(8,128)(2,1)S(1)} %get-tuple-element.26), channel_id=1, source_target_pairs={{0,1},{1,2},{2,3},{3,0},{4,7},{5,4},{6,5},{7,6},{8,9},{9,10},{10,1... | collective-permute-start | bytes 368648 | tf_op jit(solution)/shard_map/ppermute | solution.py:40
  17.2 3.7 %copy-start.1 = (bf16[512,1024]{1,0:T(8,128)(2,1)S(1)}, bf16[512,1024]{1,0:T(8,128)(2,1)}, u32[]{:S(2)}) copy-start(bf16[512,1024]{1,0:T(8,128)(2,1)} %goal_ref.1) | copy-start | bytes 3145732
  17.2 3.7 %copy-start.4 = (bf16[768,160]{1,0:T(8,128)(2,1)S(1)}, bf16[768,160]{1,0:T(8,128)(2,1)}, u32[]{:S(2)}) copy-start(bf16[768,160]{1,0:T(8,128)(2,1)} %constant.15.clone.row_t_ref) | copy-start | bytes 737284
  17.2 3.7 %copy-start.5 = (bf16[256,768]{1,0:T(8,128)(2,1)S(1)}, bf16[256,768]{1,0:T(8,128)(2,1)}, u32[]{:S(2)}) copy-start(bf16[256,768]{1,0:T(8,128)(2,1)} %constant.16.clone.col_ref) | copy-start | bytes 1179652
  20.8 26.2 %copy-start = (f32[512,1024]{1,0:T(8,128)S(1)}, f32[512,1024]{1,0:T(8,128)}, u32[]{:S(2)}) copy-start(f32[512,1024]{1,0:T(8,128)} %mask_ref.5) | copy-start | bytes 6291460
  21.6 17.1 %collective-permute-start.4 = (bf16[160,512]{1,0:T(8,128)(2,1)S(1)}, bf16[160,512]{1,0:T(8,128)(2,1)S(1)}, u32[]{:S(2)}, u32[]{:S(2)}) collective-permute-start(bf16[160,512]{1,0:T(8,128)(2,1)S(1)} %shard_map.113.mine_ref), channel_id=1, source_target_pairs={{0,3},{1,0},{2,1},{3,2},{4,5},{5,6},{6,7},{7,4},{8,11},{9,8},{10,9... | collective-permute-start | bytes 491528 | tf_op jit(solution)/shard_map/ppermute | solution.py:40
  39.3 11.1 %collective-permute-start.5 = (bf16[128,1024]{1,0:T(8,128)(2,1)S(1)}, bf16[128,1024]{1,0:T(8,128)(2,1)S(1)}, u32[]{:S(2)}, u32[]{:S(2)}) collective-permute-start(bf16[128,1024]{1,0:T(8,128)(2,1)S(1)} %get-tuple-element.30), channel_id=1, source_target_pairs={{0,4},{4,8},{8,12},{12,16},{16,20},{20,24},{24,28},{1,5},{5,9},{9,... | collective-permute-start | bytes 786440 | tf_op jit(solution)/shard_map/ppermute | solution.py:30
  45.2 8.6 %collective-permute-start.6 = (bf16[128,1024]{1,0:T(8,128)(2,1)S(1)}, bf16[128,1024]{1,0:T(8,128)(2,1)S(1)}, u32[]{:S(2)}, u32[]{:S(2)}) collective-permute-start(bf16[128,1024]{1,0:T(8,128)(2,1)S(1)} %get-tuple-element.31), channel_id=1, source_target_pairs={{4,0},{8,4},{12,8},{16,12},{20,16},{24,20},{28,24},{5,1},{9,5},{13... | collective-permute-start | bytes 786440 | tf_op jit(solution)/shard_map/ppermute | solution.py:30

commit v5 on v3

--- a/solution.py
+++ b/solution.py
@@ -24,10 +24,17 @@
     return -(-value // unit) * unit
 
 
-def stepped(block, axis, step):
+def swapped(block, axis, offset):
     count = lax.axis_size(axis)
-    pairs = [(i, i + step) for i in range(count) if 0 <= i + step < count]
+    pairs = []
+    for low in range(offset, count - 1, 2):
+        pairs += [(low, low + 1), (low + 1, low)]
     return lax.ppermute(block, axis, pairs)
+
+
+def sides(reach):
+    odd = lax.rem(lax.axis_index("row"), 2)
+    return [pl.multiple_of(side * reach, AMBIT) for side in (1 - odd, odd)]
 
 
 def turned(block, axis, step):
@@ -97,18 +104,18 @@
             out_ref[k, 6 + part] = (pos_neg - neg_pos).astype(jnp.bfloat16)
 
 
-def edges_kernel(mask_ref, target_ref, first_ref, last_ref, goal_ref, stage_ref, sems):
+def edges_kernel(mask_ref, target_ref, near_ref, cross_ref, goal_ref, stage_ref, sems):
     tile = mask_ref.shape[0]
     whole = pltpu.make_async_copy(target_ref.at[:, tile:], goal_ref, sems.at[2])
     copies = []
-    for index, start in enumerate((0, tile - AMBIT)):
+    for index, start in enumerate(sides(tile - AMBIT)):
         copy = pltpu.make_async_copy(
             mask_ref.at[pl.ds(start, AMBIT)], stage_ref.at[index], sems.at[index]
         )
         copy.start()
         copies.append(copy)
     whole.start()
-    for index, out_ref in enumerate((first_ref, last_ref)):
+    for index, out_ref in enumerate((near_ref, cross_ref)):
         copies[index].wait()
         out_ref[...] = stage_ref[index].astype(jnp.bfloat16)
     whole.wait()
@@ -132,13 +139,14 @@
 
 
 def partial_kernel(
-    live_ref, mid_ref, top_ref, bottom_ref, table_ref, col_t_ref, own_ref, low_ref, sent_ref
+    live_ref, mid_ref, near_ref, cross_ref, table_ref, col_t_ref, own_ref, low_ref, sent_ref
 ):
     extent = table_ref.shape[1]
     width = mid_ref.shape[1]
     tile = extent - 2 * AMBIT
-    total = mid_ref[...] + dot(table_ref[:, :AMBIT], top_ref[...])
-    total = total + dot(table_ref[:, extent - AMBIT :], bottom_ref[...])
+    total = mid_ref[...]
+    for start, rim_ref in zip(sides(extent - AMBIT), (near_ref, cross_ref)):
+        total = total + dot(table_ref[:, pl.ds(start, AMBIT)], rim_ref[...])
     total = total.astype(jnp.bfloat16)
     own_ref[...] = total[:, : tile + AMBIT]
     low_ref[...] = total[:, :AMBIT]
@@ -341,7 +349,7 @@
     lax.fori_loop(0, 2, work, 0)
 
 
-def returned_kernel(tile, mine_ref, sent_ref, row_t_ref, col_ref, out_ref, up_ref, down_ref, sum_ref):
+def returned_kernel(tile, mine_ref, sent_ref, row_t_ref, col_ref, out_ref, near_ref, cross_ref, sum_ref):
     width = out_ref.shape[1]
     extent = row_t_ref.shape[0]
     lanes = mine_ref.shape[1] // 2
@@ -356,8 +364,8 @@
         sum_ref[:, low:high] += dot(value, col_ref[:, low - start : high - start])
     mixed = sum_ref[...].astype(jnp.bfloat16)
     out_ref[...] = mixed
-    up_ref[...] = dot(row_t_ref[:AMBIT], mixed).astype(jnp.bfloat16)
-    down_ref[...] = dot(row_t_ref[extent - AMBIT :], mixed).astype(jnp.bfloat16)
+    for start, rim_ref in zip(sides(extent - AMBIT), (near_ref, cross_ref)):
+        rim_ref[...] = dot(row_t_ref[pl.ds(start, AMBIT)], mixed).astype(jnp.bfloat16)
 
 
 def update_kernel(mask_ref, mixed_ref, row_t_ref, out_ref, rims_ref, stage_ref, sems):
@@ -376,14 +384,16 @@
     copy.wait()
 
 
-def rims_kernel(above_ref, below_ref, rims_ref, base_ref, out_ref, stage_ref, sems):
+def rims_kernel(near_ref, cross_ref, rims_ref, base_ref, out_ref, stage_ref, sems):
     tile = out_ref.shape[0]
     copies = []
-    for index, (rim_ref, start) in enumerate(((above_ref, 0), (below_ref, tile - AMBIT))):
-        where = pl.ds(index * AMBIT, AMBIT)
-        stage_ref[where] = rims_ref[where] - step_rate * rim_ref[...].astype(jnp.float32)
+    places = zip((cross_ref, near_ref), sides(AMBIT)[::-1], sides(tile - AMBIT)[::-1])
+    for index, (rim_ref, place, start) in enumerate(places):
+        stage_ref[index] = rims_ref[pl.ds(place, AMBIT)] - step_rate * rim_ref[...].astype(
+            jnp.float32
+        )
         copy = pltpu.make_async_copy(
-            stage_ref.at[where], out_ref.at[pl.ds(start, AMBIT)], sems.at[index]
+            stage_ref.at[index], out_ref.at[pl.ds(start, AMBIT)], sems.at[index]
         )
         copy.start()
         copies.append(copy)
@@ -412,16 +422,16 @@
     hbm = pl.BlockSpec(memory_space=pltpu.HBM)
     dma = pltpu.SemaphoreType.DMA
     edge = shape((AMBIT, width), bf16)
-    first, last, goal = call(
+    near, cross, goal = call(
         edges_kernel,
         (edge, edge, shape((tile, tile), bf16)),
         [hbm, hbm],
         scratch=[pltpu.VMEM((2, AMBIT, width), f32), dma((3,))],
         limit=52,
     )(mask, target)
-    top = stepped(last, "row", 1)
-    bottom = stepped(first, "row", -1)
     other_goal = turned(goal, "col", 1)
+    cross = swapped(cross, "row", 1)
+    near = swapped(near, "row", 0)
     middle, quads = call(
         partial(early_kernel, rows, lanes, early),
         (shape((2 * rows, width), f32), shape((early, 8, rows, lanes), bf16)),
@@ -440,7 +450,7 @@
             shape((2 * rows, AMBIT + 2 * lanes), bf16),
         ),
         [smem, *vmem(5)],
-    )(live, middle, top, bottom, row_table, col_table_t)
+    )(live, middle, near, cross, row_table, col_table_t)
     sent = turned(sending, "col", 1)
     base, all_quads = call(
         partial(late_kernel, rows, lanes, early, kernels),
@@ -472,14 +482,14 @@
         row_table, row_table_t, col_table, col_table_t,
     )
     returned = turned(answers, "col", -1)
-    mixed, up, down = call(
+    mixed, near, cross = call(
         partial(returned_kernel, tile),
         (shape((2 * rows, width), bf16), shape((AMBIT, width), bf16), shape((AMBIT, width), bf16)),
         vmem(4),
         scratch=[pltpu.VMEM((2 * rows, width), f32)],
     )(answers, returned, row_table_t, col_table)
-    from_above = stepped(down, "row", 1)
-    from_below = stepped(up, "row", -1)
+    cross = swapped(cross, "row", 1)
+    near = swapped(near, "row", 0)
     anywhere = pl.BlockSpec(memory_space=pl.ANY)
     whole, rims = shape((tile, width), f32), shape((2 * AMBIT, width), f32)
     updated, edges = pl.pallas_call(
@@ -496,10 +506,10 @@
         out_shape=whole,
         in_specs=[*vmem(3), anywhere],
         out_specs=anywhere,
-        scratch_shapes=[pltpu.VMEM((2 * AMBIT, width), f32), pltpu.SemaphoreType.DMA((2,))],
+        scratch_shapes=[pltpu.VMEM((2, AMBIT, width), f32), pltpu.SemaphoreType.DMA((2,))],
         input_output_aliases={3: 0},
         compiler_params=pltpu.CompilerParams(vmem_limit_bytes=8 * MIB),
-    )(from_above, from_below, edges, updated)
+    )(near, cross, edges, updated)
 
 
 def solution(mesh):

time: 54.1 us -> 53 us (0.980)
  the two profiles are of different devices: /device:TPU:11 before, /device:TPU:1 now
where the time goes in v5:
time: 53 us; the launch traced here: 52.8 us
  Pallas kernels  25.9 us (49%)
  waiting for transfers between devices  13.7 us (26%)
  starting transfers between devices  13 us (25%)
    pallas_call x1, Pallas kernels, body(): call(partial(core_kernel, rows, lanes), shape((2 * rows, 4 * lanes), bf16...  13.2 us
    ppermute x4, starting transfers between devices, swapped(): return lax.ppermute(block, axis, pairs)  9.46 us
    ppermute x4, waiting for transfers between devices, swapped(): return lax.ppermute(block, axis, pairs)  8.66 us
    ppermute x3, waiting for transfers between devices, turned(): lax.ppermute(block, axis, [(i, (i + step) % count) for i in range(count)])  5.05 us
    ppermute x3, starting transfers between devices, turned(): lax.ppermute(block, axis, [(i, (i + step) % count) for i in range(count)])  3.57 us
    pallas_call x1, Pallas kernels, body(): call(partial(early_kernel, rows, lanes, early), (shape((2 * rows, width),...  3.57 us
    pallas_call x1, Pallas kernels, body(): call(partial(late_kernel, rows, lanes, early, kernels), (shape((2 * rows,...  3.33 us
    pallas_call x1, Pallas kernels, body(): pl.pallas_call(update_kernel, out_shape=(whole, rims), in_specs=[hbm, *vm...  1.57 us
  transfers between devices with their start and end apart: 7, of which 4 were waited for; matrix products, arithmetic and copies ran while one was open for 0% of the time, Pallas kernels for 18%

profile of v5, /device:TPU:1, one launch (start us, length us, event | category | flops | bytes accessed | tf_op | source)
XLA Modules:
  0.0 52.8 jit_solution(4721905479008371277)
XLA Ops:
  0.0 0.0 copy-start.2
  0.0 1.4 %shard_map.110 = (bf16[128,1024]{1,0:T(8,128)(2,1)S(1)}, bf16[128,1024]{1,0:T(8,128)(2,1)S(1)}, bf16[512,512]{1,0:T(8,128)(2,1)S(1)}) custom-call(f32[512,1024]{1,0:T(8,128)} %mask_ref.5, bf16[512,1024]{1,0:T(8,128)(2,1)} %goal_ref.1), custom_call_target="tpu_custom_call" | custom-call | flops 500000000 | bytes 1000000 | tf_op jit(solution)/shard_map/pallas_call | solution.py:425
  1.5 2.2 %collective-permute-start.3 = (bf16[512,512]{1,0:T(8,128)(2,1)S(1)}, bf16[512,512]{1,0:T(8,128)(2,1)S(1)}, u32[]{:S(2)}, u32[]{:S(2)}) collective-permute-start(bf16[512,512]{1,0:T(8,128)(2,1)S(1)} %get-tuple-element.28), channel_id=1, source_target_pairs={{0,1},{1,2},{2,3},{3,0},{4,5},{5,6},{6,7},{7,4},{8,9},{9,10},{10,1... | collective-permute-start | bytes 1572872 | tf_op jit(solution)/shard_map/ppermute | solution.py:42
  3.6 1.0 %collective-permute-start = (bf16[128,1024]{1,0:T(8,128)(2,1)S(1)}, bf16[128,1024]{1,0:T(8,128)(2,1)S(1)}, u32[]{:S(2)}, u32[]{:S(2)}) collective-permute-start(bf16[128,1024]{1,0:T(8,128)(2,1)S(1)} %get-tuple-element.21), channel_id=1, source_target_pairs={{0,4},{4,0},{8,12},{12,8},{16,20},{20,16},{24,28},{28,24},{1,5},{5... | collective-permute-start | bytes 786440 | tf_op jit(solution)/shard_map/ppermute | solution.py:32
  4.6 3.1 %collective-permute-start.1 = (bf16[128,1024]{1,0:T(8,128)(2,1)S(1)}, bf16[128,1024]{1,0:T(8,128)(2,1)S(1)}, u32[]{:S(2)}, u32[]{:S(2)}) collective-permute-start(bf16[128,1024]{1,0:T(8,128)(2,1)S(1)} %get-tuple-element.22), channel_id=1, source_target_pairs={{4,8},{8,4},{12,16},{16,12},{20,24},{24,20},{5,9},{9,5},{13,17},{1... | collective-permute-start | bytes 786440 | tf_op jit(solution)/shard_map/ppermute | solution.py:32
  7.7 0.0 copy-done.7
  7.7 0.0 copy-done.9
  7.8 0.0 copy-done.8
  7.8 0.0 copy-done.2
  7.8 3.6 %shard_map.109 = (f32[160,1024]{1,0:T(8,128)S(1)}, bf16[6,8,80,128]{3,2,1,0:T(8,128)(2,1)S(1)}) custom-call(f32[512,1024]{1,0:T(8,128)} %mask_ref.5, f32[2,12,144,144]{3,2,1,0:T(8,128)} %pupils_ref.3, bf16[160,768]{1,0:T(8,128)(2,1)S(1)} %copy-done.7, f32[12]{0:T(128)S(1)} %copy-done.2, bf16[160,144]{1,0:T(8,128)(2,1)S(1)} %copy-done.8, ...), custom_call_target="tpu_custom_call" | custom-call | flops 2000000000 | bytes 4000000 | tf_op jit(solution)/shard_map/pallas_call | solution.py:435
  11.4 0.0 collective-permute-done.near_ref
  11.4 3.9 %collective-permute-done.1.cross_ref = bf16[128,1024]{1,0:T(8,128)(2,1)S(1)} collective-permute-done((bf16[128,1024]{1,0:T(8,128)(2,1)S(1)}, bf16[128,1024]{1,0:T(8,128)(2,1)S(1)}, u32[]{:S(2)}, u32[]{:S(2)}) %collective-permute-start.1) | collective-permute-done | bytes 262176 | tf_op jit(solution)/shard_map/ppermute | solution.py:32
  15.2 0.0 copy-done.3
  15.2 0.0 copy-done.6
  15.2 1.1 %shard_map.111 = (bf16[160,640]{1,0:T(8,128)(2,1)S(1)}, bf16[160,128]{1,0:T(8,128)(2,1)S(1)}, bf16[160,384]{1,0:T(8,128)(2,1)S(1)}) custom-call(s32[1,2]{1,0:T(1,128)S(1)} %copy-done.3, f32[160,1024]{1,0:T(8,128)S(1)} %get-tuple-element.20.mid_ref, bf16[128,1024]{1,0:T(8,128)(2,1)S(1)} %collective-permute-done.near_ref, ...), custom_call_target="tpu_custom_call" | custom-call | flops 500000000 | bytes 1000000 | tf_op jit(solution)/shard_map/pallas_call | solution.py:445
  16.4 1.3 %collective-permute-start.2 = (bf16[160,384]{1,0:T(8,128)(2,1)S(1)}, bf16[160,384]{1,0:T(8,128)(2,1)S(1)}, u32[]{:S(2)}, u32[]{:S(2)}) collective-permute-start(bf16[160,384]{1,0:T(8,128)(2,1)S(1)} %get-tuple-element.26), channel_id=1, source_target_pairs={{0,1},{1,2},{2,3},{3,0},{4,5},{5,6},{6,7},{7,4},{8,9},{9,10},{10,1... | collective-permute-start | bytes 368648 | tf_op jit(solution)/shard_map/ppermute | solution.py:42
  17.7 3.3 %shard_map.112 = (f32[160,256]{1,0:T(8,128)S(1)}, bf16[12,8,80,128]{3,2,1,0:T(8,128)(2,1)S(1)}) custom-call(f32[2,12,144,144]{3,2,1,0:T(8,128)} %pupils_ref.3, bf16[160,640]{1,0:T(8,128)(2,1)S(1)} %get-tuple-element.23.own_ref, bf16[768,256]{1,0:T(8,128)(2,1)S(1)} %copy-done.6, bf16[6,8,80,128]{3,2,1,0:T(8,128)(2,1)S(1)} %get-tuple-element.24.quads_ref, ...), custom_call_target="tpu_custom_call" | custom-call | flops 2000000000 | bytes 4000000 | tf_op jit(solution)/shard_map/pallas_call | solution.py:455
  21.0 0.9 %collective-permute-done.2.sent_ref = bf16[160,384]{1,0:T(8,128)(2,1)S(1)} collective-permute-done((bf16[160,384]{1,0:T(8,128)(2,1)S(1)}, bf16[160,384]{1,0:T(8,128)(2,1)S(1)}, u32[]{:S(2)}, u32[]{:S(2)}) %collective-permute-start.2) | collective-permute-done | bytes 122912 | tf_op jit(solution)/shard_map/ppermute | solution.py:42
  21.9 0.0 collective-permute-done.3.other_ref
  21.9 0.0 copy-done.1
  22.0 0.0 copy-start
  22.0 13.2 %shard_map.113.mine_ref = bf16[160,512]{1,0:T(8,128)(2,1)S(1)} custom-call(s32[1,2]{1,0:T(1,128)S(1)} %copy-done.3, f32[160,256]{1,0:T(8,128)S(1)} %get-tuple-element.25.base_ref, bf16[160,384]{1,0:T(8,128)(2,1)S(1)} %collective-permute-done.2.sent_ref, bf16[160,128]{1,0:T(8,128)(2,1)S(1)} %get-tuple-element.27.low_ref, bf16[512,1024]{1,0:T(8,128)(2,1)S(1)} %copy-done.1, ...), custom_call_target="tpu_custom_call" | custom-call | flops 7500000256 | bytes 15000000 | tf_op jit(solution)/shard_map/pallas_call | solution.py:463
  35.2 0.1 collective-permute-start.4
  35.3 4.2 %collective-permute-done.4.sent_ref = bf16[160,512]{1,0:T(8,128)(2,1)S(1)} collective-permute-done((bf16[160,512]{1,0:T(8,128)(2,1)S(1)}, bf16[160,512]{1,0:T(8,128)(2,1)S(1)}, u32[]{:S(2)}, u32[]{:S(2)}) %collective-permute-start.4) | collective-permute-done | bytes 163872 | tf_op jit(solution)/shard_map/ppermute | solution.py:42
  39.4 0.6 %shard_map.114 = (bf16[160,1024]{1,0:T(8,128)(2,1)S(1)}, bf16[128,1024]{1,0:T(8,128)(2,1)S(1)}, bf16[128,1024]{1,0:T(8,128)(2,1)S(1)}) custom-call(bf16[160,512]{1,0:T(8,128)(2,1)S(1)} %shard_map.113.mine_ref, bf16[160,512]{1,0:T(8,128)(2,1)S(1)} %collective-permute-done.4.sent_ref, bf16[768,160]{1,0:T(8,128)(2,1)S(1)} %copy-done.4, ...), custom_call_target="tpu_custom_call" | custom-call | flops 500000000 | bytes 1000000 | tf_op jit(solution)/shard_map/pallas_call | solution.py:485
  40.0 0.1 collective-permute-start.5
  40.1 5.3 %collective-permute-start.6 = (bf16[128,1024]{1,0:T(8,128)(2,1)S(1)}, bf16[128,1024]{1,0:T(8,128)(2,1)S(1)}, u32[]{:S(2)}, u32[]{:S(2)}) collective-permute-start(bf16[128,1024]{1,0:T(8,128)(2,1)S(1)} %get-tuple-element.31), channel_id=1, source_target_pairs={{4,8},{8,4},{12,16},{16,12},{20,24},{24,20},{5,9},{9,5},{13,17},{1... | collective-permute-start | bytes 786440 | tf_op jit(solution)/shard_map/ppermute | solution.py:32
  45.4 0.0 copy-done
  45.4 1.6 %shard_map.115 = (f32[512,1024]{1,0:T(8,128)}, f32[256,1024]{1,0:T(8,128)S(1)}) custom-call(f32[512,1024]{1,0:T(8,128)S(1)} %copy-done, bf16[160,1024]{1,0:T(8,128)(2,1)S(1)} %get-tuple-element.32.mixed_ref, bf16[768,160]{1,0:T(8,128)(2,1)S(1)} %copy-done.4), custom_call_target="tpu_custom_call" | custom-call | flops 1000000000 | bytes 2000000 | tf_op jit(solution)/shard_map/pallas_call | solution.py:495
  47.0 0.0 collective-permute-done.5.near_ref
  47.0 4.8 %collective-permute-done.6.cross_ref = bf16[128,1024]{1,0:T(8,128)(2,1)S(1)} collective-permute-done((bf16[128,1024]{1,0:T(8,128)(2,1)S(1)}, bf16[128,1024]{1,0:T(8,128)(2,1)S(1)}, u32[]{:S(2)}, u32[]{:S(2)}) %collective-permute-start.6) | collective-permute-done | bytes 262176 | tf_op jit(solution)/shard_map/ppermute | solution.py:32
  51.8 1.0 %shard_map.116 = f32[512,1024]{1,0:T(8,128)} custom-call(bf16[128,1024]{1,0:T(8,128)(2,1)S(1)} %collective-permute-done.5.near_ref, bf16[128,1024]{1,0:T(8,128)(2,1)S(1)} %collective-permute-done.6.cross_ref, f32[256,1024]{1,0:T(8,128)S(1)} %get-tuple-element.33.rims_ref, f32[512,1024]{1,0:T(8,128)} %get-tuple-element.34.base_ref), custom_call_target="tpu_custom_call", output_to_operand_aliasing={{}: (3, {})} | custom-call | tf_op jit(solution)/shard_map/pallas_call | solution.py:504
  (10 shorter events, 0.0 us)
Async XLA Ops:
  0.0 7.7 %copy-start.7 = (bf16[160,768]{1,0:T(8,128)(2,1)S(1)}, bf16[160,768]{1,0:T(8,128)(2,1)}, u32[]{:S(2)}) copy-start(bf16[160,768]{1,0:T(8,128)(2,1)} %constant.14.clone.table_ref.row_ref) | copy-start | bytes 737284
  0.0 7.7 %copy-start.9 = (bf16[144,256]{1,0:T(8,128)(2,1)S(1)}, bf16[144,256]{1,0:T(8,128)(2,1)}, u32[]{:S(2)}) copy-start(bf16[144,256]{1,0:T(8,128)(2,1)} %constant.13.clone.col_ref) | copy-start | bytes 221188
  0.0 7.8 %copy-start.8 = (bf16[160,144]{1,0:T(8,128)(2,1)S(1)}, bf16[160,144]{1,0:T(8,128)(2,1)}, u32[]{:S(2)}) copy-start(bf16[160,144]{1,0:T(8,128)(2,1)} %constant.12.clone.row_ref) | copy-start | bytes 138244
  0.0 7.8 %copy-start.2 = (f32[12]{0:T(128)S(1)}, f32[12]{0:T(128)}, u32[]{:S(2)}) copy-start(f32[12]{0:T(128)} %weights_ref.3) | copy-start | bytes 148
  1.5 20.5 %collective-permute-start.3 = (bf16[512,512]{1,0:T(8,128)(2,1)S(1)}, bf16[512,512]{1,0:T(8,128)(2,1)S(1)}, u32[]{:S(2)}, u32[]{:S(2)}) collective-permute-start(bf16[512,512]{1,0:T(8,128)(2,1)S(1)} %get-tuple-element.28), channel_id=1, source_target_pairs={{0,1},{1,2},{2,3},{3,0},{4,5},{5,6},{6,7},{7,4},{8,9},{9,10},{10,1... | collective-permute-start | bytes 1572872 | tf_op jit(solution)/shard_map/ppermute | solution.py:42
  3.6 7.7 %collective-permute-start = (bf16[128,1024]{1,0:T(8,128)(2,1)S(1)}, bf16[128,1024]{1,0:T(8,128)(2,1)S(1)}, u32[]{:S(2)}, u32[]{:S(2)}) collective-permute-start(bf16[128,1024]{1,0:T(8,128)(2,1)S(1)} %get-tuple-element.21), channel_id=1, source_target_pairs={{0,4},{4,0},{8,12},{12,8},{16,20},{20,16},{24,28},{28,24},{1,5},{5... | collective-permute-start | bytes 786440 | tf_op jit(solution)/shard_map/ppermute | solution.py:32
  4.6 10.6 %copy-start.3 = (s32[1,2]{1,0:T(1,128)S(1)}, s32[1,2]{1,0:T(1,128)}, u32[]{:S(2)}) copy-start(s32[1,2]{1,0:T(1,128)} %live_ref.3) | copy-start | bytes 28
  4.6 10.6 %copy-start.6 = (bf16[768,256]{1,0:T(8,128)(2,1)S(1)}, bf16[768,256]{1,0:T(8,128)(2,1)}, u32[]{:S(2)}) copy-start(bf16[768,256]{1,0:T(8,128)(2,1)} %constant.17.clone.col_t_ref) | copy-start | bytes 1179652
  4.6 10.6 %collective-permute-start.1 = (bf16[128,1024]{1,0:T(8,128)(2,1)S(1)}, bf16[128,1024]{1,0:T(8,128)(2,1)S(1)}, u32[]{:S(2)}, u32[]{:S(2)}) collective-permute-start(bf16[128,1024]{1,0:T(8,128)(2,1)S(1)} %get-tuple-element.22), channel_id=1, source_target_pairs={{4,8},{8,4},{12,16},{16,12},{20,24},{24,20},{5,9},{9,5},{13,17},{1... | collective-permute-start | bytes 786440 | tf_op jit(solution)/shard_map/ppermute | solution.py:32
  16.4 5.6 %collective-permute-start.2 = (bf16[160,384]{1,0:T(8,128)(2,1)S(1)}, bf16[160,384]{1,0:T(8,128)(2,1)S(1)}, u32[]{:S(2)}, u32[]{:S(2)}) collective-permute-start(bf16[160,384]{1,0:T(8,128)(2,1)S(1)} %get-tuple-element.26), channel_id=1, source_target_pairs={{0,1},{1,2},{2,3},{3,0},{4,5},{5,6},{6,7},{7,4},{8,9},{9,10},{10,1... | collective-permute-start | bytes 368648 | tf_op jit(solution)/shard_map/ppermute | solution.py:42
  17.7 4.2 %copy-start.1 = (bf16[512,1024]{1,0:T(8,128)(2,1)S(1)}, bf16[512,1024]{1,0:T(8,128)(2,1)}, u32[]{:S(2)}) copy-start(bf16[512,1024]{1,0:T(8,128)(2,1)} %goal_ref.1) | copy-start | bytes 3145732
  17.7 4.2 %copy-start.4 = (bf16[768,160]{1,0:T(8,128)(2,1)S(1)}, bf16[768,160]{1,0:T(8,128)(2,1)}, u32[]{:S(2)}) copy-start(bf16[768,160]{1,0:T(8,128)(2,1)} %constant.15.clone.row_t_ref) | copy-start | bytes 737284
  17.7 4.2 %copy-start.5 = (bf16[256,768]{1,0:T(8,128)(2,1)S(1)}, bf16[256,768]{1,0:T(8,128)(2,1)}, u32[]{:S(2)}) copy-start(bf16[256,768]{1,0:T(8,128)(2,1)} %constant.16.clone.col_ref) | copy-start | bytes 1179652
  22.0 23.4 %copy-start = (f32[512,1024]{1,0:T(8,128)S(1)}, f32[512,1024]{1,0:T(8,128)}, u32[]{:S(2)}) copy-start(f32[512,1024]{1,0:T(8,128)} %mask_ref.5) | copy-start | bytes 6291460
  35.2 4.2 %collective-permute-start.4 = (bf16[160,512]{1,0:T(8,128)(2,1)S(1)}, bf16[160,512]{1,0:T(8,128)(2,1)S(1)}, u32[]{:S(2)}, u32[]{:S(2)}) collective-permute-start(bf16[160,512]{1,0:T(8,128)(2,1)S(1)} %shard_map.113.mine_ref), channel_id=1, source_target_pairs={{0,3},{1,0},{2,1},{3,2},{4,7},{5,4},{6,5},{7,6},{8,11},{9,8},{10,9... | collective-permute-start | bytes 491528 | tf_op jit(solution)/shard_map/ppermute | solution.py:42
  40.0 7.0 %collective-permute-start.5 = (bf16[128,1024]{1,0:T(8,128)(2,1)S(1)}, bf16[128,1024]{1,0:T(8,128)(2,1)S(1)}, u32[]{:S(2)}, u32[]{:S(2)}) collective-permute-start(bf16[128,1024]{1,0:T(8,128)(2,1)S(1)} %get-tuple-element.30), channel_id=1, source_target_pairs={{0,4},{4,0},{8,12},{12,8},{16,20},{20,16},{24,28},{28,24},{1,5},{5... | collective-permute-start | bytes 786440 | tf_op jit(solution)/shard_map/ppermute | solution.py:32
  40.1 11.7 %collective-permute-start.6 = (bf16[128,1024]{1,0:T(8,128)(2,1)S(1)}, bf16[128,1024]{1,0:T(8,128)(2,1)S(1)}, u32[]{:S(2)}, u32[]{:S(2)}) collective-permute-start(bf16[128,1024]{1,0:T(8,128)(2,1)S(1)} %get-tuple-element.31), channel_id=1, source_target_pairs={{4,8},{8,4},{12,16},{16,12},{20,24},{24,20},{5,9},{9,5},{13,17},{1... | collective-permute-start | bytes 786440 | tf_op jit(solution)/shard_map/ppermute | solution.py:32

commit v6 on v5

--- a/solution.py
+++ b/solution.py
@@ -123,19 +123,20 @@
 
 def early_kernel(
     rows, lanes, count, mask_ref, pupils_ref, table_ref, weights_ref, row_ref, col_ref,
-    mid_ref, out_ref, mask_stage, pupil_stage, sems,
+    mid_ref, out_ref, rest_ref, pupil_stage, sems,
 ):
     tile = mask_ref.shape[0]
-    mask_copy = pltpu.make_async_copy(mask_ref, mask_stage, sems.at[0])
-    mask_copy.start()
-    pupil_copy = pltpu.make_async_copy(pupils_ref.at[:, pl.ds(0, count)], pupil_stage, sems.at[1])
+    pupil_copy = pltpu.make_async_copy(pupils_ref.at[:, pl.ds(0, count)], pupil_stage, sems.at[0])
     pupil_copy.start()
-    mask_copy.wait()
+    rest = pupils_ref.shape[1] - count
+    rest_copy = pltpu.make_async_copy(pupils_ref.at[:, pl.ds(count, rest)], rest_ref, sems.at[1])
+    rest_copy.start()
     mid_ref[...] = dot(
-        table_ref[:, AMBIT : AMBIT + tile], mask_stage[...].astype(jnp.bfloat16)
+        table_ref[:, AMBIT : AMBIT + tile], mask_ref[...].astype(jnp.bfloat16)
     )
     pupil_copy.wait()
     pupil_steps(rows, lanes, 0, count, pupil_stage, weights_ref, row_ref, col_ref, out_ref)
+    rest_copy.wait()
 
 
 def partial_kernel(
@@ -162,14 +163,21 @@
 
 def late_kernel(
     rows, lanes, first, last, pupils_ref, own_ref, col_t_ref, quads_ref, weights_ref, row_ref, col_ref,
-    base_ref, out_ref, pupil_stage, sem,
+    base_ref, out_ref,
 ):
-    copy = pltpu.make_async_copy(pupils_ref.at[:, pl.ds(first, last - first)], pupil_stage, sem)
-    copy.start()
     out_ref[:first] = quads_ref[...]
     base_ref[...] = dot(own_ref[...], col_t_ref[AMBIT:])
-    copy.wait()
-    pupil_steps(rows, lanes, first, last, pupil_stage, weights_ref, row_ref, col_ref, out_ref)
+    pupil_steps(rows, lanes, first, last, pupils_ref, weights_ref, row_ref, col_ref, out_ref)
+
+
+def in_groups(count, group, run):
+    def one(index, carry):
+        run(index * group, False)
+        return carry
+
+    if count > group:
+        lax.fori_loop(0, count // group - 1, one, 0)
+    run(count - group, True)
 
 
 def core_kernel(
@@ -266,40 +274,32 @@
                     total_ref[:, where] += energy
 
             section(0, 0)
+            section(1, 1)
             total_ref[...] = jnp.zeros_like(total_ref)
 
-            def forward(i, carry):
-                k = 2 * i
-                field((k,), (0,))
-                section(k + 1, 1)
-                field((k + 1,), (1,))
-                section(jnp.minimum(k + 2, kernels - 1), 0)
-                return carry
-
-            lax.fori_loop(0, kernels // 2, forward, 0)
-
-            def slopes(ref):
+            def forward(first, last_group):
+                for step in range(0, 4, 2):
+                    bufs, nexts = (0, 1), (2, 3)
+                    if step:
+                        bufs, nexts = nexts, bufs
+                    k = first + step
+                    more = step == 0 or not last_group
+                    field((k, k + 1), bufs)
+                    if more:
+                        section(k + 2, nexts[0])
+                        section(k + 3, nexts[1])
+
+            in_groups(kernels, 4, forward)
+
+            def back(ks, bufs):
                 for where in halves:
-                    level = jnp.tanh(total_ref[:, where] - 0.5 * steepness * threshold_level)
-                    excess = 0.5 * level + 0.5 - ref[:, where].astype(jnp.float32)
-                    slope_ref[:, where] = (excess * (1.0 - level * level)).astype(jnp.bfloat16)
-
-            @pl.when(item == 0)
-            def _():
-                slopes(goal_ref)
-
-            @pl.when(item > 0)
-            def _():
-                slopes(other_ref)
-
-            def back(k, buf):
-                for where in halves:
-                    for part in range(2):
-                        cotangent = slope_ref[:, where] * field_ref[k, part, :, where]
-                        place = slice(part * 2 * rows, (part + 1) * 2 * rows)
-                        back_ref[buf, place, where] = dot(row_ref[:, inner], cotangent).astype(
-                            jnp.bfloat16
-                        )
+                    for k, buf in zip(ks, bufs):
+                        for part in range(2):
+                            cotangent = slope_ref[:, where] * field_ref[k, part, :, where]
+                            place = slice(part * 2 * rows, (part + 1) * 2 * rows)
+                            back_ref[buf, place, where] = dot(
+                                row_ref[:, inner], cotangent
+                            ).astype(jnp.bfloat16)
 
             def adjoint(k, buf):
                 wave = dot(back_ref[buf], col_t_ref[inner])
@@ -317,17 +317,34 @@
                 ans_ref[3] += mr * ui - mi * ur - pr * vr - pi * vi
 
             ans_ref[...] = jnp.zeros_like(ans_ref)
-            back(0, 0)
-
-            def backward(i, carry):
-                k = 2 * i
-                adjoint(k, 0)
-                back(k + 1, 1)
-                adjoint(k + 1, 1)
-                back(jnp.minimum(k + 2, kernels - 1), 0)
-                return carry
-
-            lax.fori_loop(0, kernels // 2, backward, 0)
+
+            def slopes(ref):
+                for where in halves:
+                    level = jnp.tanh(total_ref[:, where] - 0.5 * steepness * threshold_level)
+                    excess = 0.5 * level + 0.5 - ref[:, where].astype(jnp.float32)
+                    slope_ref[:, where] = (excess * (1.0 - level * level)).astype(jnp.bfloat16)
+                back((0, 1), (0, 1))
+
+            @pl.when(item == 0)
+            def _():
+                slopes(goal_ref)
+
+            @pl.when(item > 0)
+            def _():
+                slopes(other_ref)
+
+            def backward(first, last_group):
+                for step in range(0, 4, 2):
+                    bufs, nexts = (0, 1), (2, 3)
+                    if step:
+                        bufs, nexts = nexts, bufs
+                    k = first + step
+                    adjoint(k, bufs[0])
+                    adjoint(k + 1, bufs[1])
+                    if step == 0 or not last_group:
+                        back((k + 2, k + 3), nexts)
+
+            in_groups(kernels, 4, backward)
 
             def answer(first):
                 left, right = slice(first, first + lanes), slice(first + lanes, first + 2 * lanes)
@@ -368,16 +385,13 @@
         rim_ref[...] = dot(row_t_ref[pl.ds(start, AMBIT)], mixed).astype(jnp.bfloat16)
 
 
-def update_kernel(mask_ref, mixed_ref, row_t_ref, out_ref, rims_ref, stage_ref, sems):
+def update_kernel(mask_ref, mixed_ref, row_t_ref, out_ref, rims_ref, stage_ref, sem):
     tile = mask_ref.shape[0]
-    copy = pltpu.make_async_copy(mask_ref, stage_ref, sems.at[0])
-    copy.start()
-    copy.wait()
-    stage_ref[...] = stage_ref[...] - step_rate * dot(
+    stage_ref[...] = mask_ref[...] - step_rate * dot(
         row_t_ref[AMBIT : AMBIT + tile], mixed_ref[...]
     )
     inner = pl.ds(AMBIT, tile - 2 * AMBIT)
-    copy = pltpu.make_async_copy(stage_ref.at[inner], out_ref.at[inner], sems.at[1])
+    copy = pltpu.make_async_copy(stage_ref.at[inner], out_ref.at[inner], sem)
     copy.start()
     rims_ref[:AMBIT] = stage_ref[:AMBIT]
     rims_ref[AMBIT:] = stage_ref[tile - AMBIT :]
@@ -432,14 +446,16 @@
     other_goal = turned(goal, "col", 1)
     cross = swapped(cross, "row", 1)
     near = swapped(near, "row", 0)
-    middle, quads = call(
+    middle, quads, rest = call(
         partial(early_kernel, rows, lanes, early),
-        (shape((2 * rows, width), f32), shape((early, 8, rows, lanes), bf16)),
-        [hbm, hbm, *vmem(1), smem, *vmem(2)],
-        scratch=[
-            pltpu.VMEM((tile, width), f32), pltpu.VMEM((2, early, size, size), f32), dma((2,)),
-        ],
-        limit=50,
+        (
+            shape((2 * rows, width), f32),
+            shape((early, 8, rows, lanes), bf16),
+            shape((2, kernels - early, size, size), f32),
+        ),
+        [*vmem(1), hbm, *vmem(1), smem, *vmem(2)],
+        scratch=[pltpu.VMEM((2, early, size, size), f32), dma((2,))],
+        limit=48,
         us=4,
     )(mask, pupils, row_table, weights, row_pick, col_pick)
     own, low, sending = call(
@@ -455,23 +471,22 @@
     base, all_quads = call(
         partial(late_kernel, rows, lanes, early, kernels),
         (shape((2 * rows, 2 * lanes), f32), shape((kernels, 8, rows, lanes), bf16)),
-        [hbm, *vmem(3), smem, *vmem(2)],
-        scratch=[pltpu.VMEM((2, kernels - early, size, size), f32), dma],
-        limit=48,
+        [*vmem(4), smem, *vmem(2)],
+        limit=16,
         us=4,
-    )(pupils, own, col_table_t, quads, weights, row_pick, col_pick)
+    )(rest, own, col_table_t, quads, weights, row_pick, col_pick)
     answers = call(
         partial(core_kernel, rows, lanes),
         shape((2 * rows, 4 * lanes), bf16),
         [smem, *vmem(10)],
         scratch=[
             pltpu.VMEM((2, 2 * rows, 2 * lanes), f32),
-            pltpu.VMEM((2, 4 * rows, 2 * lanes), bf16),
-            pltpu.VMEM((2, 4 * rows, tile), bf16),
+            pltpu.VMEM((4, 4 * rows, 2 * lanes), bf16),
+            pltpu.VMEM((4, 4 * rows, tile), bf16),
             pltpu.VMEM((kernels, 2, tile, tile), bf16),
             pltpu.VMEM((tile, tile), f32),
             pltpu.VMEM((tile, tile), bf16),
-            pltpu.VMEM((2, 4 * rows, tile), bf16),
+            pltpu.VMEM((4, 4 * rows, tile), bf16),
             pltpu.VMEM((4, rows, lanes), f32),
             pltpu.VMEM((4, rows, lanes), f32),
         ],
@@ -495,9 +510,9 @@
     updated, edges = pl.pallas_call(
         update_kernel,
         out_shape=(whole, rims),
-        in_specs=[hbm, *vmem(2)],
+        in_specs=vmem(3),
         out_specs=(anywhere, *vmem(1)),
-        scratch_shapes=[pltpu.VMEM((tile, width), f32), dma((2,))],
+        scratch_shapes=[pltpu.VMEM((tile, width), f32), dma],
         cost_estimate=pl.CostEstimate(flops=10**9, bytes_accessed=2 * 10**6, transcendentals=0),
         compiler_params=pltpu.CompilerParams(vmem_limit_bytes=16 * MIB),
     )(mask, mixed, row_table_t)

time: 53 us -> 51.1 us (0.964)
  Pallas kernels: 25.9 us -> 21.8 us
  waiting for transfers between devices: 13.7 us -> 15.9 us
    pallas_call x1, Pallas kernels: 13.2 us -> 11.3 us  [body(): call(partial(core_kernel, rows, lanes), shape((2 * rows, 4 * lanes), bf16...]
    pallas_call x1, Pallas kernels: 3.33 us -> 1.77 us  [body(): call(partial(late_kernel, rows, lanes, early, kernels), (shape((2 * rows,...]
    ppermute x3, waiting for transfers between devices: 5.05 us -> 6.61 us  [turned(): lax.ppermute(block, axis, [(i, (i + step) % count) for i in range(count)])]
    ppermute x4, waiting for transfers between devices: 8.66 us -> 9.34 us  [swapped(): return lax.ppermute(block, axis, pairs)]
    pallas_call x1, Pallas kernels: 3.57 us -> 3.03 us  [body(): call(partial(early_kernel, rows, lanes, early), (shape((2 * rows, width),...]
  transfers between devices with their start and end apart: 7 -> 7, of which waited for: 4 -> 4; matrix products, arithmetic and copies ran while one was open for 0% -> 0% of each run, Pallas kernels for 18% -> 14%
where the time goes in v6:
time: 51.1 us; the launch traced here: 51 us
  Pallas kernels  21.8 us (43%)
  waiting for transfers between devices  15.9 us (31%)
  starting transfers between devices  13 us (25%)
    pallas_call x1, Pallas kernels, body(): call(partial(core_kernel, rows, lanes), shape((2 * rows, 4 * lanes), bf16...  11.3 us
    ppermute x4, starting transfers between devices, swapped(): return lax.ppermute(block, axis, pairs)  9.45 us
    ppermute x4, waiting for transfers between devices, swapped(): return lax.ppermute(block, axis, pairs)  9.34 us
    ppermute x3, waiting for transfers between devices, turned(): lax.ppermute(block, axis, [(i, (i + step) % count) for i in range(count)])  6.61 us
    ppermute x3, starting transfers between devices, turned(): lax.ppermute(block, axis, [(i, (i + step) % count) for i in range(count)])  3.58 us
    pallas_call x1, Pallas kernels, body(): call(partial(early_kernel, rows, lanes, early), (shape((2 * rows, width),...  3.03 us
    pallas_call x1, Pallas kernels, body(): call(partial(late_kernel, rows, lanes, early, kernels), (shape((2 * rows,...  1.77 us
    pallas_call x1, Pallas kernels, body(): call(edges_kernel, (edge, edge, shape((tile, tile), bf16)), [hbm, hbm], s...  1.55 us
  transfers between devices with their start and end apart: 7, of which 4 were waited for; matrix products, arithmetic and copies ran while one was open for 0% of the time, Pallas kernels for 14%

profile of v6, /device:TPU:1, one launch (start us, length us, event | category | flops | bytes accessed | tf_op | source)
XLA Modules:
  0.0 51.0 jit_solution(215000372008415436)
XLA Ops:
  0.0 0.0 copy-start
  0.0 0.0 copy-start.2
  0.0 1.5 %shard_map.110 = (bf16[128,1024]{1,0:T(8,128)(2,1)S(1)}, bf16[128,1024]{1,0:T(8,128)(2,1)S(1)}, bf16[512,512]{1,0:T(8,128)(2,1)S(1)}) custom-call(f32[512,1024]{1,0:T(8,128)} %mask_ref.5, bf16[512,1024]{1,0:T(8,128)(2,1)} %goal_ref.1), custom_call_target="tpu_custom_call" | custom-call | flops 500000000 | bytes 1000000 | tf_op jit(solution)/shard_map/pallas_call | solution.py:439
  1.6 2.2 %collective-permute-start.3 = (bf16[512,512]{1,0:T(8,128)(2,1)S(1)}, bf16[512,512]{1,0:T(8,128)(2,1)S(1)}, u32[]{:S(2)}, u32[]{:S(2)}) collective-permute-start(bf16[512,512]{1,0:T(8,128)(2,1)S(1)} %get-tuple-element.30), channel_id=1, source_target_pairs={{0,1},{1,2},{2,3},{3,0},{4,5},{5,6},{6,7},{7,4},{8,9},{9,10},{10,1... | collective-permute-start | bytes 1572872 | tf_op jit(solution)/shard_map/ppermute | solution.py:42
  3.8 1.0 %collective-permute-start = (bf16[128,1024]{1,0:T(8,128)(2,1)S(1)}, bf16[128,1024]{1,0:T(8,128)(2,1)S(1)}, u32[]{:S(2)}, u32[]{:S(2)}) collective-permute-start(bf16[128,1024]{1,0:T(8,128)(2,1)S(1)} %get-tuple-element.23), channel_id=1, source_target_pairs={{0,4},{4,0},{8,12},{12,8},{16,20},{20,16},{24,28},{28,24},{1,5},{5... | collective-permute-start | bytes 786440 | tf_op jit(solution)/shard_map/ppermute | solution.py:32
  4.7 3.1 %collective-permute-start.1 = (bf16[128,1024]{1,0:T(8,128)(2,1)S(1)}, bf16[128,1024]{1,0:T(8,128)(2,1)S(1)}, u32[]{:S(2)}, u32[]{:S(2)}) collective-permute-start(bf16[128,1024]{1,0:T(8,128)(2,1)S(1)} %get-tuple-element.24), channel_id=1, source_target_pairs={{4,8},{8,4},{12,16},{16,12},{20,24},{24,20},{5,9},{9,5},{13,17},{1... | collective-permute-start | bytes 786440 | tf_op jit(solution)/shard_map/ppermute | solution.py:32
  7.8 0.0 copy-done.7
  7.9 0.0 copy-done.9
  7.9 0.0 copy-done.8
  7.9 0.0 copy-done
  7.9 0.0 copy-done.2
  7.9 3.0 %shard_map.109 = (f32[160,1024]{1,0:T(8,128)S(1)}, bf16[6,8,80,128]{3,2,1,0:T(8,128)(2,1)S(1)}, f32[2,6,144,144]{3,2,1,0:T(8,128)S(1)}) custom-call(f32[512,1024]{1,0:T(8,128)S(1)} %copy-done, f32[2,12,144,144]{3,2,1,0:T(8,128)} %pupils_ref.1, bf16[160,768]{1,0:T(8,128)(2,1)S(1)} %copy-done.7, f32[12]{0:T(128)S(1)} %copy-done.2, ...), custom_call_target="tpu_custom_call" | custom-call | flops 2000000000 | bytes 4000000 | tf_op jit(solution)/shard_map/pallas_call | solution.py:449
  10.9 0.0 collective-permute-done.near_ref
  10.9 4.4 %collective-permute-done.1.cross_ref = bf16[128,1024]{1,0:T(8,128)(2,1)S(1)} collective-permute-done((bf16[128,1024]{1,0:T(8,128)(2,1)S(1)}, bf16[128,1024]{1,0:T(8,128)(2,1)S(1)}, u32[]{:S(2)}, u32[]{:S(2)}) %collective-permute-start.1) | collective-permute-done | bytes 262176 | tf_op jit(solution)/shard_map/ppermute | solution.py:32
  15.4 0.0 copy-done.3
  15.4 0.0 copy-done.6
  15.4 1.1 %shard_map.111 = (bf16[160,640]{1,0:T(8,128)(2,1)S(1)}, bf16[160,128]{1,0:T(8,128)(2,1)S(1)}, bf16[160,384]{1,0:T(8,128)(2,1)S(1)}) custom-call(s32[1,2]{1,0:T(1,128)S(1)} %copy-done.3, f32[160,1024]{1,0:T(8,128)S(1)} %get-tuple-element.22.mid_ref, bf16[128,1024]{1,0:T(8,128)(2,1)S(1)} %collective-permute-done.near_ref, ...), custom_call_target="tpu_custom_call" | custom-call | flops 500000000 | bytes 1000000 | tf_op jit(solution)/shard_map/pallas_call | solution.py:461
  16.5 1.4 %collective-permute-start.2 = (bf16[160,384]{1,0:T(8,128)(2,1)S(1)}, bf16[160,384]{1,0:T(8,128)(2,1)S(1)}, u32[]{:S(2)}, u32[]{:S(2)}) collective-permute-start(bf16[160,384]{1,0:T(8,128)(2,1)S(1)} %get-tuple-element.28), channel_id=1, source_target_pairs={{0,1},{1,2},{2,3},{3,0},{4,5},{5,6},{6,7},{7,4},{8,9},{9,10},{10,1... | collective-permute-start | bytes 368648 | tf_op jit(solution)/shard_map/ppermute | solution.py:42
  17.8 1.8 %shard_map.112 = (f32[160,256]{1,0:T(8,128)S(1)}, bf16[12,8,80,128]{3,2,1,0:T(8,128)(2,1)S(1)}) custom-call(f32[2,6,144,144]{3,2,1,0:T(8,128)S(1)} %get-tuple-element.21.pupils_ref, bf16[160,640]{1,0:T(8,128)(2,1)S(1)} %get-tuple-element.25.own_ref, bf16[768,256]{1,0:T(8,128)(2,1)S(1)} %copy-done.6, bf16[6,8,80,128]{3,2,1,0:T(8,128)(2,1)S(1)} %get-tuple-element.26.quads_ref, ...), custom_call_target="tpu_custom_call" | custom-call | flops 2000000000 | bytes 4000000 | tf_op jit(solution)/shard_map/pallas_call | solution.py:471
  19.6 2.4 %collective-permute-done.2.sent_ref = bf16[160,384]{1,0:T(8,128)(2,1)S(1)} collective-permute-done((bf16[160,384]{1,0:T(8,128)(2,1)S(1)}, bf16[160,384]{1,0:T(8,128)(2,1)S(1)}, u32[]{:S(2)}, u32[]{:S(2)}) %collective-permute-start.2) | collective-permute-done | bytes 122912 | tf_op jit(solution)/shard_map/ppermute | solution.py:42
  22.0 0.0 collective-permute-done.3.other_ref
  22.0 0.0 copy-done.5
  22.1 11.3 %shard_map.113.mine_ref = bf16[160,512]{1,0:T(8,128)(2,1)S(1)} custom-call(s32[1,2]{1,0:T(1,128)S(1)} %copy-done.3, f32[160,256]{1,0:T(8,128)S(1)} %get-tuple-element.27.base_ref, bf16[160,384]{1,0:T(8,128)(2,1)S(1)} %collective-permute-done.2.sent_ref, bf16[160,128]{1,0:T(8,128)(2,1)S(1)} %get-tuple-element.29.low_ref, bf16[512,1024]{1,0:T(8,128)(2,1)S(1)} %copy-done.1, ...), custom_call_target="tpu_custom_call" | custom-call | flops 7500000256 | bytes 15000000 | tf_op jit(solution)/shard_map/pallas_call | solution.py:478
  33.4 0.1 collective-permute-start.4
  33.5 4.2 %collective-permute-done.4.sent_ref = bf16[160,512]{1,0:T(8,128)(2,1)S(1)} collective-permute-done((bf16[160,512]{1,0:T(8,128)(2,1)S(1)}, bf16[160,512]{1,0:T(8,128)(2,1)S(1)}, u32[]{:S(2)}, u32[]{:S(2)}) %collective-permute-start.4) | collective-permute-done | bytes 163872 | tf_op jit(solution)/shard_map/ppermute | solution.py:42
  37.6 0.6 %shard_map.114 = (bf16[160,1024]{1,0:T(8,128)(2,1)S(1)}, bf16[128,1024]{1,0:T(8,128)(2,1)S(1)}, bf16[128,1024]{1,0:T(8,128)(2,1)S(1)}) custom-call(bf16[160,512]{1,0:T(8,128)(2,1)S(1)} %shard_map.113.mine_ref, bf16[160,512]{1,0:T(8,128)(2,1)S(1)} %collective-permute-done.4.sent_ref, bf16[768,160]{1,0:T(8,128)(2,1)S(1)} %copy-done.4, ...), custom_call_target="tpu_custom_call" | custom-call | flops 500000000 | bytes 1000000 | tf_op jit(solution)/shard_map/pallas_call | solution.py:500
  38.2 0.1 collective-permute-start.5
  38.3 5.3 %collective-permute-start.6 = (bf16[128,1024]{1,0:T(8,128)(2,1)S(1)}, bf16[128,1024]{1,0:T(8,128)(2,1)S(1)}, u32[]{:S(2)}, u32[]{:S(2)}) collective-permute-start(bf16[128,1024]{1,0:T(8,128)(2,1)S(1)} %get-tuple-element.33), channel_id=1, source_target_pairs={{4,8},{8,4},{12,16},{16,12},{20,24},{24,20},{5,9},{9,5},{13,17},{1... | collective-permute-start | bytes 786440 | tf_op jit(solution)/shard_map/ppermute | solution.py:32
  43.6 1.4 %shard_map.115 = (f32[512,1024]{1,0:T(8,128)}, f32[256,1024]{1,0:T(8,128)S(1)}) custom-call(f32[512,1024]{1,0:T(8,128)S(1)} %copy-done, bf16[160,1024]{1,0:T(8,128)(2,1)S(1)} %get-tuple-element.34.mixed_ref, bf16[768,160]{1,0:T(8,128)(2,1)S(1)} %copy-done.4), custom_call_target="tpu_custom_call" | custom-call | flops 1000000000 | bytes 2000000 | tf_op jit(solution)/shard_map/pallas_call | solution.py:510
  45.0 0.0 collective-permute-done.5.near_ref
  45.0 4.9 %collective-permute-done.6.cross_ref = bf16[128,1024]{1,0:T(8,128)(2,1)S(1)} collective-permute-done((bf16[128,1024]{1,0:T(8,128)(2,1)S(1)}, bf16[128,1024]{1,0:T(8,128)(2,1)S(1)}, u32[]{:S(2)}, u32[]{:S(2)}) %collective-permute-start.6) | collective-permute-done | bytes 262176 | tf_op jit(solution)/shard_map/ppermute | solution.py:32
  49.9 1.0 %shard_map.116 = f32[512,1024]{1,0:T(8,128)} custom-call(bf16[128,1024]{1,0:T(8,128)(2,1)S(1)} %collective-permute-done.5.near_ref, bf16[128,1024]{1,0:T(8,128)(2,1)S(1)} %collective-permute-done.6.cross_ref, f32[256,1024]{1,0:T(8,128)S(1)} %get-tuple-element.35.rims_ref, f32[512,1024]{1,0:T(8,128)} %get-tuple-element.36.base_ref), custom_call_target="tpu_custom_call", output_to_operand_aliasing={{}: (3, {})} | custom-call | tf_op jit(solution)/shard_map/pallas_call | solution.py:519
  (10 shorter events, 0.0 us)
Async XLA Ops:
  0.0 7.9 %copy-start.7 = (bf16[160,768]{1,0:T(8,128)(2,1)S(1)}, bf16[160,768]{1,0:T(8,128)(2,1)}, u32[]{:S(2)}) copy-start(bf16[160,768]{1,0:T(8,128)(2,1)} %constant.14.clone.table_ref.row_ref) | copy-start | bytes 737284
  0.0 7.9 %copy-start.9 = (bf16[144,256]{1,0:T(8,128)(2,1)S(1)}, bf16[144,256]{1,0:T(8,128)(2,1)}, u32[]{:S(2)}) copy-start(bf16[144,256]{1,0:T(8,128)(2,1)} %constant.13.clone.col_ref) | copy-start | bytes 221188
  0.0 7.9 %copy-start.8 = (bf16[160,144]{1,0:T(8,128)(2,1)S(1)}, bf16[160,144]{1,0:T(8,128)(2,1)}, u32[]{:S(2)}) copy-start(bf16[160,144]{1,0:T(8,128)(2,1)} %constant.12.clone.row_ref) | copy-start | bytes 138244
  0.0 7.9 %copy-start = (f32[512,1024]{1,0:T(8,128)S(1)}, f32[512,1024]{1,0:T(8,128)}, u32[]{:S(2)}) copy-start(f32[512,1024]{1,0:T(8,128)} %mask_ref.5) | copy-start | bytes 6291460
  0.0 7.9 %copy-start.2 = (f32[12]{0:T(128)S(1)}, f32[12]{0:T(128)}, u32[]{:S(2)}) copy-start(f32[12]{0:T(128)} %weights_ref.3) | copy-start | bytes 148
  1.6 20.5 %collective-permute-start.3 = (bf16[512,512]{1,0:T(8,128)(2,1)S(1)}, bf16[512,512]{1,0:T(8,128)(2,1)S(1)}, u32[]{:S(2)}, u32[]{:S(2)}) collective-permute-start(bf16[512,512]{1,0:T(8,128)(2,1)S(1)} %get-tuple-element.30), channel_id=1, source_target_pairs={{0,1},{1,2},{2,3},{3,0},{4,5},{5,6},{6,7},{7,4},{8,9},{9,10},{10,1... | collective-permute-start | bytes 1572872 | tf_op jit(solution)/shard_map/ppermute | solution.py:42
  3.8 7.2 %collective-permute-start = (bf16[128,1024]{1,0:T(8,128)(2,1)S(1)}, bf16[128,1024]{1,0:T(8,128)(2,1)S(1)}, u32[]{:S(2)}, u32[]{:S(2)}) collective-permute-start(bf16[128,1024]{1,0:T(8,128)(2,1)S(1)} %get-tuple-element.23), channel_id=1, source_target_pairs={{0,4},{4,0},{8,12},{12,8},{16,20},{20,16},{24,28},{28,24},{1,5},{5... | collective-permute-start | bytes 786440 | tf_op jit(solution)/shard_map/ppermute | solution.py:32
  4.7 10.6 %copy-start.3 = (s32[1,2]{1,0:T(1,128)S(1)}, s32[1,2]{1,0:T(1,128)}, u32[]{:S(2)}) copy-start(s32[1,2]{1,0:T(1,128)} %live_ref.3) | copy-start | bytes 28
  4.7 10.6 %copy-start.6 = (bf16[768,256]{1,0:T(8,128)(2,1)S(1)}, bf16[768,256]{1,0:T(8,128)(2,1)}, u32[]{:S(2)}) copy-start(bf16[768,256]{1,0:T(8,128)(2,1)} %constant.17.clone.col_t_ref) | copy-start | bytes 1179652
  4.7 10.6 %collective-permute-start.1 = (bf16[128,1024]{1,0:T(8,128)(2,1)S(1)}, bf16[128,1024]{1,0:T(8,128)(2,1)S(1)}, u32[]{:S(2)}, u32[]{:S(2)}) collective-permute-start(bf16[128,1024]{1,0:T(8,128)(2,1)S(1)} %get-tuple-element.24), channel_id=1, source_target_pairs={{4,8},{8,4},{12,16},{16,12},{20,24},{24,20},{5,9},{9,5},{13,17},{1... | collective-permute-start | bytes 786440 | tf_op jit(solution)/shard_map/ppermute | solution.py:32
  16.5 5.6 %collective-permute-start.2 = (bf16[160,384]{1,0:T(8,128)(2,1)S(1)}, bf16[160,384]{1,0:T(8,128)(2,1)S(1)}, u32[]{:S(2)}, u32[]{:S(2)}) collective-permute-start(bf16[160,384]{1,0:T(8,128)(2,1)S(1)} %get-tuple-element.28), channel_id=1, source_target_pairs={{0,1},{1,2},{2,3},{3,0},{4,5},{5,6},{6,7},{7,4},{8,9},{9,10},{10,1... | collective-permute-start | bytes 368648 | tf_op jit(solution)/shard_map/ppermute | solution.py:42
  17.8 4.2 %copy-start.1 = (bf16[512,1024]{1,0:T(8,128)(2,1)S(1)}, bf16[512,1024]{1,0:T(8,128)(2,1)}, u32[]{:S(2)}) copy-start(bf16[512,1024]{1,0:T(8,128)(2,1)} %goal_ref.1) | copy-start | bytes 3145732
  17.8 4.2 %copy-start.4 = (bf16[768,160]{1,0:T(8,128)(2,1)S(1)}, bf16[768,160]{1,0:T(8,128)(2,1)}, u32[]{:S(2)}) copy-start(bf16[768,160]{1,0:T(8,128)(2,1)} %constant.15.clone.row_t_ref) | copy-start | bytes 737284
  17.8 4.2 %copy-start.5 = (bf16[256,768]{1,0:T(8,128)(2,1)S(1)}, bf16[256,768]{1,0:T(8,128)(2,1)}, u32[]{:S(2)}) copy-start(bf16[256,768]{1,0:T(8,128)(2,1)} %constant.16.clone.col_ref) | copy-start | bytes 1179652
  33.4 4.2 %collective-permute-start.4 = (bf16[160,512]{1,0:T(8,128)(2,1)S(1)}, bf16[160,512]{1,0:T(8,128)(2,1)S(1)}, u32[]{:S(2)}, u32[]{:S(2)}) collective-permute-start(bf16[160,512]{1,0:T(8,128)(2,1)S(1)} %shard_map.113.mine_ref), channel_id=1, source_target_pairs={{0,3},{1,0},{2,1},{3,2},{4,7},{5,4},{6,5},{7,6},{8,11},{9,8},{10,9... | collective-permute-start | bytes 491528 | tf_op jit(solution)/shard_map/ppermute | solution.py:42
  38.2 6.8 %collective-permute-start.5 = (bf16[128,1024]{1,0:T(8,128)(2,1)S(1)}, bf16[128,1024]{1,0:T(8,128)(2,1)S(1)}, u32[]{:S(2)}, u32[]{:S(2)}) collective-permute-start(bf16[128,1024]{1,0:T(8,128)(2,1)S(1)} %get-tuple-element.32), channel_id=1, source_target_pairs={{0,4},{4,0},{8,12},{12,8},{16,20},{20,16},{24,28},{28,24},{1,5},{5... | collective-permute-start | bytes 786440 | tf_op jit(solution)/shard_map/ppermute | solution.py:32
  38.3 11.7 %collective-permute-start.6 = (bf16[128,1024]{1,0:T(8,128)(2,1)S(1)}, bf16[128,1024]{1,0:T(8,128)(2,1)S(1)}, u32[]{:S(2)}, u32[]{:S(2)}) collective-permute-start(bf16[128,1024]{1,0:T(8,128)(2,1)S(1)} %get-tuple-element.33), channel_id=1, source_target_pairs={{4,8},{8,4},{12,16},{16,12},{20,24},{24,20},{5,9},{9,5},{13,17},{1... | collective-permute-start | bytes 786440 | tf_op jit(solution)/shard_map/ppermute | solution.py:32

commit v7 on v6

--- a/solution.py
+++ b/solution.py
@@ -37,9 +37,8 @@
     return [pl.multiple_of(side * reach, AMBIT) for side in (1 - odd, odd)]
 
 
-def turned(block, axis, step):
-    count = lax.axis_size(axis)
-    return lax.ppermute(block, axis, [(i, (i + step) % count) for i in range(count)])
+def col_parity():
+    return lax.rem(lax.axis_index("col"), 2)
 
 
 def dot(leading, trailing):
@@ -106,7 +105,8 @@
 
 def edges_kernel(mask_ref, target_ref, near_ref, cross_ref, goal_ref, stage_ref, sems):
     tile = mask_ref.shape[0]
-    whole = pltpu.make_async_copy(target_ref.at[:, tile:], goal_ref, sems.at[2])
+    far = pl.multiple_of((1 - col_parity()) * tile, LANE)
+    whole = pltpu.make_async_copy(target_ref.at[:, pl.ds(far, tile)], goal_ref, sems.at[2])
     copies = []
     for index, start in enumerate(sides(tile - AMBIT)):
         copy = pltpu.make_async_copy(
@@ -140,7 +140,7 @@
 
 
 def partial_kernel(
-    live_ref, mid_ref, near_ref, cross_ref, table_ref, col_t_ref, own_ref, low_ref, sent_ref
+    live_ref, mid_ref, near_ref, cross_ref, table_ref, col_t_ref, own_ref, kept_ref, facing_ref, sent_ref
 ):
     extent = table_ref.shape[1]
     width = mid_ref.shape[1]
@@ -149,16 +149,31 @@
     for start, rim_ref in zip(sides(extent - AMBIT), (near_ref, cross_ref)):
         total = total + dot(table_ref[:, pl.ds(start, AMBIT)], rim_ref[...])
     total = total.astype(jnp.bfloat16)
-    own_ref[...] = total[:, : tile + AMBIT]
-    low_ref[...] = total[:, :AMBIT]
-    sent_ref[:, :AMBIT] = total[:, width - AMBIT :]
-    main = dot(total[:, tile - AMBIT :], col_t_ref[: tile + AMBIT])
-    shape = main.shape
-    flag = (lax.broadcasted_iota(jnp.int32, shape, 0) == shape[0] - 1) & (
-        lax.broadcasted_iota(jnp.int32, shape, 1) == shape[1] - 1
-    )
-    live = live_ref[0, live_ref.shape[1] - 1].astype(jnp.float32)
-    sent_ref[:, AMBIT:] = jnp.where(flag, live, main).astype(jnp.bfloat16)
+    parity = col_parity()
+    live = live_ref[0, 1 - parity].astype(jnp.float32)
+
+    def store(near, far, far_table, facing, kept):
+        own_ref[...] = total[:, near]
+        kept_ref[...] = total[:, kept]
+        facing_ref[...] = total[:, facing]
+        main = dot(total[:, far], col_t_ref[far_table])
+        shape = main.shape
+        flag = (lax.broadcasted_iota(jnp.int32, shape, 0) == shape[0] - 1) & (
+            lax.broadcasted_iota(jnp.int32, shape, 1) == shape[1] - 1
+        )
+        sent_ref[...] = jnp.where(flag, live, main).astype(jnp.bfloat16)
+
+    reach = tile + AMBIT
+    first, last = slice(0, reach), slice(width - reach, width)
+    low, high = slice(0, AMBIT), slice(width - AMBIT, width)
+
+    @pl.when(parity == 0)
+    def _():
+        store(first, last, slice(0, reach), low, high)
+
+    @pl.when(parity > 0)
+    def _():
+        store(last, first, slice(AMBIT, extent), high, low)
 
 
 def late_kernel(
@@ -166,7 +181,9 @@
     base_ref, out_ref,
 ):
     out_ref[:first] = quads_ref[...]
-    base_ref[...] = dot(own_ref[...], col_t_ref[AMBIT:])
+    reach = own_ref.shape[1]
+    start = pl.multiple_of((1 - col_parity()) * AMBIT, AMBIT)
+    base_ref[...] = dot(own_ref[...], col_t_ref[pl.ds(start, reach)])
     pupil_steps(rows, lanes, first, last, pupils_ref, weights_ref, row_ref, col_ref, out_ref)
 
 
@@ -185,8 +202,9 @@
     lanes,
     live_ref,
     base_ref,
+    facing_ref,
     sent_ref,
-    low_ref,
+    kept_ref,
     goal_ref,
     other_ref,
     pupil_ref,
@@ -195,6 +213,7 @@
     col_ref,
     col_t_ref,
     out_ref,
+    other_out_ref,
     spec_ref,
     amp_ref,
     sec_ref,
@@ -210,19 +229,17 @@
     kernels = pupil_ref.shape[0]
     halves = [slice(start, start + 2 * LANE) for start in range(0, tile, 2 * LANE)]
     inner = slice(AMBIT, AMBIT + tile)
-    outer = lax.axis_index("col") == 0
-    left = sent_ref[:, :AMBIT]
-    left = jnp.where(outer, jnp.zeros_like(left), left)
-    spec_ref[0] = base_ref[...] + dot(left, col_t_ref[:AMBIT])
-    right = low_ref[...]
-    right = jnp.where(outer, jnp.zeros_like(right), right)
-    spec_ref[1] = sent_ref[:, AMBIT:].astype(jnp.float32) + dot(right, col_t_ref[extent - AMBIT :])
-    corner = sent_ref[2 * rows - 16 :, AMBIT + 2 * lanes - LANE :].astype(jnp.float32)
+    parity = col_parity()
+    end = col_t_ref[pl.ds(pl.multiple_of(parity * (extent - AMBIT), AMBIT), AMBIT)]
+    spec_ref[0] = base_ref[...] + dot(facing_ref[...], end)
+    spec_ref[1] = sent_ref[...].astype(jnp.float32) + dot(kept_ref[...], end)
+    corner = sent_ref[2 * rows - 16 :, 2 * lanes - LANE :].astype(jnp.float32)
     other_live = jnp.max(corner[15:, LANE - 1 :])
     out_ref[...] = jnp.zeros_like(out_ref)
+    other_out_ref[...] = jnp.zeros_like(other_out_ref)
 
     def work(item, carry):
-        live = jnp.where(item == 0, live_ref[0, 0].astype(jnp.float32), other_live) > 0.0
+        live = jnp.where(item == 0, live_ref[0, parity].astype(jnp.float32), other_live) > 0.0
 
         @pl.when(live)
         def _():
@@ -318,20 +335,21 @@
 
             ans_ref[...] = jnp.zeros_like(ans_ref)
 
-            def slopes(ref):
+            def slopes(ref, first):
                 for where in halves:
+                    place = pl.ds(pl.multiple_of(first + where.start, LANE), 2 * LANE)
                     level = jnp.tanh(total_ref[:, where] - 0.5 * steepness * threshold_level)
-                    excess = 0.5 * level + 0.5 - ref[:, where].astype(jnp.float32)
+                    excess = 0.5 * level + 0.5 - ref[:, place].astype(jnp.float32)
                     slope_ref[:, where] = (excess * (1.0 - level * level)).astype(jnp.bfloat16)
                 back((0, 1), (0, 1))
 
             @pl.when(item == 0)
             def _():
-                slopes(goal_ref)
+                slopes(goal_ref, parity * tile)
 
             @pl.when(item > 0)
             def _():
-                slopes(other_ref)
+                slopes(other_ref, 0)
 
             def backward(first, last_group):
                 for step in range(0, 4, 2):
@@ -346,36 +364,42 @@
 
             in_groups(kernels, 4, backward)
 
-            def answer(first):
-                left, right = slice(first, first + lanes), slice(first + lanes, first + 2 * lanes)
-                out_ref[:rows, left] = (ans_ref[0] + ans_ref[2]).astype(jnp.bfloat16)
-                out_ref[:rows, right] = (ans_ref[3] - ans_ref[1]).astype(jnp.bfloat16)
-                out_ref[rows:, left] = (-(ans_ref[1] + ans_ref[3])).astype(jnp.bfloat16)
-                out_ref[rows:, right] = (ans_ref[2] - ans_ref[0]).astype(jnp.bfloat16)
+            def answer(ref):
+                ref[:rows, :lanes] = (ans_ref[0] + ans_ref[2]).astype(jnp.bfloat16)
+                ref[:rows, lanes:] = (ans_ref[3] - ans_ref[1]).astype(jnp.bfloat16)
+                ref[rows:, :lanes] = (-(ans_ref[1] + ans_ref[3])).astype(jnp.bfloat16)
+                ref[rows:, lanes:] = (ans_ref[2] - ans_ref[0]).astype(jnp.bfloat16)
 
             @pl.when(item == 0)
             def _():
-                answer(0)
+                answer(out_ref)
 
             @pl.when(item > 0)
             def _():
-                answer(2 * lanes)
+                answer(other_out_ref)
 
         return carry
 
     lax.fori_loop(0, 2, work, 0)
 
 
-def returned_kernel(tile, mine_ref, sent_ref, row_t_ref, col_ref, out_ref, near_ref, cross_ref, sum_ref):
+def returned_kernel(
+    tile, mine_ref, other_ref, paired_ref, facing_ref, row_t_ref, col_ref, out_ref, near_ref, cross_ref, sum_ref
+):
     width = out_ref.shape[1]
     extent = row_t_ref.shape[0]
-    lanes = mine_ref.shape[1] // 2
-    place = lax.axis_index("col")
-    before, after = mine_ref[:, lanes:], sent_ref[:, :lanes]
-    before = jnp.where(place == 0, jnp.zeros_like(before), before)
-    after = jnp.where(place == lax.axis_size("col") - 1, jnp.zeros_like(after), after)
+    odd = col_parity() > 0
+    mine, other, paired, facing = (
+        ref[...] for ref in (mine_ref, other_ref, paired_ref, facing_ref)
+    )
+    values = (
+        jnp.where(odd, other, facing),
+        jnp.where(odd, paired, mine),
+        jnp.where(odd, mine, paired),
+        jnp.where(odd, facing, other),
+    )
     sum_ref[...] = jnp.zeros_like(sum_ref)
-    for place, value in zip(range(-1, 3), (before, mine_ref[:, :lanes], sent_ref[:, lanes:], after)):
+    for place, value in zip(range(-1, 3), values):
         start = place * tile - AMBIT
         low, high = max(0, start), min(width, start + extent)
         sum_ref[:, low:high] += dot(value, col_ref[:, low - start : high - start])
@@ -443,7 +467,7 @@
         scratch=[pltpu.VMEM((2, AMBIT, width), f32), dma((3,))],
         limit=52,
     )(mask, target)
-    other_goal = turned(goal, "col", 1)
+    other_goal = swapped(goal, "col", 0)
     cross = swapped(cross, "row", 1)
     near = swapped(near, "row", 0)
     middle, quads, rest = call(
@@ -458,16 +482,18 @@
         limit=48,
         us=4,
     )(mask, pupils, row_table, weights, row_pick, col_pick)
-    own, low, sending = call(
+    own, kept, facing, sending = call(
         partial_kernel,
         (
             shape((2 * rows, tile + AMBIT), bf16),
             shape((2 * rows, AMBIT), bf16),
-            shape((2 * rows, AMBIT + 2 * lanes), bf16),
+            shape((2 * rows, AMBIT), bf16),
+            shape((2 * rows, 2 * lanes), bf16),
         ),
         [smem, *vmem(5)],
     )(live, middle, near, cross, row_table, col_table_t)
-    sent = turned(sending, "col", 1)
+    sent = swapped(sending, "col", 0)
+    faced = swapped(facing, "col", 1)
     base, all_quads = call(
         partial(late_kernel, rows, lanes, early, kernels),
         (shape((2 * rows, 2 * lanes), f32), shape((kernels, 8, rows, lanes), bf16)),
@@ -475,10 +501,11 @@
         limit=16,
         us=4,
     )(rest, own, col_table_t, quads, weights, row_pick, col_pick)
-    answers = call(
+    answer = shape((2 * rows, 2 * lanes), bf16)
+    mine, other = call(
         partial(core_kernel, rows, lanes),
-        shape((2 * rows, 4 * lanes), bf16),
-        [smem, *vmem(10)],
+        (answer, answer),
+        [smem, *vmem(11)],
         scratch=[
             pltpu.VMEM((2, 2 * rows, 2 * lanes), f32),
             pltpu.VMEM((4, 4 * rows, 2 * lanes), bf16),
@@ -493,16 +520,17 @@
         limit=36,
         us=15,
     )(
-        live, base, sent, low, target, other_goal, all_quads,
+        live, base, faced, sent, kept, target, other_goal, all_quads,
         row_table, row_table_t, col_table, col_table_t,
     )
-    returned = turned(answers, "col", -1)
+    paired = swapped(other, "col", 0)
+    returned = swapped(mine, "col", 1)
     mixed, near, cross = call(
         partial(returned_kernel, tile),
         (shape((2 * rows, width), bf16), shape((AMBIT, width), bf16), shape((AMBIT, width), bf16)),
-        vmem(4),
+        vmem(6),
         scratch=[pltpu.VMEM((2 * rows, width), f32)],
-    )(answers, returned, row_table_t, col_table)
+    )(mine, other, paired, returned, row_table_t, col_table)
     cross = swapped(cross, "row", 1)
     near = swapped(near, "row", 0)
     anywhere = pl.BlockSpec(memory_space=pl.ANY)

time: 51.1 us -> 54 us (1.057)
  the two profiles are of different devices: /device:TPU:1 before, /device:TPU:11 now
where the time goes in v7:
time: 54 us; the launch traced here: 53.4 us
  starting transfers between devices  26.2 us (49%)
  waiting for transfers between devices  15.7 us (29%)
  Pallas kernels  11.2 us (21%)
    ppermute x9, starting transfers between devices, swapped(): return lax.ppermute(block, axis, pairs)  26.2 us
    ppermute x9, waiting for transfers between devices, swapped(): return lax.ppermute(block, axis, pairs)  15.7 us
    pallas_call x1, Pallas kernels, body(): call(partial(early_kernel, rows, lanes, early), (shape((2 * rows, width),...  3.03 us
    pallas_call x1, Pallas kernels, body(): call(partial(late_kernel, rows, lanes, early, kernels), (shape((2 * rows,...  1.77 us
    pallas_call x1, Pallas kernels, body(): call(edges_kernel, (edge, edge, shape((tile, tile), bf16)), [hbm, hbm], s...  1.55 us
    pallas_call x1, Pallas kernels, body(): pl.pallas_call(update_kernel, out_shape=(whole, rims), in_specs=vmem(3),...  1.41 us
    pallas_call x1, Pallas kernels, body(): call(partial_kernel, (shape((2 * rows, tile + AMBIT), bf16), shape((2 * r...  1.11 us
  transfers between devices with their start and end apart: 9, of which 5 were waited for; matrix products, arithmetic and copies ran while one was open for 0% of the time, Pallas kernels for 14%

profile of v7, /device:TPU:11, one launch (start us, length us, event | category | flops | bytes accessed | tf_op | source)
XLA Modules:
  0.0 53.4 jit_solution(1519667518638337616)
XLA Ops:
  0.0 0.0 copy-start
  0.0 0.0 copy-start.2
  0.0 1.5 %shard_map.110 = (bf16[128,1024]{1,0:T(8,128)(2,1)S(1)}, bf16[128,1024]{1,0:T(8,128)(2,1)S(1)}, bf16[512,512]{1,0:T(8,128)(2,1)S(1)}) custom-call(f32[512,1024]{1,0:T(8,128)} %mask_ref.5, bf16[512,1024]{1,0:T(8,128)(2,1)} %goal_ref.1), custom_call_target="tpu_custom_call" | custom-call | flops 500000000 | bytes 1000000 | tf_op jit(solution)/shard_map/pallas_call | solution.py:463
  1.6 0.2 collective-permute-start.4
  1.8 1.0 %collective-permute-start = (bf16[128,1024]{1,0:T(8,128)(2,1)S(1)}, bf16[128,1024]{1,0:T(8,128)(2,1)S(1)}, u32[]{:S(2)}, u32[]{:S(2)}) collective-permute-start(bf16[128,1024]{1,0:T(8,128)(2,1)S(1)} %get-tuple-element.26), channel_id=1, source_target_pairs={{0,4},{4,0},{8,12},{12,8},{16,20},{20,16},{24,28},{28,24},{1,5},{5... | collective-permute-start | bytes 786440 | tf_op jit(solution)/shard_map/ppermute | solution.py:32
  2.8 3.1 %collective-permute-start.1 = (bf16[128,1024]{1,0:T(8,128)(2,1)S(1)}, bf16[128,1024]{1,0:T(8,128)(2,1)S(1)}, u32[]{:S(2)}, u32[]{:S(2)}) collective-permute-start(bf16[128,1024]{1,0:T(8,128)(2,1)S(1)} %get-tuple-element.27), channel_id=1, source_target_pairs={{4,8},{8,4},{12,16},{16,12},{20,24},{24,20},{5,9},{9,5},{13,17},{1... | collective-permute-start | bytes 786440 | tf_op jit(solution)/shard_map/ppermute | solution.py:32
  6.0 3.0 %shard_map.109 = (f32[160,1024]{1,0:T(8,128)S(1)}, bf16[6,8,80,128]{3,2,1,0:T(8,128)(2,1)S(1)}, f32[2,6,144,144]{3,2,1,0:T(8,128)S(1)}) custom-call(f32[512,1024]{1,0:T(8,128)S(1)} %copy-done, f32[2,12,144,144]{3,2,1,0:T(8,128)} %pupils_ref.1, bf16[160,768]{1,0:T(8,128)(2,1)S(1)} %copy-done.7, f32[12]{0:T(128)S(1)} %copy-done.2, ...), custom_call_target="tpu_custom_call" | custom-call | flops 2000000000 | bytes 4000000 | tf_op jit(solution)/shard_map/pallas_call | solution.py:473
  9.0 0.0 collective-permute-done.near_ref
  9.0 4.7 %collective-permute-done.1.cross_ref = bf16[128,1024]{1,0:T(8,128)(2,1)S(1)} collective-permute-done((bf16[128,1024]{1,0:T(8,128)(2,1)S(1)}, bf16[128,1024]{1,0:T(8,128)(2,1)S(1)}, u32[]{:S(2)}, u32[]{:S(2)}) %collective-permute-start.1) | collective-permute-done | bytes 262176 | tf_op jit(solution)/shard_map/ppermute | solution.py:32
  13.7 1.1 %shard_map.111 = (bf16[160,640]{1,0:T(8,128)(2,1)S(1)}, bf16[160,128]{1,0:T(8,128)(2,1)S(1)}, bf16[160,128]{1,0:T(8,128)(2,1)S(1)}, bf16[160,256]{1,0:T(8,128)(2,1)S(1)}) custom-call(s32[1,2]{1,0:T(1,128)S(1)} %copy-done.3, f32[160,1024]{1,0:T(8,128)S(1)} %get-tuple-element.25.mid_ref, bf16[128,1024]{1,0:T(8,128)(2,1)S(1)} %collective-permute-done.near_ref, ...), custom_call_target="tpu_custom_call" | custom-call | flops 500000000 | bytes 1000000 | tf_op jit(solution)/shard_map/pallas_call | solution.py:485
  14.8 4.3 %collective-permute-start.2 = (bf16[160,128]{1,0:T(8,128)(2,1)S(1)}, bf16[160,128]{1,0:T(8,128)(2,1)S(1)}, u32[]{:S(2)}, u32[]{:S(2)}) collective-permute-start(bf16[160,128]{1,0:T(8,128)(2,1)S(1)} %get-tuple-element.31), channel_id=1, source_target_pairs={{1,2},{2,1},{5,6},{6,5},{9,10},{10,9},{13,14},{14,13},{17,18},{18,... | collective-permute-start | bytes 122888 | tf_op jit(solution)/shard_map/ppermute | solution.py:32
  19.1 0.1 collective-permute-start.3
  19.2 0.0 copy-start.1
  19.2 0.0 copy-start.4
  19.2 0.0 copy-start.5
  19.2 1.8 %shard_map.112 = (f32[160,256]{1,0:T(8,128)S(1)}, bf16[12,8,80,128]{3,2,1,0:T(8,128)(2,1)S(1)}) custom-call(f32[2,6,144,144]{3,2,1,0:T(8,128)S(1)} %get-tuple-element.24.pupils_ref, bf16[160,640]{1,0:T(8,128)(2,1)S(1)} %get-tuple-element.28.own_ref, bf16[768,256]{1,0:T(8,128)(2,1)S(1)} %copy-done.6, bf16[6,8,80,128]{3,2,1,0:T(8,128)(2,1)S(1)} %get-tuple-element.29.quads_ref, ...), custom_call_target="tpu_custom_call" | custom-call | flops 2000000000 | bytes 4000000 | tf_op jit(solution)/shard_map/pallas_call | solution.py:497
  21.0 0.0 collective-permute-done.2.facing_ref
  21.0 1.4 %collective-permute-done.3.sent_ref = bf16[160,256]{1,0:T(8,128)(2,1)S(1)} collective-permute-done((bf16[160,256]{1,0:T(8,128)(2,1)S(1)}, bf16[160,256]{1,0:T(8,128)(2,1)S(1)}, u32[]{:S(2)}, u32[]{:S(2)}) %collective-permute-start.3) | collective-permute-done | bytes 81952 | tf_op jit(solution)/shard_map/ppermute | solution.py:32
  22.5 0.0 collective-permute-done.4.other_ref
  22.5 0.0 copy-done.4
  22.5 0.8 %shard_map.113 = (bf16[160,256]{1,0:T(8,128)(2,1)S(1)}, bf16[160,256]{1,0:T(8,128)(2,1)S(1)}) custom-call(s32[1,2]{1,0:T(1,128)S(1)} %copy-done.3, f32[160,256]{1,0:T(8,128)S(1)} %get-tuple-element.30.base_ref, bf16[160,128]{1,0:T(8,128)(2,1)S(1)} %collective-permute-done.2.facing_ref, bf16[160,256]{1,0:T(8,128)(2,1)S(1)} %collective-permute-done.3.sent_ref, ...), custom_call_target="tpu_custom_call" | custom-call | flops 7500000256 | bytes 15000000 | tf_op jit(solution)/shard_map/pallas_call | solution.py:505
  23.3 12.5 %collective-permute-start.6 = (bf16[160,256]{1,0:T(8,128)(2,1)S(1)}, bf16[160,256]{1,0:T(8,128)(2,1)S(1)}, u32[]{:S(2)}, u32[]{:S(2)}) collective-permute-start(bf16[160,256]{1,0:T(8,128)(2,1)S(1)} %get-tuple-element.36.mine_ref), channel_id=1, source_target_pairs={{1,2},{2,1},{5,6},{6,5},{9,10},{10,9},{13,14},{14,13},{17,18},{18,... | collective-permute-start | bytes 245768 | tf_op jit(solution)/shard_map/ppermute | solution.py:32
  35.8 0.1 collective-permute-start.5
  35.8 2.0 %collective-permute-done.6.facing_ref = bf16[160,256]{1,0:T(8,128)(2,1)S(1)} collective-permute-done((bf16[160,256]{1,0:T(8,128)(2,1)S(1)}, bf16[160,256]{1,0:T(8,128)(2,1)S(1)}, u32[]{:S(2)}, u32[]{:S(2)}) %collective-permute-start.6) | collective-permute-done | bytes 81952 | tf_op jit(solution)/shard_map/ppermute | solution.py:32
  37.8 2.4 %collective-permute-done.5.paired_ref = bf16[160,256]{1,0:T(8,128)(2,1)S(1)} collective-permute-done((bf16[160,256]{1,0:T(8,128)(2,1)S(1)}, bf16[160,256]{1,0:T(8,128)(2,1)S(1)}, u32[]{:S(2)}, u32[]{:S(2)}) %collective-permute-start.5) | collective-permute-done | bytes 81952 | tf_op jit(solution)/shard_map/ppermute | solution.py:32
  40.2 0.5 %shard_map.114 = (bf16[160,1024]{1,0:T(8,128)(2,1)S(1)}, bf16[128,1024]{1,0:T(8,128)(2,1)S(1)}, bf16[128,1024]{1,0:T(8,128)(2,1)S(1)}) custom-call(bf16[160,256]{1,0:T(8,128)(2,1)S(1)} %get-tuple-element.36.mine_ref, bf16[160,256]{1,0:T(8,128)(2,1)S(1)} %get-tuple-element.37.other_ref, bf16[160,256]{1,0:T(8,128)(2,1)S(1)} %collective-permute-done.5.paired_ref, ...), custom_call_target="tpu_custom_call" | custom-call | flops 500000000 | bytes 1000000 | tf_op jit(solution)/shard_map/pallas_call | solution.py:528
  40.7 0.6 %collective-permute-start.7 = (bf16[128,1024]{1,0:T(8,128)(2,1)S(1)}, bf16[128,1024]{1,0:T(8,128)(2,1)S(1)}, u32[]{:S(2)}, u32[]{:S(2)}) collective-permute-start(bf16[128,1024]{1,0:T(8,128)(2,1)S(1)} %get-tuple-element.38), channel_id=1, source_target_pairs={{0,4},{4,0},{8,12},{12,8},{16,20},{20,16},{24,28},{28,24},{1,5},{5... | collective-permute-start | bytes 786440 | tf_op jit(solution)/shard_map/ppermute | solution.py:32
  41.3 4.4 %collective-permute-start.8 = (bf16[128,1024]{1,0:T(8,128)(2,1)S(1)}, bf16[128,1024]{1,0:T(8,128)(2,1)S(1)}, u32[]{:S(2)}, u32[]{:S(2)}) collective-permute-start(bf16[128,1024]{1,0:T(8,128)(2,1)S(1)} %get-tuple-element.39), channel_id=1, source_target_pairs={{4,8},{8,4},{12,16},{16,12},{20,24},{24,20},{5,9},{9,5},{13,17},{1... | collective-permute-start | bytes 786440 | tf_op jit(solution)/shard_map/ppermute | solution.py:32
  45.7 1.4 %shard_map.115 = (f32[512,1024]{1,0:T(8,128)}, f32[256,1024]{1,0:T(8,128)S(1)}) custom-call(f32[512,1024]{1,0:T(8,128)S(1)} %copy-done, bf16[160,1024]{1,0:T(8,128)(2,1)S(1)} %get-tuple-element.40.mixed_ref, bf16[768,160]{1,0:T(8,128)(2,1)S(1)} %copy-done.4), custom_call_target="tpu_custom_call" | custom-call | flops 1000000000 | bytes 2000000 | tf_op jit(solution)/shard_map/pallas_call | solution.py:538
  47.1 0.0 collective-permute-done.7.near_ref
  47.1 5.2 %collective-permute-done.8.cross_ref = bf16[128,1024]{1,0:T(8,128)(2,1)S(1)} collective-permute-done((bf16[128,1024]{1,0:T(8,128)(2,1)S(1)}, bf16[128,1024]{1,0:T(8,128)(2,1)S(1)}, u32[]{:S(2)}, u32[]{:S(2)}) %collective-permute-start.8) | collective-permute-done | bytes 262176 | tf_op jit(solution)/shard_map/ppermute | solution.py:32
  52.4 1.0 %shard_map.116 = f32[512,1024]{1,0:T(8,128)} custom-call(bf16[128,1024]{1,0:T(8,128)(2,1)S(1)} %collective-permute-done.7.near_ref, bf16[128,1024]{1,0:T(8,128)(2,1)S(1)} %collective-permute-done.8.cross_ref, f32[256,1024]{1,0:T(8,128)S(1)} %get-tuple-element.41.rims_ref, f32[512,1024]{1,0:T(8,128)} %get-tuple-element.42.base_ref), custom_call_target="tpu_custom_call", output_to_operand_aliasing={{}: (3, {})} | custom-call | tf_op jit(solution)/shard_map/pallas_call | solution.py:547
  (14 shorter events, 0.0 us)
Async XLA Ops:
  0.0 5.9 %copy-start.7 = (bf16[160,768]{1,0:T(8,128)(2,1)S(1)}, bf16[160,768]{1,0:T(8,128)(2,1)}, u32[]{:S(2)}) copy-start(bf16[160,768]{1,0:T(8,128)(2,1)} %constant.14.clone.table_ref.row_ref) | copy-start | bytes 737284
  0.0 5.9 %copy-start.9 = (bf16[144,256]{1,0:T(8,128)(2,1)S(1)}, bf16[144,256]{1,0:T(8,128)(2,1)}, u32[]{:S(2)}) copy-start(bf16[144,256]{1,0:T(8,128)(2,1)} %constant.13.clone.col_ref) | copy-start | bytes 221188
  0.0 5.9 %copy-start.8 = (bf16[160,144]{1,0:T(8,128)(2,1)S(1)}, bf16[160,144]{1,0:T(8,128)(2,1)}, u32[]{:S(2)}) copy-start(bf16[160,144]{1,0:T(8,128)(2,1)} %constant.12.clone.row_ref) | copy-start | bytes 138244
  0.0 5.9 %copy-start = (f32[512,1024]{1,0:T(8,128)S(1)}, f32[512,1024]{1,0:T(8,128)}, u32[]{:S(2)}) copy-start(f32[512,1024]{1,0:T(8,128)} %mask_ref.5) | copy-start | bytes 6291460
  0.0 5.9 %copy-start.2 = (f32[12]{0:T(128)S(1)}, f32[12]{0:T(128)}, u32[]{:S(2)}) copy-start(f32[12]{0:T(128)} %weights_ref.3) | copy-start | bytes 148
  1.6 20.9 %collective-permute-start.4 = (bf16[512,512]{1,0:T(8,128)(2,1)S(1)}, bf16[512,512]{1,0:T(8,128)(2,1)S(1)}, u32[]{:S(2)}, u32[]{:S(2)}) collective-permute-start(bf16[512,512]{1,0:T(8,128)(2,1)S(1)} %get-tuple-element.34), channel_id=1, source_target_pairs={{0,1},{1,0},{2,3},{3,2},{4,5},{5,4},{6,7},{7,6},{8,9},{9,8},{10,11... | collective-permute-start | bytes 1572872 | tf_op jit(solution)/shard_map/ppermute | solution.py:32
  1.8 7.2 %collective-permute-start = (bf16[128,1024]{1,0:T(8,128)(2,1)S(1)}, bf16[128,1024]{1,0:T(8,128)(2,1)S(1)}, u32[]{:S(2)}, u32[]{:S(2)}) collective-permute-start(bf16[128,1024]{1,0:T(8,128)(2,1)S(1)} %get-tuple-element.26), channel_id=1, source_target_pairs={{0,4},{4,0},{8,12},{12,8},{16,20},{20,16},{24,28},{28,24},{1,5},{5... | collective-permute-start | bytes 786440 | tf_op jit(solution)/shard_map/ppermute | solution.py:32
  2.8 10.9 %copy-start.3 = (s32[1,2]{1,0:T(1,128)S(1)}, s32[1,2]{1,0:T(1,128)}, u32[]{:S(2)}) copy-start(s32[1,2]{1,0:T(1,128)} %live_ref.3) | copy-start | bytes 28
  2.8 10.9 %copy-start.6 = (bf16[768,256]{1,0:T(8,128)(2,1)S(1)}, bf16[768,256]{1,0:T(8,128)(2,1)}, u32[]{:S(2)}) copy-start(bf16[768,256]{1,0:T(8,128)(2,1)} %constant.17.clone.col_t_ref) | copy-start | bytes 1179652
  2.8 10.9 %collective-permute-start.1 = (bf16[128,1024]{1,0:T(8,128)(2,1)S(1)}, bf16[128,1024]{1,0:T(8,128)(2,1)S(1)}, u32[]{:S(2)}, u32[]{:S(2)}) collective-permute-start(bf16[128,1024]{1,0:T(8,128)(2,1)S(1)} %get-tuple-element.27), channel_id=1, source_target_pairs={{4,8},{8,4},{12,16},{16,12},{20,24},{24,20},{5,9},{9,5},{13,17},{1... | collective-permute-start | bytes 786440 | tf_op jit(solution)/shard_map/ppermute | solution.py:32
  14.8 6.2 %collective-permute-start.2 = (bf16[160,128]{1,0:T(8,128)(2,1)S(1)}, bf16[160,128]{1,0:T(8,128)(2,1)S(1)}, u32[]{:S(2)}, u32[]{:S(2)}) collective-permute-start(bf16[160,128]{1,0:T(8,128)(2,1)S(1)} %get-tuple-element.31), channel_id=1, source_target_pairs={{1,2},{2,1},{5,6},{6,5},{9,10},{10,9},{13,14},{14,13},{17,18},{18,... | collective-permute-start | bytes 122888 | tf_op jit(solution)/shard_map/ppermute | solution.py:32
  19.1 3.4 %collective-permute-start.3 = (bf16[160,256]{1,0:T(8,128)(2,1)S(1)}, bf16[160,256]{1,0:T(8,128)(2,1)S(1)}, u32[]{:S(2)}, u32[]{:S(2)}) collective-permute-start(bf16[160,256]{1,0:T(8,128)(2,1)S(1)} %get-tuple-element.32), channel_id=1, source_target_pairs={{0,1},{1,0},{2,3},{3,2},{4,5},{5,4},{6,7},{7,6},{8,9},{9,8},{10,11... | collective-permute-start | bytes 245768 | tf_op jit(solution)/shard_map/ppermute | solution.py:32
  19.2 3.3 %copy-start.1 = (bf16[512,1024]{1,0:T(8,128)(2,1)S(1)}, bf16[512,1024]{1,0:T(8,128)(2,1)}, u32[]{:S(2)}) copy-start(bf16[512,1024]{1,0:T(8,128)(2,1)} %goal_ref.1) | copy-start | bytes 3145732
  19.2 3.3 %copy-start.4 = (bf16[768,160]{1,0:T(8,128)(2,1)S(1)}, bf16[768,160]{1,0:T(8,128)(2,1)}, u32[]{:S(2)}) copy-start(bf16[768,160]{1,0:T(8,128)(2,1)} %constant.15.clone.row_t_ref) | copy-start | bytes 737284
  19.2 3.3 %copy-start.5 = (bf16[256,768]{1,0:T(8,128)(2,1)S(1)}, bf16[256,768]{1,0:T(8,128)(2,1)}, u32[]{:S(2)}) copy-start(bf16[256,768]{1,0:T(8,128)(2,1)} %constant.16.clone.col_ref) | copy-start | bytes 1179652
  23.3 14.6 %collective-permute-start.6 = (bf16[160,256]{1,0:T(8,128)(2,1)S(1)}, bf16[160,256]{1,0:T(8,128)(2,1)S(1)}, u32[]{:S(2)}, u32[]{:S(2)}) collective-permute-start(bf16[160,256]{1,0:T(8,128)(2,1)S(1)} %get-tuple-element.36.mine_ref), channel_id=1, source_target_pairs={{1,2},{2,1},{5,6},{6,5},{9,10},{10,9},{13,14},{14,13},{17,18},{18,... | collective-permute-start | bytes 245768 | tf_op jit(solution)/shard_map/ppermute | solution.py:32
  35.8 4.4 %collective-permute-start.5 = (bf16[160,256]{1,0:T(8,128)(2,1)S(1)}, bf16[160,256]{1,0:T(8,128)(2,1)S(1)}, u32[]{:S(2)}, u32[]{:S(2)}) collective-permute-start(bf16[160,256]{1,0:T(8,128)(2,1)S(1)} %get-tuple-element.37.other_ref), channel_id=1, source_target_pairs={{0,1},{1,0},{2,3},{3,2},{4,5},{5,4},{6,7},{7,6},{8,9},{9,8},{10,11... | collective-permute-start | bytes 245768 | tf_op jit(solution)/shard_map/ppermute | solution.py:32
  40.7 6.4 %collective-permute-start.7 = (bf16[128,1024]{1,0:T(8,128)(2,1)S(1)}, bf16[128,1024]{1,0:T(8,128)(2,1)S(1)}, u32[]{:S(2)}, u32[]{:S(2)}) collective-permute-start(bf16[128,1024]{1,0:T(8,128)(2,1)S(1)} %get-tuple-element.38), channel_id=1, source_target_pairs={{0,4},{4,0},{8,12},{12,8},{16,20},{20,16},{24,28},{28,24},{1,5},{5... | collective-permute-start | bytes 786440 | tf_op jit(solution)/shard_map/ppermute | solution.py:32
  41.3 11.1 %collective-permute-start.8 = (bf16[128,1024]{1,0:T(8,128)(2,1)S(1)}, bf16[128,1024]{1,0:T(8,128)(2,1)S(1)}, u32[]{:S(2)}, u32[]{:S(2)}) collective-permute-start(bf16[128,1024]{1,0:T(8,128)(2,1)S(1)} %get-tuple-element.39), channel_id=1, source_target_pairs={{4,8},{8,4},{12,16},{16,12},{20,24},{24,20},{5,9},{9,5},{13,17},{1... | collective-permute-start | bytes 786440 | tf_op jit(solution)/shard_map/ppermute | solution.py:32

commit v8 on v6

--- a/solution.py
+++ b/solution.py
@@ -275,7 +275,7 @@
 
             section(0, 0)
             section(1, 1)
-            total_ref[...] = jnp.zeros_like(total_ref)
+            total_ref[...] = jnp.full_like(total_ref, -0.5 * steepness * threshold_level)
 
             def forward(first, last_group):
                 for step in range(0, 4, 2):
@@ -320,7 +320,7 @@
 
             def slopes(ref):
                 for where in halves:
-                    level = jnp.tanh(total_ref[:, where] - 0.5 * steepness * threshold_level)
+                    level = jnp.tanh(total_ref[:, where])
                     excess = 0.5 * level + 0.5 - ref[:, where].astype(jnp.float32)
                     slope_ref[:, where] = (excess * (1.0 - level * level)).astype(jnp.bfloat16)
                 back((0, 1), (0, 1))
@@ -385,34 +385,26 @@
         rim_ref[...] = dot(row_t_ref[pl.ds(start, AMBIT)], mixed).astype(jnp.bfloat16)
 
 
-def update_kernel(mask_ref, mixed_ref, row_t_ref, out_ref, rims_ref, stage_ref, sem):
+def update_kernel(mask_ref, mixed_ref, near_ref, row_t_ref, out_ref, rim_ref, stage_ref, sem):
     tile = mask_ref.shape[0]
     stage_ref[...] = mask_ref[...] - step_rate * dot(
         row_t_ref[AMBIT : AMBIT + tile], mixed_ref[...]
     )
-    inner = pl.ds(AMBIT, tile - 2 * AMBIT)
-    copy = pltpu.make_async_copy(stage_ref.at[inner], out_ref.at[inner], sem)
+    near, cross = (pl.ds(start, AMBIT) for start in sides(tile - AMBIT))
+    stage_ref[near] = stage_ref[near] - step_rate * near_ref[...].astype(jnp.float32)
+    kept = pl.ds(pl.multiple_of((1 - lax.rem(lax.axis_index("row"), 2)) * AMBIT, AMBIT), tile - AMBIT)
+    copy = pltpu.make_async_copy(stage_ref.at[kept], out_ref.at[kept], sem)
     copy.start()
-    rims_ref[:AMBIT] = stage_ref[:AMBIT]
-    rims_ref[AMBIT:] = stage_ref[tile - AMBIT :]
+    rim_ref[...] = stage_ref[cross]
     copy.wait()
 
 
-def rims_kernel(near_ref, cross_ref, rims_ref, base_ref, out_ref, stage_ref, sems):
-    tile = out_ref.shape[0]
-    copies = []
-    places = zip((cross_ref, near_ref), sides(AMBIT)[::-1], sides(tile - AMBIT)[::-1])
-    for index, (rim_ref, place, start) in enumerate(places):
-        stage_ref[index] = rims_ref[pl.ds(place, AMBIT)] - step_rate * rim_ref[...].astype(
-            jnp.float32
-        )
-        copy = pltpu.make_async_copy(
-            stage_ref.at[index], out_ref.at[pl.ds(start, AMBIT)], sems.at[index]
-        )
-        copy.start()
-        copies.append(copy)
-    for copy in copies:
-        copy.wait()
+def rim_kernel(cross_ref, rim_ref, base_ref, out_ref, stage_ref, sem):
+    start = sides(out_ref.shape[0] - AMBIT)[1]
+    stage_ref[...] = rim_ref[...] - step_rate * cross_ref[...].astype(jnp.float32)
+    copy = pltpu.make_async_copy(stage_ref, out_ref.at[pl.ds(start, AMBIT)], sem)
+    copy.start()
+    copy.wait()
 
 
 def body(mask, target, live, pupils, weights):
@@ -506,25 +498,25 @@
     cross = swapped(cross, "row", 1)
     near = swapped(near, "row", 0)
     anywhere = pl.BlockSpec(memory_space=pl.ANY)
-    whole, rims = shape((tile, width), f32), shape((2 * AMBIT, width), f32)
-    updated, edges = pl.pallas_call(
+    whole, rim = shape((tile, width), f32), shape((AMBIT, width), f32)
+    updated, rim = pl.pallas_call(
         update_kernel,
-        out_shape=(whole, rims),
-        in_specs=vmem(3),
+        out_shape=(whole, rim),
+        in_specs=vmem(4),
         out_specs=(anywhere, *vmem(1)),
         scratch_shapes=[pltpu.VMEM((tile, width), f32), dma],
         cost_estimate=pl.CostEstimate(flops=10**9, bytes_accessed=2 * 10**6, transcendentals=0),
         compiler_params=pltpu.CompilerParams(vmem_limit_bytes=16 * MIB),
-    )(mask, mixed, row_table_t)
+    )(mask, mixed, near, row_table_t)
     return pl.pallas_call(
-        rims_kernel,
+        rim_kernel,
         out_shape=whole,
-        in_specs=[*vmem(3), anywhere],
+        in_specs=[*vmem(2), anywhere],
         out_specs=anywhere,
-        scratch_shapes=[pltpu.VMEM((2, AMBIT, width), f32), pltpu.SemaphoreType.DMA((2,))],
-        input_output_aliases={3: 0},
+        scratch_shapes=[pltpu.VMEM((AMBIT, width), f32), dma],
+        input_output_aliases={2: 0},
         compiler_params=pltpu.CompilerParams(vmem_limit_bytes=8 * MIB),
-    )(near, cross, edges, updated)
+    )(cross, rim, updated)
 
 
 def solution(mesh):

time: 51.1 us -> 50.9 us (level)
  transfers between devices with their start and end apart: 7 -> 7, of which waited for: 4 -> 4; matrix products, arithmetic and copies ran while one was open for 0% -> 0% of each run, Pallas kernels for 14% -> 15%
where the time goes in v8:
time: 50.9 us; the launch traced here: 50.7 us
  Pallas kernels  21.8 us (43%)
  waiting for transfers between devices  15.6 us (31%)
  starting transfers between devices  13 us (26%)
    pallas_call x1, Pallas kernels, body(): call(partial(core_kernel, rows, lanes), shape((2 * rows, 4 * lanes), bf16...  11.3 us
    ppermute x4, starting transfers between devices, swapped(): return lax.ppermute(block, axis, pairs)  9.46 us
    ppermute x4, waiting for transfers between devices, swapped(): return lax.ppermute(block, axis, pairs)  9.03 us
    ppermute x3, waiting for transfers between devices, turned(): lax.ppermute(block, axis, [(i, (i + step) % count) for i in range(count)])  6.61 us
    ppermute x3, starting transfers between devices, turned(): lax.ppermute(block, axis, [(i, (i + step) % count) for i in range(count)])  3.58 us
    pallas_call x1, Pallas kernels, body(): call(partial(early_kernel, rows, lanes, early), (shape((2 * rows, width),...  3.03 us
    pallas_call x1, Pallas kernels, body(): call(partial(late_kernel, rows, lanes, early, kernels), (shape((2 * rows,...  1.77 us
    pallas_call x1, Pallas kernels, body(): pl.pallas_call(update_kernel, out_shape=(whole, rim), in_specs=vmem(4), o...  1.72 us
  transfers between devices with their start and end apart: 7, of which 4 were waited for; matrix products, arithmetic and copies ran while one was open for 0% of the time, Pallas kernels for 15%

profile of v8, /device:TPU:1, one launch (start us, length us, event | category | flops | bytes accessed | tf_op | source)
XLA Modules:
  0.0 50.7 jit_solution(2470321845889225817)
XLA Ops:
  0.0 0.0 copy-start
  0.0 0.0 copy-start.2
  0.0 1.5 %shard_map.110 = (bf16[128,1024]{1,0:T(8,128)(2,1)S(1)}, bf16[128,1024]{1,0:T(8,128)(2,1)S(1)}, bf16[512,512]{1,0:T(8,128)(2,1)S(1)}) custom-call(f32[512,1024]{1,0:T(8,128)} %mask_ref.5, bf16[512,1024]{1,0:T(8,128)(2,1)} %goal_ref.1), custom_call_target="tpu_custom_call" | custom-call | flops 500000000 | bytes 1000000 | tf_op jit(solution)/shard_map/pallas_call | solution.py:431
  1.6 2.2 %collective-permute-start.3 = (bf16[512,512]{1,0:T(8,128)(2,1)S(1)}, bf16[512,512]{1,0:T(8,128)(2,1)S(1)}, u32[]{:S(2)}, u32[]{:S(2)}) collective-permute-start(bf16[512,512]{1,0:T(8,128)(2,1)S(1)} %get-tuple-element.30), channel_id=1, source_target_pairs={{0,1},{1,2},{2,3},{3,0},{4,5},{5,6},{6,7},{7,4},{8,9},{9,10},{10,1... | collective-permute-start | bytes 1572872 | tf_op jit(solution)/shard_map/ppermute | solution.py:42
  3.8 1.0 %collective-permute-start = (bf16[128,1024]{1,0:T(8,128)(2,1)S(1)}, bf16[128,1024]{1,0:T(8,128)(2,1)S(1)}, u32[]{:S(2)}, u32[]{:S(2)}) collective-permute-start(bf16[128,1024]{1,0:T(8,128)(2,1)S(1)} %get-tuple-element.23), channel_id=1, source_target_pairs={{0,4},{4,0},{8,12},{12,8},{16,20},{20,16},{24,28},{28,24},{1,5},{5... | collective-permute-start | bytes 786440 | tf_op jit(solution)/shard_map/ppermute | solution.py:32
  4.7 3.1 %collective-permute-start.1 = (bf16[128,1024]{1,0:T(8,128)(2,1)S(1)}, bf16[128,1024]{1,0:T(8,128)(2,1)S(1)}, u32[]{:S(2)}, u32[]{:S(2)}) collective-permute-start(bf16[128,1024]{1,0:T(8,128)(2,1)S(1)} %get-tuple-element.24), channel_id=1, source_target_pairs={{4,8},{8,4},{12,16},{16,12},{20,24},{24,20},{5,9},{9,5},{13,17},{1... | collective-permute-start | bytes 786440 | tf_op jit(solution)/shard_map/ppermute | solution.py:32
  7.8 0.0 copy-done.7
  7.9 0.0 copy-done.9
  7.9 0.0 copy-done.8
  7.9 0.0 copy-done
  7.9 0.0 copy-done.2
  7.9 3.0 %shard_map.109 = (f32[160,1024]{1,0:T(8,128)S(1)}, bf16[6,8,80,128]{3,2,1,0:T(8,128)(2,1)S(1)}, f32[2,6,144,144]{3,2,1,0:T(8,128)S(1)}) custom-call(f32[512,1024]{1,0:T(8,128)S(1)} %copy-done, f32[2,12,144,144]{3,2,1,0:T(8,128)} %pupils_ref.1, bf16[160,768]{1,0:T(8,128)(2,1)S(1)} %copy-done.7, f32[12]{0:T(128)S(1)} %copy-done.2, ...), custom_call_target="tpu_custom_call" | custom-call | flops 2000000000 | bytes 4000000 | tf_op jit(solution)/shard_map/pallas_call | solution.py:441
  10.9 0.0 collective-permute-done.near_ref
  10.9 4.4 %collective-permute-done.1.cross_ref = bf16[128,1024]{1,0:T(8,128)(2,1)S(1)} collective-permute-done((bf16[128,1024]{1,0:T(8,128)(2,1)S(1)}, bf16[128,1024]{1,0:T(8,128)(2,1)S(1)}, u32[]{:S(2)}, u32[]{:S(2)}) %collective-permute-start.1) | collective-permute-done | bytes 262176 | tf_op jit(solution)/shard_map/ppermute | solution.py:32
  15.4 0.0 copy-done.3
  15.4 0.0 copy-done.6
  15.4 1.1 %shard_map.111 = (bf16[160,640]{1,0:T(8,128)(2,1)S(1)}, bf16[160,128]{1,0:T(8,128)(2,1)S(1)}, bf16[160,384]{1,0:T(8,128)(2,1)S(1)}) custom-call(s32[1,2]{1,0:T(1,128)S(1)} %copy-done.3, f32[160,1024]{1,0:T(8,128)S(1)} %get-tuple-element.22.mid_ref, bf16[128,1024]{1,0:T(8,128)(2,1)S(1)} %collective-permute-done.near_ref, ...), custom_call_target="tpu_custom_call" | custom-call | flops 500000000 | bytes 1000000 | tf_op jit(solution)/shard_map/pallas_call | solution.py:453
  16.5 1.4 %collective-permute-start.2 = (bf16[160,384]{1,0:T(8,128)(2,1)S(1)}, bf16[160,384]{1,0:T(8,128)(2,1)S(1)}, u32[]{:S(2)}, u32[]{:S(2)}) collective-permute-start(bf16[160,384]{1,0:T(8,128)(2,1)S(1)} %get-tuple-element.28), channel_id=1, source_target_pairs={{0,1},{1,2},{2,3},{3,0},{4,5},{5,6},{6,7},{7,4},{8,9},{9,10},{10,1... | collective-permute-start | bytes 368648 | tf_op jit(solution)/shard_map/ppermute | solution.py:42
  17.8 1.8 %shard_map.112 = (f32[160,256]{1,0:T(8,128)S(1)}, bf16[12,8,80,128]{3,2,1,0:T(8,128)(2,1)S(1)}) custom-call(f32[2,6,144,144]{3,2,1,0:T(8,128)S(1)} %get-tuple-element.21.pupils_ref, bf16[160,640]{1,0:T(8,128)(2,1)S(1)} %get-tuple-element.25.own_ref, bf16[768,256]{1,0:T(8,128)(2,1)S(1)} %copy-done.6, bf16[6,8,80,128]{3,2,1,0:T(8,128)(2,1)S(1)} %get-tuple-element.26.quads_ref, ...), custom_call_target="tpu_custom_call" | custom-call | flops 2000000000 | bytes 4000000 | tf_op jit(solution)/shard_map/pallas_call | solution.py:463
  19.6 2.4 %collective-permute-done.2.sent_ref = bf16[160,384]{1,0:T(8,128)(2,1)S(1)} collective-permute-done((bf16[160,384]{1,0:T(8,128)(2,1)S(1)}, bf16[160,384]{1,0:T(8,128)(2,1)S(1)}, u32[]{:S(2)}, u32[]{:S(2)}) %collective-permute-start.2) | collective-permute-done | bytes 122912 | tf_op jit(solution)/shard_map/ppermute | solution.py:42
  22.0 0.0 collective-permute-done.3.other_ref
  22.0 0.0 copy-done.5
  22.1 11.3 %shard_map.113.mine_ref = bf16[160,512]{1,0:T(8,128)(2,1)S(1)} custom-call(s32[1,2]{1,0:T(1,128)S(1)} %copy-done.3, f32[160,256]{1,0:T(8,128)S(1)} %get-tuple-element.27.base_ref, bf16[160,384]{1,0:T(8,128)(2,1)S(1)} %collective-permute-done.2.sent_ref, bf16[160,128]{1,0:T(8,128)(2,1)S(1)} %get-tuple-element.29.low_ref, bf16[512,1024]{1,0:T(8,128)(2,1)S(1)} %copy-done.1, ...), custom_call_target="tpu_custom_call" | custom-call | flops 7500000256 | bytes 15000000 | tf_op jit(solution)/shard_map/pallas_call | solution.py:470
  33.3 0.1 collective-permute-start.4
  33.4 4.2 %collective-permute-done.4.sent_ref = bf16[160,512]{1,0:T(8,128)(2,1)S(1)} collective-permute-done((bf16[160,512]{1,0:T(8,128)(2,1)S(1)}, bf16[160,512]{1,0:T(8,128)(2,1)S(1)}, u32[]{:S(2)}, u32[]{:S(2)}) %collective-permute-start.4) | collective-permute-done | bytes 163872 | tf_op jit(solution)/shard_map/ppermute | solution.py:42
  37.6 0.6 %shard_map.114 = (bf16[160,1024]{1,0:T(8,128)(2,1)S(1)}, bf16[128,1024]{1,0:T(8,128)(2,1)S(1)}, bf16[128,1024]{1,0:T(8,128)(2,1)S(1)}) custom-call(bf16[160,512]{1,0:T(8,128)(2,1)S(1)} %shard_map.113.mine_ref, bf16[160,512]{1,0:T(8,128)(2,1)S(1)} %collective-permute-done.4.sent_ref, bf16[768,160]{1,0:T(8,128)(2,1)S(1)} %copy-done.4, ...), custom_call_target="tpu_custom_call" | custom-call | flops 500000000 | bytes 1000000 | tf_op jit(solution)/shard_map/pallas_call | solution.py:492
  38.1 0.1 collective-permute-start.6
  38.2 5.3 %collective-permute-start.5 = (bf16[128,1024]{1,0:T(8,128)(2,1)S(1)}, bf16[128,1024]{1,0:T(8,128)(2,1)S(1)}, u32[]{:S(2)}, u32[]{:S(2)}) collective-permute-start(bf16[128,1024]{1,0:T(8,128)(2,1)S(1)} %get-tuple-element.32), channel_id=1, source_target_pairs={{4,8},{8,4},{12,16},{16,12},{20,24},{24,20},{5,9},{9,5},{13,17},{1... | collective-permute-start | bytes 786440 | tf_op jit(solution)/shard_map/ppermute | solution.py:32
  43.5 0.0 collective-permute-done.6.near_ref
  43.5 1.7 %shard_map.115 = (f32[512,1024]{1,0:T(8,128)}, f32[128,1024]{1,0:T(8,128)S(1)}) custom-call(f32[512,1024]{1,0:T(8,128)S(1)} %copy-done, bf16[160,1024]{1,0:T(8,128)(2,1)S(1)} %get-tuple-element.33.mixed_ref, bf16[128,1024]{1,0:T(8,128)(2,1)S(1)} %collective-permute-done.6.near_ref, bf16[768,160]{1,0:T(8,128)(2,1)S(1)} %copy-done.4), custom_call_target="tpu_custom_call" | custom-call | flops 1000000000 | bytes 2000000 | tf_op jit(solution)/shard_map/pallas_call | solution.py:502
  45.3 4.6 %collective-permute-done.5.cross_ref = bf16[128,1024]{1,0:T(8,128)(2,1)S(1)} collective-permute-done((bf16[128,1024]{1,0:T(8,128)(2,1)S(1)}, bf16[128,1024]{1,0:T(8,128)(2,1)S(1)}, u32[]{:S(2)}, u32[]{:S(2)}) %collective-permute-start.5) | collective-permute-done | bytes 262176 | tf_op jit(solution)/shard_map/ppermute | solution.py:32
  49.9 0.9 %shard_map.116 = f32[512,1024]{1,0:T(8,128)} custom-call(bf16[128,1024]{1,0:T(8,128)(2,1)S(1)} %collective-permute-done.5.cross_ref, f32[128,1024]{1,0:T(8,128)S(1)} %get-tuple-element.35.rim_ref, f32[512,1024]{1,0:T(8,128)} %get-tuple-element.36.base_ref), custom_call_target="tpu_custom_call", output_to_operand_aliasing={{}: (2, {})} | custom-call | tf_op jit(solution)/shard_map/pallas_call | solution.py:511
  (10 shorter events, 0.0 us)
Async XLA Ops:
  0.0 7.9 %copy-start.7 = (bf16[160,768]{1,0:T(8,128)(2,1)S(1)}, bf16[160,768]{1,0:T(8,128)(2,1)}, u32[]{:S(2)}) copy-start(bf16[160,768]{1,0:T(8,128)(2,1)} %constant.14.clone.table_ref.row_ref) | copy-start | bytes 737284
  0.0 7.9 %copy-start.9 = (bf16[144,256]{1,0:T(8,128)(2,1)S(1)}, bf16[144,256]{1,0:T(8,128)(2,1)}, u32[]{:S(2)}) copy-start(bf16[144,256]{1,0:T(8,128)(2,1)} %constant.13.clone.col_ref) | copy-start | bytes 221188
  0.0 7.9 %copy-start.8 = (bf16[160,144]{1,0:T(8,128)(2,1)S(1)}, bf16[160,144]{1,0:T(8,128)(2,1)}, u32[]{:S(2)}) copy-start(bf16[160,144]{1,0:T(8,128)(2,1)} %constant.12.clone.row_ref) | copy-start | bytes 138244
  0.0 7.9 %copy-start = (f32[512,1024]{1,0:T(8,128)S(1)}, f32[512,1024]{1,0:T(8,128)}, u32[]{:S(2)}) copy-start(f32[512,1024]{1,0:T(8,128)} %mask_ref.5) | copy-start | bytes 6291460
  0.0 7.9 %copy-start.2 = (f32[12]{0:T(128)S(1)}, f32[12]{0:T(128)}, u32[]{:S(2)}) copy-start(f32[12]{0:T(128)} %weights_ref.3) | copy-start | bytes 148
  1.6 20.5 %collective-permute-start.3 = (bf16[512,512]{1,0:T(8,128)(2,1)S(1)}, bf16[512,512]{1,0:T(8,128)(2,1)S(1)}, u32[]{:S(2)}, u32[]{:S(2)}) collective-permute-start(bf16[512,512]{1,0:T(8,128)(2,1)S(1)} %get-tuple-element.30), channel_id=1, source_target_pairs={{0,1},{1,2},{2,3},{3,0},{4,5},{5,6},{6,7},{7,4},{8,9},{9,10},{10,1... | collective-permute-start | bytes 1572872 | tf_op jit(solution)/shard_map/ppermute | solution.py:42
  3.8 7.2 %collective-permute-start = (bf16[128,1024]{1,0:T(8,128)(2,1)S(1)}, bf16[128,1024]{1,0:T(8,128)(2,1)S(1)}, u32[]{:S(2)}, u32[]{:S(2)}) collective-permute-start(bf16[128,1024]{1,0:T(8,128)(2,1)S(1)} %get-tuple-element.23), channel_id=1, source_target_pairs={{0,4},{4,0},{8,12},{12,8},{16,20},{20,16},{24,28},{28,24},{1,5},{5... | collective-permute-start | bytes 786440 | tf_op jit(solution)/shard_map/ppermute | solution.py:32
  4.7 10.6 %copy-start.3 = (s32[1,2]{1,0:T(1,128)S(1)}, s32[1,2]{1,0:T(1,128)}, u32[]{:S(2)}) copy-start(s32[1,2]{1,0:T(1,128)} %live_ref.3) | copy-start | bytes 28
  4.7 10.6 %copy-start.6 = (bf16[768,256]{1,0:T(8,128)(2,1)S(1)}, bf16[768,256]{1,0:T(8,128)(2,1)}, u32[]{:S(2)}) copy-start(bf16[768,256]{1,0:T(8,128)(2,1)} %constant.17.clone.col_t_ref) | copy-start | bytes 1179652
  4.7 10.6 %collective-permute-start.1 = (bf16[128,1024]{1,0:T(8,128)(2,1)S(1)}, bf16[128,1024]{1,0:T(8,128)(2,1)S(1)}, u32[]{:S(2)}, u32[]{:S(2)}) collective-permute-start(bf16[128,1024]{1,0:T(8,128)(2,1)S(1)} %get-tuple-element.24), channel_id=1, source_target_pairs={{4,8},{8,4},{12,16},{16,12},{20,24},{24,20},{5,9},{9,5},{13,17},{1... | collective-permute-start | bytes 786440 | tf_op jit(solution)/shard_map/ppermute | solution.py:32
  16.5 5.6 %collective-permute-start.2 = (bf16[160,384]{1,0:T(8,128)(2,1)S(1)}, bf16[160,384]{1,0:T(8,128)(2,1)S(1)}, u32[]{:S(2)}, u32[]{:S(2)}) collective-permute-start(bf16[160,384]{1,0:T(8,128)(2,1)S(1)} %get-tuple-element.28), channel_id=1, source_target_pairs={{0,1},{1,2},{2,3},{3,0},{4,5},{5,6},{6,7},{7,4},{8,9},{9,10},{10,1... | collective-permute-start | bytes 368648 | tf_op jit(solution)/shard_map/ppermute | solution.py:42
  17.8 4.2 %copy-start.1 = (bf16[512,1024]{1,0:T(8,128)(2,1)S(1)}, bf16[512,1024]{1,0:T(8,128)(2,1)}, u32[]{:S(2)}) copy-start(bf16[512,1024]{1,0:T(8,128)(2,1)} %goal_ref.1) | copy-start | bytes 3145732
  17.8 4.2 %copy-start.4 = (bf16[768,160]{1,0:T(8,128)(2,1)S(1)}, bf16[768,160]{1,0:T(8,128)(2,1)}, u32[]{:S(2)}) copy-start(bf16[768,160]{1,0:T(8,128)(2,1)} %constant.15.clone.row_t_ref) | copy-start | bytes 737284
  17.8 4.2 %copy-start.5 = (bf16[256,768]{1,0:T(8,128)(2,1)S(1)}, bf16[256,768]{1,0:T(8,128)(2,1)}, u32[]{:S(2)}) copy-start(bf16[256,768]{1,0:T(8,128)(2,1)} %constant.16.clone.col_ref) | copy-start | bytes 1179652
  33.3 4.2 %collective-permute-start.4 = (bf16[160,512]{1,0:T(8,128)(2,1)S(1)}, bf16[160,512]{1,0:T(8,128)(2,1)S(1)}, u32[]{:S(2)}, u32[]{:S(2)}) collective-permute-start(bf16[160,512]{1,0:T(8,128)(2,1)S(1)} %shard_map.113.mine_ref), channel_id=1, source_target_pairs={{0,3},{1,0},{2,1},{3,2},{4,7},{5,4},{6,5},{7,6},{8,11},{9,8},{10,9... | collective-permute-start | bytes 491528 | tf_op jit(solution)/shard_map/ppermute | solution.py:42
  38.1 5.4 %collective-permute-start.6 = (bf16[128,1024]{1,0:T(8,128)(2,1)S(1)}, bf16[128,1024]{1,0:T(8,128)(2,1)S(1)}, u32[]{:S(2)}, u32[]{:S(2)}) collective-permute-start(bf16[128,1024]{1,0:T(8,128)(2,1)S(1)} %get-tuple-element.34), channel_id=1, source_target_pairs={{0,4},{4,0},{8,12},{12,8},{16,20},{20,16},{24,28},{28,24},{1,5},{5... | collective-permute-start | bytes 786440 | tf_op jit(solution)/shard_map/ppermute | solution.py:32
  38.2 11.7 %collective-permute-start.5 = (bf16[128,1024]{1,0:T(8,128)(2,1)S(1)}, bf16[128,1024]{1,0:T(8,128)(2,1)S(1)}, u32[]{:S(2)}, u32[]{:S(2)}) collective-permute-start(bf16[128,1024]{1,0:T(8,128)(2,1)S(1)} %get-tuple-element.32), channel_id=1, source_target_pairs={{4,8},{8,4},{12,16},{16,12},{20,24},{24,20},{5,9},{9,5},{13,17},{1... | collective-permute-start | bytes 786440 | tf_op jit(solution)/shard_map/ppermute | solution.py:32

commit v9 on v8

--- a/solution.py
+++ b/solution.py
@@ -91,7 +91,7 @@
 
 def pupil_steps(rows, lanes, first, last, pupils_ref, weights_ref, row_ref, col_ref, out_ref):
     for k in range(first, last):
-        scale = jnp.sqrt(jnp.full((1, 1), weights_ref[k] * (0.5 * steepness), jnp.float32))
+        scale = jnp.sqrt(weights_ref[:, k : k + 1] * (0.5 * steepness))
         for part in range(2):
             values = (pupils_ref[part, k - first] * scale).astype(jnp.bfloat16)
             columns = dot(values, col_ref[...]).astype(jnp.bfloat16)
@@ -157,7 +157,7 @@
     flag = (lax.broadcasted_iota(jnp.int32, shape, 0) == shape[0] - 1) & (
         lax.broadcasted_iota(jnp.int32, shape, 1) == shape[1] - 1
     )
-    live = live_ref[0, live_ref.shape[1] - 1].astype(jnp.float32)
+    live = live_ref[:, live_ref.shape[1] - 1 :].astype(jnp.float32)
     sent_ref[:, AMBIT:] = jnp.where(flag, live, main).astype(jnp.bfloat16)
 
 
@@ -219,10 +219,11 @@
     spec_ref[1] = sent_ref[:, AMBIT:].astype(jnp.float32) + dot(right, col_t_ref[extent - AMBIT :])
     corner = sent_ref[2 * rows - 16 :, AMBIT + 2 * lanes - LANE :].astype(jnp.float32)
     other_live = jnp.max(corner[15:, LANE - 1 :])
+    own_live = jnp.max(live_ref[:, :1].astype(jnp.float32))
     out_ref[...] = jnp.zeros_like(out_ref)
 
     def work(item, carry):
-        live = jnp.where(item == 0, live_ref[0, 0].astype(jnp.float32), other_live) > 0.0
+        live = jnp.where(item == 0, own_live, other_live) > 0.0
 
         @pl.when(live)
         def _():
@@ -422,7 +423,7 @@
     col_table, col_table_t = jnp.asarray(col_np, jnp.bfloat16), jnp.asarray(col_np.T, jnp.bfloat16)
     bf16, f32 = jnp.bfloat16, jnp.float32
     shape = jax.ShapeDtypeStruct
-    smem = pl.BlockSpec(memory_space=pltpu.SMEM)
+    weights = weights.reshape(1, kernels)
     early = kernels // 2
 
     hbm = pl.BlockSpec(memory_space=pltpu.HBM)
@@ -445,7 +446,7 @@
             shape((early, 8, rows, lanes), bf16),
             shape((2, kernels - early, size, size), f32),
         ),
-        [*vmem(1), hbm, *vmem(1), smem, *vmem(2)],
+        [*vmem(1), hbm, *vmem(4)],
         scratch=[pltpu.VMEM((2, early, size, size), f32), dma((2,))],
         limit=48,
         us=4,
@@ -457,20 +458,20 @@
             shape((2 * rows, AMBIT), bf16),
             shape((2 * rows, AMBIT + 2 * lanes), bf16),
         ),
-        [smem, *vmem(5)],
+        vmem(6),
     )(live, middle, near, cross, row_table, col_table_t)
     sent = turned(sending, "col", 1)
     base, all_quads = call(
         partial(late_kernel, rows, lanes, early, kernels),
         (shape((2 * rows, 2 * lanes), f32), shape((kernels, 8, rows, lanes), bf16)),
-        [*vmem(4), smem, *vmem(2)],
+        vmem(7),
         limit=16,
         us=4,
     )(rest, own, col_table_t, quads, weights, row_pick, col_pick)
     answers = call(
         partial(core_kernel, rows, lanes),
         shape((2 * rows, 4 * lanes), bf16),
-        [smem, *vmem(10)],
+        vmem(11),
         scratch=[
             pltpu.VMEM((2, 2 * rows, 2 * lanes), f32),
             pltpu.VMEM((4, 4 * rows, 2 * lanes), bf16),

time: 50.9 us -> 49.7 us (0.976)
  Pallas kernels: 21.8 us -> 19.9 us
  waiting for transfers between devices: 15.6 us -> 16.5 us
    pallas_call x1, Pallas kernels: 11.3 us -> 10.7 us  [body(): call(partial(core_kernel, rows, lanes), shape((2 * rows, 4 * lanes), bf16...]
    pallas_call x1, Pallas kernels: 1.09 us -> 0.55 us  [body(): call(partial_kernel, (shape((2 * rows, tile + AMBIT), bf16), shape((2 * r...]
  transfers between devices with their start and end apart: 7 -> 7, of which waited for: 4 -> 4; matrix products, arithmetic and copies ran while one was open for 0% -> 0% of each run, Pallas kernels for 15% -> 12%
where the time goes in v9:
time: 49.7 us; the launch traced here: 49.5 us
  Pallas kernels  19.9 us (40%)
  waiting for transfers between devices  16.5 us (33%)
  starting transfers between devices  12.9 us (26%)
    pallas_call x1, Pallas kernels, body(): call(partial(core_kernel, rows, lanes), shape((2 * rows, 4 * lanes), bf16...  10.7 us
    ppermute x4, waiting for transfers between devices, swapped(): return lax.ppermute(block, axis, pairs)  9.46 us
    ppermute x4, starting transfers between devices, swapped(): return lax.ppermute(block, axis, pairs)  9.33 us
    ppermute x3, waiting for transfers between devices, turned(): lax.ppermute(block, axis, [(i, (i + step) % count) for i in range(count)])  7.07 us
    ppermute x3, starting transfers between devices, turned(): lax.ppermute(block, axis, [(i, (i + step) % count) for i in range(count)])  3.57 us
    pallas_call x1, Pallas kernels, body(): call(partial(early_kernel, rows, lanes, early), (shape((2 * rows, width),...  2.59 us
    pallas_call x1, Pallas kernels, body(): pl.pallas_call(update_kernel, out_shape=(whole, rim), in_specs=vmem(4), o...  1.71 us
    pallas_call x1, Pallas kernels, body(): call(edges_kernel, (edge, edge, shape((tile, tile), bf16)), [hbm, hbm], s...  1.55 us
  transfers between devices with their start and end apart: 7, of which 4 were waited for; matrix products, arithmetic and copies ran while one was open for 0% of the time, Pallas kernels for 12%

profile of v9, /device:TPU:1, one launch (start us, length us, event | category | flops | bytes accessed | tf_op | source)
XLA Modules:
  0.0 49.5 jit_solution(17706070366369104158)
XLA Ops:
  0.0 0.0 copy-start
  0.0 0.0 copy-start.2
  0.0 1.5 %shard_map.110 = (bf16[128,1024]{1,0:T(8,128)(2,1)S(1)}, bf16[128,1024]{1,0:T(8,128)(2,1)S(1)}, bf16[512,512]{1,0:T(8,128)(2,1)S(1)}) custom-call(f32[512,1024]{1,0:T(8,128)} %mask_ref.5, bf16[512,1024]{1,0:T(8,128)(2,1)} %goal_ref.1), custom_call_target="tpu_custom_call" | custom-call | flops 500000000 | bytes 1000000 | tf_op jit(solution)/shard_map/pallas_call | solution.py:432
  1.6 2.2 %collective-permute-start.3 = (bf16[512,512]{1,0:T(8,128)(2,1)S(1)}, bf16[512,512]{1,0:T(8,128)(2,1)S(1)}, u32[]{:S(2)}, u32[]{:S(2)}) collective-permute-start(bf16[512,512]{1,0:T(8,128)(2,1)S(1)} %get-tuple-element.30), channel_id=1, source_target_pairs={{0,1},{1,2},{2,3},{3,0},{4,5},{5,6},{6,7},{7,4},{8,9},{9,10},{10,1... | collective-permute-start | bytes 1572872 | tf_op jit(solution)/shard_map/ppermute | solution.py:42
  3.8 1.0 %collective-permute-start = (bf16[128,1024]{1,0:T(8,128)(2,1)S(1)}, bf16[128,1024]{1,0:T(8,128)(2,1)S(1)}, u32[]{:S(2)}, u32[]{:S(2)}) collective-permute-start(bf16[128,1024]{1,0:T(8,128)(2,1)S(1)} %get-tuple-element.23), channel_id=1, source_target_pairs={{0,4},{4,0},{8,12},{12,8},{16,20},{20,16},{24,28},{28,24},{1,5},{5... | collective-permute-start | bytes 786440 | tf_op jit(solution)/shard_map/ppermute | solution.py:32
  4.7 3.0 %collective-permute-start.1 = (bf16[128,1024]{1,0:T(8,128)(2,1)S(1)}, bf16[128,1024]{1,0:T(8,128)(2,1)S(1)}, u32[]{:S(2)}, u32[]{:S(2)}) collective-permute-start(bf16[128,1024]{1,0:T(8,128)(2,1)S(1)} %get-tuple-element.24), channel_id=1, source_target_pairs={{4,8},{8,4},{12,16},{16,12},{20,24},{24,20},{5,9},{9,5},{13,17},{1... | collective-permute-start | bytes 786440 | tf_op jit(solution)/shard_map/ppermute | solution.py:32
  7.7 0.0 copy-done.7
  7.7 0.0 copy-done.9
  7.7 0.0 copy-done.8
  7.7 0.0 copy-done
  7.8 0.0 copy-done.2
  7.8 0.0 copy-start.3
  7.8 0.0 copy-start.6
  7.8 2.6 %shard_map.109 = (f32[160,1024]{1,0:T(8,128)S(1)}, bf16[6,8,80,128]{3,2,1,0:T(8,128)(2,1)S(1)}, f32[2,6,144,144]{3,2,1,0:T(8,128)S(1)}) custom-call(f32[512,1024]{1,0:T(8,128)S(1)} %copy-done, f32[2,12,144,144]{3,2,1,0:T(8,128)} %pupils_ref.1, bf16[160,768]{1,0:T(8,128)(2,1)S(1)} %copy-done.7, f32[1,12]{1,0:T(1,128)S(1)} %bitcast.1, ...), custom_call_target="tpu_custom_call" | custom-call | flops 2000000000 | bytes 4000000 | tf_op jit(solution)/shard_map/pallas_call | solution.py:442
  10.4 0.0 collective-permute-done.near_ref
  10.4 4.8 %collective-permute-done.1.cross_ref = bf16[128,1024]{1,0:T(8,128)(2,1)S(1)} collective-permute-done((bf16[128,1024]{1,0:T(8,128)(2,1)S(1)}, bf16[128,1024]{1,0:T(8,128)(2,1)S(1)}, u32[]{:S(2)}, u32[]{:S(2)}) %collective-permute-start.1) | collective-permute-done | bytes 262176 | tf_op jit(solution)/shard_map/ppermute | solution.py:32
  15.2 0.6 %shard_map.111 = (bf16[160,640]{1,0:T(8,128)(2,1)S(1)}, bf16[160,128]{1,0:T(8,128)(2,1)S(1)}, bf16[160,384]{1,0:T(8,128)(2,1)S(1)}) custom-call(s32[1,2]{1,0:T(1,128)S(1)} %copy-done.3, f32[160,1024]{1,0:T(8,128)S(1)} %get-tuple-element.22.mid_ref, bf16[128,1024]{1,0:T(8,128)(2,1)S(1)} %collective-permute-done.near_ref, ...), custom_call_target="tpu_custom_call" | custom-call | flops 500000000 | bytes 1000000 | tf_op jit(solution)/shard_map/pallas_call | solution.py:454
  15.8 1.3 %collective-permute-start.2 = (bf16[160,384]{1,0:T(8,128)(2,1)S(1)}, bf16[160,384]{1,0:T(8,128)(2,1)S(1)}, u32[]{:S(2)}, u32[]{:S(2)}) collective-permute-start(bf16[160,384]{1,0:T(8,128)(2,1)S(1)} %get-tuple-element.28), channel_id=1, source_target_pairs={{0,1},{1,2},{2,3},{3,0},{4,5},{5,6},{6,7},{7,4},{8,9},{9,10},{10,1... | collective-permute-start | bytes 368648 | tf_op jit(solution)/shard_map/ppermute | solution.py:42
  17.1 1.3 %shard_map.112 = (f32[160,256]{1,0:T(8,128)S(1)}, bf16[12,8,80,128]{3,2,1,0:T(8,128)(2,1)S(1)}) custom-call(f32[2,6,144,144]{3,2,1,0:T(8,128)S(1)} %get-tuple-element.21.pupils_ref, bf16[160,640]{1,0:T(8,128)(2,1)S(1)} %get-tuple-element.25.own_ref, bf16[768,256]{1,0:T(8,128)(2,1)S(1)} %copy-done.6, bf16[6,8,80,128]{3,2,1,0:T(8,128)(2,1)S(1)} %get-tuple-element.26.quads_ref, ...), custom_call_target="tpu_custom_call" | custom-call | flops 2000000000 | bytes 4000000 | tf_op jit(solution)/shard_map/pallas_call | solution.py:464
  18.5 2.9 %collective-permute-done.2.sent_ref = bf16[160,384]{1,0:T(8,128)(2,1)S(1)} collective-permute-done((bf16[160,384]{1,0:T(8,128)(2,1)S(1)}, bf16[160,384]{1,0:T(8,128)(2,1)S(1)}, u32[]{:S(2)}, u32[]{:S(2)}) %collective-permute-start.2) | collective-permute-done | bytes 122912 | tf_op jit(solution)/shard_map/ppermute | solution.py:42
  21.4 0.0 collective-permute-done.3.other_ref
  21.4 0.0 copy-done.5
  21.4 10.7 %shard_map.113.mine_ref = bf16[160,512]{1,0:T(8,128)(2,1)S(1)} custom-call(s32[1,2]{1,0:T(1,128)S(1)} %copy-done.3, f32[160,256]{1,0:T(8,128)S(1)} %get-tuple-element.27.base_ref, bf16[160,384]{1,0:T(8,128)(2,1)S(1)} %collective-permute-done.2.sent_ref, bf16[160,128]{1,0:T(8,128)(2,1)S(1)} %get-tuple-element.29.low_ref, bf16[512,1024]{1,0:T(8,128)(2,1)S(1)} %copy-done.1, ...), custom_call_target="tpu_custom_call" | custom-call | flops 7500000256 | bytes 15000000 | tf_op jit(solution)/shard_map/pallas_call | solution.py:471
  32.1 0.1 collective-permute-start.4
  32.2 4.2 %collective-permute-done.4.sent_ref = bf16[160,512]{1,0:T(8,128)(2,1)S(1)} collective-permute-done((bf16[160,512]{1,0:T(8,128)(2,1)S(1)}, bf16[160,512]{1,0:T(8,128)(2,1)S(1)}, u32[]{:S(2)}, u32[]{:S(2)}) %collective-permute-start.4) | collective-permute-done | bytes 163872 | tf_op jit(solution)/shard_map/ppermute | solution.py:42
  36.3 0.6 %shard_map.114 = (bf16[160,1024]{1,0:T(8,128)(2,1)S(1)}, bf16[128,1024]{1,0:T(8,128)(2,1)S(1)}, bf16[128,1024]{1,0:T(8,128)(2,1)S(1)}) custom-call(bf16[160,512]{1,0:T(8,128)(2,1)S(1)} %shard_map.113.mine_ref, bf16[160,512]{1,0:T(8,128)(2,1)S(1)} %collective-permute-done.4.sent_ref, bf16[768,160]{1,0:T(8,128)(2,1)S(1)} %copy-done.4, ...), custom_call_target="tpu_custom_call" | custom-call | flops 500000000 | bytes 1000000 | tf_op jit(solution)/shard_map/pallas_call | solution.py:493
  36.9 0.1 collective-permute-start.6
  37.0 5.3 %collective-permute-start.5 = (bf16[128,1024]{1,0:T(8,128)(2,1)S(1)}, bf16[128,1024]{1,0:T(8,128)(2,1)S(1)}, u32[]{:S(2)}, u32[]{:S(2)}) collective-permute-start(bf16[128,1024]{1,0:T(8,128)(2,1)S(1)} %get-tuple-element.32), channel_id=1, source_target_pairs={{4,8},{8,4},{12,16},{16,12},{20,24},{24,20},{5,9},{9,5},{13,17},{1... | collective-permute-start | bytes 786440 | tf_op jit(solution)/shard_map/ppermute | solution.py:32
  42.3 0.0 collective-permute-done.6.near_ref
  42.3 1.7 %shard_map.115 = (f32[512,1024]{1,0:T(8,128)}, f32[128,1024]{1,0:T(8,128)S(1)}) custom-call(f32[512,1024]{1,0:T(8,128)S(1)} %copy-done, bf16[160,1024]{1,0:T(8,128)(2,1)S(1)} %get-tuple-element.33.mixed_ref, bf16[128,1024]{1,0:T(8,128)(2,1)S(1)} %collective-permute-done.6.near_ref, bf16[768,160]{1,0:T(8,128)(2,1)S(1)} %copy-done.4), custom_call_target="tpu_custom_call" | custom-call | flops 1000000000 | bytes 2000000 | tf_op jit(solution)/shard_map/pallas_call | solution.py:503
  44.0 4.6 %collective-permute-done.5.cross_ref = bf16[128,1024]{1,0:T(8,128)(2,1)S(1)} collective-permute-done((bf16[128,1024]{1,0:T(8,128)(2,1)S(1)}, bf16[128,1024]{1,0:T(8,128)(2,1)S(1)}, u32[]{:S(2)}, u32[]{:S(2)}) %collective-permute-start.5) | collective-permute-done | bytes 262176 | tf_op jit(solution)/shard_map/ppermute | solution.py:32
  48.7 0.9 %shard_map.116 = f32[512,1024]{1,0:T(8,128)} custom-call(bf16[128,1024]{1,0:T(8,128)(2,1)S(1)} %collective-permute-done.5.cross_ref, f32[128,1024]{1,0:T(8,128)S(1)} %get-tuple-element.35.rim_ref, f32[512,1024]{1,0:T(8,128)} %get-tuple-element.36.base_ref), custom_call_target="tpu_custom_call", output_to_operand_aliasing={{}: (2, {})} | custom-call | tf_op jit(solution)/shard_map/pallas_call | solution.py:512
  (10 shorter events, 0.0 us)
Async XLA Ops:
  0.0 7.7 %copy-start.7 = (bf16[160,768]{1,0:T(8,128)(2,1)S(1)}, bf16[160,768]{1,0:T(8,128)(2,1)}, u32[]{:S(2)}) copy-start(bf16[160,768]{1,0:T(8,128)(2,1)} %constant.14.clone.table_ref.row_ref) | copy-start | bytes 737284
  0.0 7.7 %copy-start.9 = (bf16[144,256]{1,0:T(8,128)(2,1)S(1)}, bf16[144,256]{1,0:T(8,128)(2,1)}, u32[]{:S(2)}) copy-start(bf16[144,256]{1,0:T(8,128)(2,1)} %constant.13.clone.col_ref) | copy-start | bytes 221188
  0.0 7.7 %copy-start.8 = (bf16[160,144]{1,0:T(8,128)(2,1)S(1)}, bf16[160,144]{1,0:T(8,128)(2,1)}, u32[]{:S(2)}) copy-start(bf16[160,144]{1,0:T(8,128)(2,1)} %constant.12.clone.row_ref) | copy-start | bytes 138244
  0.0 7.7 %copy-start = (f32[512,1024]{1,0:T(8,128)S(1)}, f32[512,1024]{1,0:T(8,128)}, u32[]{:S(2)}) copy-start(f32[512,1024]{1,0:T(8,128)} %mask_ref.5) | copy-start | bytes 6291460
  0.0 7.7 %copy-start.2 = (f32[12]{0:T(128)S(1)}, f32[12]{0:T(128)}, u32[]{:S(2)}) copy-start(f32[12]{0:T(128)} %param.15) | copy-start | bytes 148
  1.6 19.8 %collective-permute-start.3 = (bf16[512,512]{1,0:T(8,128)(2,1)S(1)}, bf16[512,512]{1,0:T(8,128)(2,1)S(1)}, u32[]{:S(2)}, u32[]{:S(2)}) collective-permute-start(bf16[512,512]{1,0:T(8,128)(2,1)S(1)} %get-tuple-element.30), channel_id=1, source_target_pairs={{0,1},{1,2},{2,3},{3,0},{4,5},{5,6},{6,7},{7,4},{8,9},{9,10},{10,1... | collective-permute-start | bytes 1572872 | tf_op jit(solution)/shard_map/ppermute | solution.py:42
  3.8 6.6 %collective-permute-start = (bf16[128,1024]{1,0:T(8,128)(2,1)S(1)}, bf16[128,1024]{1,0:T(8,128)(2,1)S(1)}, u32[]{:S(2)}, u32[]{:S(2)}) collective-permute-start(bf16[128,1024]{1,0:T(8,128)(2,1)S(1)} %get-tuple-element.23), channel_id=1, source_target_pairs={{0,4},{4,0},{8,12},{12,8},{16,20},{20,16},{24,28},{28,24},{1,5},{5... | collective-permute-start | bytes 786440 | tf_op jit(solution)/shard_map/ppermute | solution.py:32
  4.7 10.5 %collective-permute-start.1 = (bf16[128,1024]{1,0:T(8,128)(2,1)S(1)}, bf16[128,1024]{1,0:T(8,128)(2,1)S(1)}, u32[]{:S(2)}, u32[]{:S(2)}) collective-permute-start(bf16[128,1024]{1,0:T(8,128)(2,1)S(1)} %get-tuple-element.24), channel_id=1, source_target_pairs={{4,8},{8,4},{12,16},{16,12},{20,24},{24,20},{5,9},{9,5},{13,17},{1... | collective-permute-start | bytes 786440 | tf_op jit(solution)/shard_map/ppermute | solution.py:32
  7.8 7.5 %copy-start.3 = (s32[1,2]{1,0:T(1,128)S(1)}, s32[1,2]{1,0:T(1,128)}, u32[]{:S(2)}) copy-start(s32[1,2]{1,0:T(1,128)} %live_ref.3) | copy-start | bytes 28
  7.8 7.4 %copy-start.6 = (bf16[768,256]{1,0:T(8,128)(2,1)S(1)}, bf16[768,256]{1,0:T(8,128)(2,1)}, u32[]{:S(2)}) copy-start(bf16[768,256]{1,0:T(8,128)(2,1)} %constant.17.clone.col_t_ref) | copy-start | bytes 1179652
  15.8 5.6 %collective-permute-start.2 = (bf16[160,384]{1,0:T(8,128)(2,1)S(1)}, bf16[160,384]{1,0:T(8,128)(2,1)S(1)}, u32[]{:S(2)}, u32[]{:S(2)}) collective-permute-start(bf16[160,384]{1,0:T(8,128)(2,1)S(1)} %get-tuple-element.28), channel_id=1, source_target_pairs={{0,1},{1,2},{2,3},{3,0},{4,5},{5,6},{6,7},{7,4},{8,9},{9,10},{10,1... | collective-permute-start | bytes 368648 | tf_op jit(solution)/shard_map/ppermute | solution.py:42
  17.1 4.2 %copy-start.1 = (bf16[512,1024]{1,0:T(8,128)(2,1)S(1)}, bf16[512,1024]{1,0:T(8,128)(2,1)}, u32[]{:S(2)}) copy-start(bf16[512,1024]{1,0:T(8,128)(2,1)} %goal_ref.1) | copy-start | bytes 3145732
  17.1 4.2 %copy-start.4 = (bf16[768,160]{1,0:T(8,128)(2,1)S(1)}, bf16[768,160]{1,0:T(8,128)(2,1)}, u32[]{:S(2)}) copy-start(bf16[768,160]{1,0:T(8,128)(2,1)} %constant.15.clone.row_t_ref) | copy-start | bytes 737284
  17.1 4.2 %copy-start.5 = (bf16[256,768]{1,0:T(8,128)(2,1)S(1)}, bf16[256,768]{1,0:T(8,128)(2,1)}, u32[]{:S(2)}) copy-start(bf16[256,768]{1,0:T(8,128)(2,1)} %constant.16.clone.col_ref) | copy-start | bytes 1179652
  32.1 4.2 %collective-permute-start.4 = (bf16[160,512]{1,0:T(8,128)(2,1)S(1)}, bf16[160,512]{1,0:T(8,128)(2,1)S(1)}, u32[]{:S(2)}, u32[]{:S(2)}) collective-permute-start(bf16[160,512]{1,0:T(8,128)(2,1)S(1)} %shard_map.113.mine_ref), channel_id=1, source_target_pairs={{0,3},{1,0},{2,1},{3,2},{4,7},{5,4},{6,5},{7,6},{8,11},{9,8},{10,9... | collective-permute-start | bytes 491528 | tf_op jit(solution)/shard_map/ppermute | solution.py:42
  36.9 5.4 %collective-permute-start.6 = (bf16[128,1024]{1,0:T(8,128)(2,1)S(1)}, bf16[128,1024]{1,0:T(8,128)(2,1)S(1)}, u32[]{:S(2)}, u32[]{:S(2)}) collective-permute-start(bf16[128,1024]{1,0:T(8,128)(2,1)S(1)} %get-tuple-element.34), channel_id=1, source_target_pairs={{0,4},{4,0},{8,12},{12,8},{16,20},{20,16},{24,28},{28,24},{1,5},{5... | collective-permute-start | bytes 786440 | tf_op jit(solution)/shard_map/ppermute | solution.py:32
  37.0 11.7 %collective-permute-start.5 = (bf16[128,1024]{1,0:T(8,128)(2,1)S(1)}, bf16[128,1024]{1,0:T(8,128)(2,1)S(1)}, u32[]{:S(2)}, u32[]{:S(2)}) collective-permute-start(bf16[128,1024]{1,0:T(8,128)(2,1)S(1)} %get-tuple-element.32), channel_id=1, source_target_pairs={{4,8},{8,4},{12,16},{16,12},{20,24},{24,20},{5,9},{9,5},{13,17},{1... | collective-permute-start | bytes 786440 | tf_op jit(solution)/shard_map/ppermute | solution.py:32

commit v10 on v9

--- a/solution.py
+++ b/solution.py
@@ -402,10 +402,20 @@
 
 def rim_kernel(cross_ref, rim_ref, base_ref, out_ref, stage_ref, sem):
     start = sides(out_ref.shape[0] - AMBIT)[1]
-    stage_ref[...] = rim_ref[...] - step_rate * cross_ref[...].astype(jnp.float32)
-    copy = pltpu.make_async_copy(stage_ref, out_ref.at[pl.ds(start, AMBIT)], sem)
-    copy.start()
-    copy.wait()
+    step = AMBIT // 2
+    copies = []
+    for index in range(2):
+        where = pl.ds(index * step, step)
+        stage_ref[where] = rim_ref[where] - step_rate * cross_ref[where].astype(jnp.float32)
+        copy = pltpu.make_async_copy(
+            stage_ref.at[where],
+            out_ref.at[pl.ds(pl.multiple_of(start + index * step, step), step)],
+            sem.at[index],
+        )
+        copy.start()
+        copies.append(copy)
+    for copy in copies:
+        copy.wait()
 
 
 def body(mask, target, live, pupils, weights):
@@ -514,7 +524,7 @@
         out_shape=whole,
         in_specs=[*vmem(2), anywhere],
         out_specs=anywhere,
-        scratch_shapes=[pltpu.VMEM((AMBIT, width), f32), dma],
+        scratch_shapes=[pltpu.VMEM((AMBIT, width), f32), dma((2,))],
         input_output_aliases={2: 0},
         compiler_params=pltpu.CompilerParams(vmem_limit_bytes=8 * MIB),
     )(cross, rim, updated)

time: 49.7 us -> 49.7 us (level)
  no operation moved by 1% of the time
where the time goes in v10:
time: 49.7 us; the launch traced here: 49.5 us
  Pallas kernels  19.8 us (40%)
  waiting for transfers between devices  16.5 us (33%)
  starting transfers between devices  12.9 us (26%)
    pallas_call x1, Pallas kernels, body(): call(partial(core_kernel, rows, lanes), shape((2 * rows, 4 * lanes), bf16...  10.7 us
    ppermute x4, waiting for transfers between devices, swapped(): return lax.ppermute(block, axis, pairs)  9.46 us
    ppermute x4, starting transfers between devices, swapped(): return lax.ppermute(block, axis, pairs)  9.33 us
    ppermute x3, waiting for transfers between devices, turned(): lax.ppermute(block, axis, [(i, (i + step) % count) for i in range(count)])  7.07 us
    ppermute x3, starting transfers between devices, turned(): lax.ppermute(block, axis, [(i, (i + step) % count) for i in range(count)])  3.57 us
    pallas_call x1, Pallas kernels, body(): call(partial(early_kernel, rows, lanes, early), (shape((2 * rows, width),...  2.59 us
    pallas_call x1, Pallas kernels, body(): pl.pallas_call(update_kernel, out_shape=(whole, rim), in_specs=vmem(4), o...  1.71 us
    pallas_call x1, Pallas kernels, body(): call(edges_kernel, (edge, edge, shape((tile, tile), bf16)), [hbm, hbm], s...  1.55 us
  transfers between devices with their start and end apart: 7, of which 4 were waited for; matrix products, arithmetic and copies ran while one was open for 0% of the time, Pallas kernels for 12%

profile of v10, /device:TPU:1, one launch (start us, length us, event | category | flops | bytes accessed | tf_op | source)
XLA Modules:
  0.0 49.5 jit_solution(5323928661141996059)
XLA Ops:
  0.0 0.0 copy-start
  0.0 0.0 copy-start.2
  0.0 1.5 %shard_map.110 = (bf16[128,1024]{1,0:T(8,128)(2,1)S(1)}, bf16[128,1024]{1,0:T(8,128)(2,1)S(1)}, bf16[512,512]{1,0:T(8,128)(2,1)S(1)}) custom-call(f32[512,1024]{1,0:T(8,128)} %mask_ref.5, bf16[512,1024]{1,0:T(8,128)(2,1)} %goal_ref.1), custom_call_target="tpu_custom_call" | custom-call | flops 500000000 | bytes 1000000 | tf_op jit(solution)/shard_map/pallas_call | solution.py:442
  1.6 2.2 %collective-permute-start.3 = (bf16[512,512]{1,0:T(8,128)(2,1)S(1)}, bf16[512,512]{1,0:T(8,128)(2,1)S(1)}, u32[]{:S(2)}, u32[]{:S(2)}) collective-permute-start(bf16[512,512]{1,0:T(8,128)(2,1)S(1)} %get-tuple-element.30), channel_id=1, source_target_pairs={{0,1},{1,2},{2,3},{3,0},{4,5},{5,6},{6,7},{7,4},{8,9},{9,10},{10,1... | collective-permute-start | bytes 1572872 | tf_op jit(solution)/shard_map/ppermute | solution.py:42
  3.8 1.0 %collective-permute-start = (bf16[128,1024]{1,0:T(8,128)(2,1)S(1)}, bf16[128,1024]{1,0:T(8,128)(2,1)S(1)}, u32[]{:S(2)}, u32[]{:S(2)}) collective-permute-start(bf16[128,1024]{1,0:T(8,128)(2,1)S(1)} %get-tuple-element.23), channel_id=1, source_target_pairs={{0,4},{4,0},{8,12},{12,8},{16,20},{20,16},{24,28},{28,24},{1,5},{5... | collective-permute-start | bytes 786440 | tf_op jit(solution)/shard_map/ppermute | solution.py:32
  4.7 3.0 %collective-permute-start.1 = (bf16[128,1024]{1,0:T(8,128)(2,1)S(1)}, bf16[128,1024]{1,0:T(8,128)(2,1)S(1)}, u32[]{:S(2)}, u32[]{:S(2)}) collective-permute-start(bf16[128,1024]{1,0:T(8,128)(2,1)S(1)} %get-tuple-element.24), channel_id=1, source_target_pairs={{4,8},{8,4},{12,16},{16,12},{20,24},{24,20},{5,9},{9,5},{13,17},{1... | collective-permute-start | bytes 786440 | tf_op jit(solution)/shard_map/ppermute | solution.py:32
  7.7 0.0 copy-done.7
  7.7 0.0 copy-done.9
  7.7 0.0 copy-done.8
  7.7 0.0 copy-done
  7.8 0.0 copy-done.2
  7.8 0.0 copy-start.3
  7.8 0.0 copy-start.6
  7.8 2.6 %shard_map.109 = (f32[160,1024]{1,0:T(8,128)S(1)}, bf16[6,8,80,128]{3,2,1,0:T(8,128)(2,1)S(1)}, f32[2,6,144,144]{3,2,1,0:T(8,128)S(1)}) custom-call(f32[512,1024]{1,0:T(8,128)S(1)} %copy-done, f32[2,12,144,144]{3,2,1,0:T(8,128)} %pupils_ref.1, bf16[160,768]{1,0:T(8,128)(2,1)S(1)} %copy-done.7, f32[1,12]{1,0:T(1,128)S(1)} %bitcast.1, ...), custom_call_target="tpu_custom_call" | custom-call | flops 2000000000 | bytes 4000000 | tf_op jit(solution)/shard_map/pallas_call | solution.py:452
  10.4 0.0 collective-permute-done.near_ref
  10.4 4.8 %collective-permute-done.1.cross_ref = bf16[128,1024]{1,0:T(8,128)(2,1)S(1)} collective-permute-done((bf16[128,1024]{1,0:T(8,128)(2,1)S(1)}, bf16[128,1024]{1,0:T(8,128)(2,1)S(1)}, u32[]{:S(2)}, u32[]{:S(2)}) %collective-permute-start.1) | collective-permute-done | bytes 262176 | tf_op jit(solution)/shard_map/ppermute | solution.py:32
  15.2 0.6 %shard_map.111 = (bf16[160,640]{1,0:T(8,128)(2,1)S(1)}, bf16[160,128]{1,0:T(8,128)(2,1)S(1)}, bf16[160,384]{1,0:T(8,128)(2,1)S(1)}) custom-call(s32[1,2]{1,0:T(1,128)S(1)} %copy-done.3, f32[160,1024]{1,0:T(8,128)S(1)} %get-tuple-element.22.mid_ref, bf16[128,1024]{1,0:T(8,128)(2,1)S(1)} %collective-permute-done.near_ref, ...), custom_call_target="tpu_custom_call" | custom-call | flops 500000000 | bytes 1000000 | tf_op jit(solution)/shard_map/pallas_call | solution.py:464
  15.8 1.3 %collective-permute-start.2 = (bf16[160,384]{1,0:T(8,128)(2,1)S(1)}, bf16[160,384]{1,0:T(8,128)(2,1)S(1)}, u32[]{:S(2)}, u32[]{:S(2)}) collective-permute-start(bf16[160,384]{1,0:T(8,128)(2,1)S(1)} %get-tuple-element.28), channel_id=1, source_target_pairs={{0,1},{1,2},{2,3},{3,0},{4,5},{5,6},{6,7},{7,4},{8,9},{9,10},{10,1... | collective-permute-start | bytes 368648 | tf_op jit(solution)/shard_map/ppermute | solution.py:42
  17.1 1.3 %shard_map.112 = (f32[160,256]{1,0:T(8,128)S(1)}, bf16[12,8,80,128]{3,2,1,0:T(8,128)(2,1)S(1)}) custom-call(f32[2,6,144,144]{3,2,1,0:T(8,128)S(1)} %get-tuple-element.21.pupils_ref, bf16[160,640]{1,0:T(8,128)(2,1)S(1)} %get-tuple-element.25.own_ref, bf16[768,256]{1,0:T(8,128)(2,1)S(1)} %copy-done.6, bf16[6,8,80,128]{3,2,1,0:T(8,128)(2,1)S(1)} %get-tuple-element.26.quads_ref, ...), custom_call_target="tpu_custom_call" | custom-call | flops 2000000000 | bytes 4000000 | tf_op jit(solution)/shard_map/pallas_call | solution.py:474
  18.5 2.9 %collective-permute-done.2.sent_ref = bf16[160,384]{1,0:T(8,128)(2,1)S(1)} collective-permute-done((bf16[160,384]{1,0:T(8,128)(2,1)S(1)}, bf16[160,384]{1,0:T(8,128)(2,1)S(1)}, u32[]{:S(2)}, u32[]{:S(2)}) %collective-permute-start.2) | collective-permute-done | bytes 122912 | tf_op jit(solution)/shard_map/ppermute | solution.py:42
  21.4 0.0 collective-permute-done.3.other_ref
  21.4 0.0 copy-done.5
  21.4 10.7 %shard_map.113.mine_ref = bf16[160,512]{1,0:T(8,128)(2,1)S(1)} custom-call(s32[1,2]{1,0:T(1,128)S(1)} %copy-done.3, f32[160,256]{1,0:T(8,128)S(1)} %get-tuple-element.27.base_ref, bf16[160,384]{1,0:T(8,128)(2,1)S(1)} %collective-permute-done.2.sent_ref, bf16[160,128]{1,0:T(8,128)(2,1)S(1)} %get-tuple-element.29.low_ref, bf16[512,1024]{1,0:T(8,128)(2,1)S(1)} %copy-done.1, ...), custom_call_target="tpu_custom_call" | custom-call | flops 7500000256 | bytes 15000000 | tf_op jit(solution)/shard_map/pallas_call | solution.py:481
  32.1 0.1 collective-permute-start.4
  32.2 4.2 %collective-permute-done.4.sent_ref = bf16[160,512]{1,0:T(8,128)(2,1)S(1)} collective-permute-done((bf16[160,512]{1,0:T(8,128)(2,1)S(1)}, bf16[160,512]{1,0:T(8,128)(2,1)S(1)}, u32[]{:S(2)}, u32[]{:S(2)}) %collective-permute-start.4) | collective-permute-done | bytes 163872 | tf_op jit(solution)/shard_map/ppermute | solution.py:42
  36.3 0.6 %shard_map.114 = (bf16[160,1024]{1,0:T(8,128)(2,1)S(1)}, bf16[128,1024]{1,0:T(8,128)(2,1)S(1)}, bf16[128,1024]{1,0:T(8,128)(2,1)S(1)}) custom-call(bf16[160,512]{1,0:T(8,128)(2,1)S(1)} %shard_map.113.mine_ref, bf16[160,512]{1,0:T(8,128)(2,1)S(1)} %collective-permute-done.4.sent_ref, bf16[768,160]{1,0:T(8,128)(2,1)S(1)} %copy-done.4, ...), custom_call_target="tpu_custom_call" | custom-call | flops 500000000 | bytes 1000000 | tf_op jit(solution)/shard_map/pallas_call | solution.py:503
  36.9 0.1 collective-permute-start.6
  37.0 5.3 %collective-permute-start.5 = (bf16[128,1024]{1,0:T(8,128)(2,1)S(1)}, bf16[128,1024]{1,0:T(8,128)(2,1)S(1)}, u32[]{:S(2)}, u32[]{:S(2)}) collective-permute-start(bf16[128,1024]{1,0:T(8,128)(2,1)S(1)} %get-tuple-element.32), channel_id=1, source_target_pairs={{4,8},{8,4},{12,16},{16,12},{20,24},{24,20},{5,9},{9,5},{13,17},{1... | collective-permute-start | bytes 786440 | tf_op jit(solution)/shard_map/ppermute | solution.py:32
  42.3 0.0 collective-permute-done.6.near_ref
  42.3 1.7 %shard_map.115 = (f32[512,1024]{1,0:T(8,128)}, f32[128,1024]{1,0:T(8,128)S(1)}) custom-call(f32[512,1024]{1,0:T(8,128)S(1)} %copy-done, bf16[160,1024]{1,0:T(8,128)(2,1)S(1)} %get-tuple-element.33.mixed_ref, bf16[128,1024]{1,0:T(8,128)(2,1)S(1)} %collective-permute-done.6.near_ref, bf16[768,160]{1,0:T(8,128)(2,1)S(1)} %copy-done.4), custom_call_target="tpu_custom_call" | custom-call | flops 1000000000 | bytes 2000000 | tf_op jit(solution)/shard_map/pallas_call | solution.py:513
  44.0 4.6 %collective-permute-done.5.cross_ref = bf16[128,1024]{1,0:T(8,128)(2,1)S(1)} collective-permute-done((bf16[128,1024]{1,0:T(8,128)(2,1)S(1)}, bf16[128,1024]{1,0:T(8,128)(2,1)S(1)}, u32[]{:S(2)}, u32[]{:S(2)}) %collective-permute-start.5) | collective-permute-done | bytes 262176 | tf_op jit(solution)/shard_map/ppermute | solution.py:32
  48.7 0.8 %shard_map.116 = f32[512,1024]{1,0:T(8,128)} custom-call(bf16[128,1024]{1,0:T(8,128)(2,1)S(1)} %collective-permute-done.5.cross_ref, f32[128,1024]{1,0:T(8,128)S(1)} %get-tuple-element.35.rim_ref, f32[512,1024]{1,0:T(8,128)} %get-tuple-element.36.base_ref), custom_call_target="tpu_custom_call", output_to_operand_aliasing={{}: (2, {})} | custom-call | tf_op jit(solution)/shard_map/pallas_call | solution.py:522
  (10 shorter events, 0.0 us)
Async XLA Ops:
  0.0 7.7 %copy-start.7 = (bf16[160,768]{1,0:T(8,128)(2,1)S(1)}, bf16[160,768]{1,0:T(8,128)(2,1)}, u32[]{:S(2)}) copy-start(bf16[160,768]{1,0:T(8,128)(2,1)} %constant.14.clone.table_ref.row_ref) | copy-start | bytes 737284
  0.0 7.7 %copy-start.9 = (bf16[144,256]{1,0:T(8,128)(2,1)S(1)}, bf16[144,256]{1,0:T(8,128)(2,1)}, u32[]{:S(2)}) copy-start(bf16[144,256]{1,0:T(8,128)(2,1)} %constant.13.clone.col_ref) | copy-start | bytes 221188
  0.0 7.7 %copy-start.8 = (bf16[160,144]{1,0:T(8,128)(2,1)S(1)}, bf16[160,144]{1,0:T(8,128)(2,1)}, u32[]{:S(2)}) copy-start(bf16[160,144]{1,0:T(8,128)(2,1)} %constant.12.clone.row_ref) | copy-start | bytes 138244
  0.0 7.7 %copy-start = (f32[512,1024]{1,0:T(8,128)S(1)}, f32[512,1024]{1,0:T(8,128)}, u32[]{:S(2)}) copy-start(f32[512,1024]{1,0:T(8,128)} %mask_ref.5) | copy-start | bytes 6291460
  0.0 7.7 %copy-start.2 = (f32[12]{0:T(128)S(1)}, f32[12]{0:T(128)}, u32[]{:S(2)}) copy-start(f32[12]{0:T(128)} %param.15) | copy-start | bytes 148
  1.6 19.8 %collective-permute-start.3 = (bf16[512,512]{1,0:T(8,128)(2,1)S(1)}, bf16[512,512]{1,0:T(8,128)(2,1)S(1)}, u32[]{:S(2)}, u32[]{:S(2)}) collective-permute-start(bf16[512,512]{1,0:T(8,128)(2,1)S(1)} %get-tuple-element.30), channel_id=1, source_target_pairs={{0,1},{1,2},{2,3},{3,0},{4,5},{5,6},{6,7},{7,4},{8,9},{9,10},{10,1... | collective-permute-start | bytes 1572872 | tf_op jit(solution)/shard_map/ppermute | solution.py:42
  3.8 6.6 %collective-permute-start = (bf16[128,1024]{1,0:T(8,128)(2,1)S(1)}, bf16[128,1024]{1,0:T(8,128)(2,1)S(1)}, u32[]{:S(2)}, u32[]{:S(2)}) collective-permute-start(bf16[128,1024]{1,0:T(8,128)(2,1)S(1)} %get-tuple-element.23), channel_id=1, source_target_pairs={{0,4},{4,0},{8,12},{12,8},{16,20},{20,16},{24,28},{28,24},{1,5},{5... | collective-permute-start | bytes 786440 | tf_op jit(solution)/shard_map/ppermute | solution.py:32
  4.7 10.5 %collective-permute-start.1 = (bf16[128,1024]{1,0:T(8,128)(2,1)S(1)}, bf16[128,1024]{1,0:T(8,128)(2,1)S(1)}, u32[]{:S(2)}, u32[]{:S(2)}) collective-permute-start(bf16[128,1024]{1,0:T(8,128)(2,1)S(1)} %get-tuple-element.24), channel_id=1, source_target_pairs={{4,8},{8,4},{12,16},{16,12},{20,24},{24,20},{5,9},{9,5},{13,17},{1... | collective-permute-start | bytes 786440 | tf_op jit(solution)/shard_map/ppermute | solution.py:32
  7.8 7.5 %copy-start.3 = (s32[1,2]{1,0:T(1,128)S(1)}, s32[1,2]{1,0:T(1,128)}, u32[]{:S(2)}) copy-start(s32[1,2]{1,0:T(1,128)} %live_ref.3) | copy-start | bytes 28
  7.8 7.4 %copy-start.6 = (bf16[768,256]{1,0:T(8,128)(2,1)S(1)}, bf16[768,256]{1,0:T(8,128)(2,1)}, u32[]{:S(2)}) copy-start(bf16[768,256]{1,0:T(8,128)(2,1)} %constant.17.clone.col_t_ref) | copy-start | bytes 1179652
  15.8 5.6 %collective-permute-start.2 = (bf16[160,384]{1,0:T(8,128)(2,1)S(1)}, bf16[160,384]{1,0:T(8,128)(2,1)S(1)}, u32[]{:S(2)}, u32[]{:S(2)}) collective-permute-start(bf16[160,384]{1,0:T(8,128)(2,1)S(1)} %get-tuple-element.28), channel_id=1, source_target_pairs={{0,1},{1,2},{2,3},{3,0},{4,5},{5,6},{6,7},{7,4},{8,9},{9,10},{10,1... | collective-permute-start | bytes 368648 | tf_op jit(solution)/shard_map/ppermute | solution.py:42
  17.1 4.2 %copy-start.1 = (bf16[512,1024]{1,0:T(8,128)(2,1)S(1)}, bf16[512,1024]{1,0:T(8,128)(2,1)}, u32[]{:S(2)}) copy-start(bf16[512,1024]{1,0:T(8,128)(2,1)} %goal_ref.1) | copy-start | bytes 3145732
  17.1 4.2 %copy-start.4 = (bf16[768,160]{1,0:T(8,128)(2,1)S(1)}, bf16[768,160]{1,0:T(8,128)(2,1)}, u32[]{:S(2)}) copy-start(bf16[768,160]{1,0:T(8,128)(2,1)} %constant.15.clone.row_t_ref) | copy-start | bytes 737284
  17.1 4.2 %copy-start.5 = (bf16[256,768]{1,0:T(8,128)(2,1)S(1)}, bf16[256,768]{1,0:T(8,128)(2,1)}, u32[]{:S(2)}) copy-start(bf16[256,768]{1,0:T(8,128)(2,1)} %constant.16.clone.col_ref) | copy-start | bytes 1179652
  32.1 4.2 %collective-permute-start.4 = (bf16[160,512]{1,0:T(8,128)(2,1)S(1)}, bf16[160,512]{1,0:T(8,128)(2,1)S(1)}, u32[]{:S(2)}, u32[]{:S(2)}) collective-permute-start(bf16[160,512]{1,0:T(8,128)(2,1)S(1)} %shard_map.113.mine_ref), channel_id=1, source_target_pairs={{0,3},{1,0},{2,1},{3,2},{4,7},{5,4},{6,5},{7,6},{8,11},{9,8},{10,9... | collective-permute-start | bytes 491528 | tf_op jit(solution)/shard_map/ppermute | solution.py:42
  36.9 5.4 %collective-permute-start.6 = (bf16[128,1024]{1,0:T(8,128)(2,1)S(1)}, bf16[128,1024]{1,0:T(8,128)(2,1)S(1)}, u32[]{:S(2)}, u32[]{:S(2)}) collective-permute-start(bf16[128,1024]{1,0:T(8,128)(2,1)S(1)} %get-tuple-element.34), channel_id=1, source_target_pairs={{0,4},{4,0},{8,12},{12,8},{16,20},{20,16},{24,28},{28,24},{1,5},{5... | collective-permute-start | bytes 786440 | tf_op jit(solution)/shard_map/ppermute | solution.py:32
  37.0 11.7 %collective-permute-start.5 = (bf16[128,1024]{1,0:T(8,128)(2,1)S(1)}, bf16[128,1024]{1,0:T(8,128)(2,1)S(1)}, u32[]{:S(2)}, u32[]{:S(2)}) collective-permute-start(bf16[128,1024]{1,0:T(8,128)(2,1)S(1)} %get-tuple-element.32), channel_id=1, source_target_pairs={{4,8},{8,4},{12,16},{16,12},{20,24},{24,20},{5,9},{9,5},{13,17},{1... | collective-permute-start | bytes 786440 | tf_op jit(solution)/shard_map/ppermute | solution.py:32
